TPU v7x, 32 devices: a whole 2x2x4 slice. The times are simulated.
32 devices in a mesh: ctx: 8 (over z, x), fsdp: 4 (over y, core).
Axes of the slice: x: 2, y: 2, z: 4, core: 2. Of those that a mesh axis runs over, the one named last changes fastest.
Arguments:
- tokens: bfloat16 [8, 1024, 768], P('fsdp', 'ctx'), may hold values from -6 to 6
- chars: bfloat16 [8, 1360, 768], P('fsdp', 'ctx'), may hold values from -6 to 6
- segment: int32 [8, 1024], P('fsdp', 'ctx'), may hold values from 0 to 3, as said below
- char_end: int32 [8, 1024], P('fsdp', 'ctx'), may hold values from 0 to 169, as said below
- w_qkv: bfloat16 [768, 2304], P('fsdp'), may hold values from -0.21875 to 0.21875
- w_out: bfloat16 [768, 768], P('fsdp'), may hold values from -4 to 4
- norm1_gain: bfloat16 [768], P('fsdp'), may hold values from 0.5 to 1.5
- norm1_bias: bfloat16 [768], P('fsdp'), may hold values from -1.796875 to 1.796875
- w_up: bfloat16 [768, 3072], P('fsdp'), may hold values from -0.21875 to 0.21875
- b_up: bfloat16 [3072], P('fsdp'), may hold values from -1.796875 to 1.796875
- w_down: bfloat16 [3072, 768], P('fsdp'), may hold values from -0.109375 to 0.109375
- norm2_gain: bfloat16 [768], P('fsdp'), may hold values from 0.5 to 1.5
- norm2_bias: bfloat16 [768], P('fsdp'), may hold values from -1.796875 to 1.796875
- w_gru: bfloat16 [768, 1536], P('fsdp'), may hold values from -0.21875 to 0.21875
- b_gate: bfloat16 [768], P('fsdp'), may hold values from 2.5 to 9
- w_ftok: bfloat16 [768, 768], P('fsdp'), may hold values from -0.21875 to 0.21875
- w_fchr: bfloat16 [768, 768], P('fsdp'), may hold values from -1.75 to 1.75
- w_conv: bfloat16 [3, 1536, 1536], P(None, 'fsdp'), may hold values from -0.09375 to 0.09375
- norm3_gain: bfloat16 [768], P('fsdp'), may hold values from 0.5 to 1.5
- norm3_bias: bfloat16 [768], P('fsdp'), may hold values from -1.796875 to 1.796875
- norm4_gain: bfloat16 [768], P('fsdp'), may hold values from 0.5 to 1.5
- norm4_bias: bfloat16 [768], P('fsdp'), may hold values from -1.796875 to 1.796875
- d_token: bfloat16 [8, 1024, 768], P('fsdp', 'ctx'), may hold values from -6 to 6
- d_char: bfloat16 [8, 1024, 768], P('fsdp', 'ctx'), may hold values from -6 to 6
Outputs:
- token_out: bfloat16 [8, 1024, 768], P('fsdp', 'ctx')
- char_out: bfloat16 [8, 1024, 768], P('fsdp', 'ctx')
- d_tokens: bfloat16 [8, 1024, 768], P('fsdp', 'ctx')
- d_chars: bfloat16 [8, 1360, 768], P('fsdp', 'ctx')
- qkv_grad: float32 [768, 2304], P('fsdp')
- wout_grad: float32 [768, 768], P('fsdp')
- gain1_grad: float32 [768], P('fsdp')
- bias1_grad: float32 [768], P('fsdp')
- up_grad: float32 [768, 3072], P('fsdp')
- bup_grad: float32 [3072], P('fsdp')
- down_grad: float32 [3072, 768], P('fsdp')
- gain2_grad: float32 [768], P('fsdp')
- bias2_grad: float32 [768], P('fsdp')
- gru_grad: float32 [768, 1536], P('fsdp')
- bgate_grad: float32 [768], P('fsdp')
- ftok_grad: float32 [768, 768], P('fsdp')
- fchr_grad: float32 [768, 768], P('fsdp')
- conv_grad: float32 [3, 1536, 1536], P(None, 'fsdp')
- gain3_grad: float32 [768], P('fsdp')
- bias3_grad: float32 [768], P('fsdp')
- gain4_grad: float32 [768], P('fsdp')
- bias4_grad: float32 [768], P('fsdp')
Inputs may be any that keep to these rules, and one draw needn't show every extreme that they name: Within each sequence the ids start at 0, never fall and rise by one where a new segment begins; the segment with id 1 begins on the first index of ctx and ends on the last, every other segment lies within the first or the last 128 tokens. `char_end`: each aligned block of 128 tokens (one index of ctx) owns the block of 170 characters at the same index; a token's value is its last character as an index within that block, strictly rising along the block, the block's last token ending at 169.
All inputs are finite; a program needn't handle non-finite values.
Results may differ from a plain program's by a relative error of at most 0.02.
Values may be sent and summed in bfloat16 or wider, within the bound.
No kernel may reach another device: no remote copies, remote signals or barrier semaphores. Data moves between devices by JAX's collectives and lax.ppermute only.
A program may use at most 320 MiB of HBM per device.

v0:
```python
import functools

import jax
import jax.numpy as jnp
from jax import lax
from jax.experimental import pallas as pl
from jax.experimental.pallas import tpu as pltpu
from jax.sharding import PartitionSpec as P

HEADS = 12
HEAD_DIM = 64
GRU_H = 384
EPSILON = 1e-05
BLOCK_LIMIT = 1024
FAR = 1e9
VMEM_BYTES = 40 * 1024 * 1024

F32 = jnp.float32
BF16 = jnp.bfloat16


def matmul(left, right):
    return jnp.dot(left, right, preferred_element_type=F32)


def matmul_nt(left, right):
    return lax.dot_general(left, right, (((1,), (1,)), ((), ())), preferred_element_type=F32)


def matmul_tn(left, right):
    return lax.dot_general(left, right, (((0,), (0,)), ((), ())), preferred_element_type=F32)


def layer_norm(value, gain, shift):
    center = value - jnp.mean(value, axis=-1, keepdims=True)
    inverse = lax.rsqrt(jnp.mean(center * center, axis=-1, keepdims=True) + EPSILON)
    normed = center * inverse
    return normed * gain + shift, (normed, inverse)


def layer_norm_back(grad, gain, kept):
    normed, inverse = kept
    scaled = grad * gain
    into = inverse * (
        scaled
        - jnp.mean(scaled, axis=-1, keepdims=True)
        - normed * jnp.mean(scaled * normed, axis=-1, keepdims=True)
    )
    return into, jnp.sum(grad * normed, axis=0), jnp.sum(grad, axis=0)


def params(**more):
    return pltpu.CompilerParams(vmem_limit_bytes=VMEM_BYTES, **more)


def cost(flops, moved, transcendentals=0):
    return pl.CostEstimate(
        flops=int(flops), bytes_accessed=int(moved), transcendentals=int(transcendentals)
    )


def two_parts(value):
    high = value.astype(BF16)
    return high, (value - high.astype(F32)).astype(BF16)


KINDS = 4


def store_edges(edge_ref, cols, rows):
    parts = [half.astype(F32) for row in rows for half in two_parts(row)]
    parts = parts + [jnp.zeros_like(parts[0])] * (KINDS - len(parts))
    parts = jnp.concatenate(parts, axis=0)
    for sequence in range(edge_ref.shape[0] // KINDS):

        @pl.when(pl.program_id(0) == sequence)
        def store():
            edge_ref[pl.ds(sequence * KINDS, KINDS), cols] = parts


def edges_to_block(edges, rows):
    count = edges.shape[1] // HEAD_DIM
    pieces = [edges[:, i * HEAD_DIM : (i + 1) * HEAD_DIM] for i in range(count)]
    pieces.append(jnp.zeros((rows - count * edges.shape[0], HEAD_DIM), F32))
    return jnp.concatenate(pieces, axis=0).astype(BF16)


def edges_of_block(block):
    block = block.astype(F32)
    count = 2 * GRU_H // HEAD_DIM
    return jnp.concatenate([block[i * 8 : (i + 1) * 8] for i in range(count)], axis=1)


def entering_row(decays, drives, sequence, count, flip):
    me = lax.axis_index("ctx")
    halves = []
    for side in (0, 1):
        cols = slice(side * GRU_H, (side + 1) * GRU_H)
        total = jnp.zeros((1, GRU_H), F32)
        backward = (side == 1) != flip
        order = range(count - 1, 0, -1) if backward else range(count - 1)
        for other in order:
            decay, drive = decays(other, sequence, cols), drives(other, sequence, cols)
            there = me < other if backward else me > other
            total = jnp.where(there, decay * total + drive, total)
        halves.append(total)
    return jnp.concatenate(halves, axis=1)


def edge_reader(ref, kind):
    def read(other, sequence, cols):
        at = sequence * KINDS + 2 * kind
        return ref[other, at : at + 1, cols] + ref[other, at + 1 : at + 2, cols]

    return read


def shift_rows(value, by, fill, up):
    rows = value.shape[0]
    row = lax.broadcasted_iota(jnp.int32, value.shape, 0)
    if up:
        return jnp.where(row < rows - by, pltpu.roll(value, rows - by, 0), fill)
    return jnp.where(row >= by, pltpu.roll(value, by, 0), fill)


def scan_rows(decay, drive, up):
    by = 1
    while by < decay.shape[0]:
        drive = drive + decay * shift_rows(drive, by, 0.0, up)
        decay = decay * shift_rows(decay, by, 1.0, up)
        by = by * 2
    return decay, drive


def gru_forward_kernel(
    real, chars_ref, w_ref, bias_ref, start_ref, first_ref, end_ref, last_ref,
    gate_ref, cand_ref, decay_ref, cum_ref, state_ref, edge_ref,
):
    columns = matmul(chars_ref[0], w_ref[:, : 4 * GRU_H])
    rows = columns.shape[0]
    tokens = start_ref.shape[2]
    place = lax.broadcasted_iota(jnp.int32, (rows, tokens), 0)
    inside = lax.broadcasted_iota(jnp.int32, (rows, GRU_H), 0) < real
    resets = [
        jnp.sum(jnp.where(place == at[0], flag[0], 0.0), axis=1, keepdims=True)
        for at, flag in ((start_ref, first_ref), (end_ref, last_ref))
    ]
    for side in (0, 1):
        cols = pl.ds(side * GRU_H, GRU_H)
        base = 2 * side * GRU_H
        gate = jax.nn.sigmoid(columns[:, base : base + GRU_H] + bias_ref[:, cols])
        cand = jnp.tanh(columns[:, base + GRU_H : base + 2 * GRU_H])
        decay = jnp.where(inside, gate * (1.0 - resets[side]), 1.0)
        drive = jnp.where(inside, (1.0 - gate) * cand, 0.0)
        gate_ref[0, :, cols] = gate
        cand_ref[0, :, cols] = cand
        decay_ref[0, :, cols] = decay
        cum, state = scan_rows(decay, drive, side == 1)
        cum_ref[0, :, cols] = cum
        state_ref[0, :, cols] = state
        at = 0 if side else real - 1
        store_edges(edge_ref, cols, (cum[at : at + 1], state[at : at + 1]))


def char_tok_kernel(state_ref, cum_ref, edges_ref, end_ref, start_ref, out_ref, enter_ref):
    batch, tokens = end_ref.shape[:2]
    for sequence in range(batch):
        enter = entering_row(
            edge_reader(edges_ref, 0), edge_reader(edges_ref, 1), sequence, edges_ref.shape[0],
            False,
        )
        enter_ref[sequence] = enter
        state = state_ref[sequence] + cum_ref[sequence] * enter
        high, low = two_parts(state)
        place = lax.broadcasted_iota(jnp.int32, (tokens, state.shape[0]), 1)
        for side, at in ((0, end_ref), (1, start_ref)):
            pick = jnp.where(place == at[sequence], 1.0, 0.0).astype(BF16)
            cols = slice(side * GRU_H, (side + 1) * GRU_H)
            out_ref[pl.ds(sequence * tokens, tokens), pl.ds(side * GRU_H, GRU_H)] = matmul(
                pick, high[:, cols]
            ) + matmul(pick, low[:, cols])


def gru_back_kernel(
    real, grad_ref, decay_ref, end_ref, start_ref, spread_ref, cum_ref, carried_ref, edge_ref
):
    rows = decay_ref.shape[1]
    tokens = end_ref.shape[2]
    place = lax.broadcasted_iota(jnp.int32, (rows, tokens), 0)
    high, low = two_parts(grad_ref[0])
    for side, at in ((0, end_ref), (1, start_ref)):
        put = jnp.where(place == at[0], 1.0, 0.0).astype(BF16)
        cols = slice(side * GRU_H, (side + 1) * GRU_H)
        there = pl.ds(side * GRU_H, GRU_H)
        spread = matmul(put, high[:, cols]) + matmul(put, low[:, cols])
        decay = decay_ref[0, :, there]
        cum, carried = scan_rows(decay, decay * spread, side == 0)
        spread_ref[0, :, there] = spread
        cum_ref[0, :, there] = cum
        carried_ref[0, :, there] = carried
        at = real - 1 if side else 0
        store_edges(edge_ref, there, (carried[at : at + 1],))


def gru_grad_kernel(
    real, gate_ref, cand_ref, decay_ref, cum_ref, state_ref, enter_ref,
    spread_ref, back_cum_ref, carried_ref, back_enter_ref, out_ref, bias_ref,
):
    rows = gate_ref.shape[1]
    inside = lax.broadcasted_iota(jnp.int32, (rows, GRU_H), 0) < real
    for side in (0, 1):
        there = pl.ds(side * GRU_H, GRU_H)
        gate = gate_ref[0, :, there]
        cand = cand_ref[0, :, there]
        decay = decay_ref[0, :, there]
        enter = enter_ref[0, :, there]
        back_enter = back_enter_ref[0, :, there]
        state = state_ref[0, :, there] + cum_ref[0, :, there] * enter
        carried = carried_ref[0, :, there] + back_cum_ref[0, :, there] * back_enter
        previous = shift_rows(state, 1, enter, side == 1)
        adjoint = spread_ref[0, :, there] + shift_rows(carried, 1, back_enter, side == 0)
        adjoint = jnp.where(inside, adjoint, 0.0)
        rest = adjoint * (1.0 - gate)
        to_gate = rest * (previous * decay - cand * gate)
        to_cand = rest * (1.0 - cand * cand)
        out_ref[0, :, pl.ds(2 * side * GRU_H, GRU_H)] = to_gate.astype(BF16)
        out_ref[0, :, pl.ds((2 * side + 1) * GRU_H, GRU_H)] = to_cand.astype(BF16)
        bias_ref[0, :, there] = jnp.sum(to_gate, axis=0, keepdims=True)


def per_sequence(*tail):
    return pl.BlockSpec((1,) + tail, lambda s: (s,) + (0,) * len(tail))


def whole_block(*shape):
    return pl.BlockSpec(shape, lambda s: (0,) * len(shape))


def gru_forward(chars, w_gru, bias, start, first, end, last, real):
    batch, rows, width = chars.shape
    tokens = start.shape[2]
    two = 2 * GRU_H
    kept = jax.ShapeDtypeStruct((batch, rows, two), F32)
    return pl.pallas_call(
        functools.partial(gru_forward_kernel, real),
        grid=(batch,),
        in_specs=[per_sequence(rows, width), whole_block(width, w_gru.shape[1]), whole_block(1, two)]
        + [per_sequence(1, tokens)] * 4,
        out_specs=[per_sequence(rows, two)] * 5 + [whole_block(KINDS * batch, two)],
        out_shape=[kept] * 5 + [jax.ShapeDtypeStruct((KINDS * batch, two), F32)],
        compiler_params=params(),
        cost_estimate=cost(
            2 * batch * rows * width * 2 * two,
            chars.size * 2 + w_gru.size * 2 + 20 * batch * rows * two,
            2 * batch * rows * two,
        ),
        name="gru_forward",
    )(chars, w_gru, bias, start, first, end, last)


def gather_states(state, cum, edges, end, start):
    batch, rows, two = state.shape
    tokens = end.shape[1]
    return pl.pallas_call(
        char_tok_kernel,
        out_shape=[
            jax.ShapeDtypeStruct((batch * tokens, two), F32),
            jax.ShapeDtypeStruct((batch, 1, two), F32),
        ],
        compiler_params=params(),
        cost_estimate=cost(
            4 * batch * rows * tokens * two, 8 * batch * rows * two + 4 * batch * tokens * two
        ),
        name="gather_states",
    )(state, cum, edges, end, start)


def gru_back(grad, decay, end, start, real):
    batch, rows, two = decay.shape
    tokens = end.shape[2]
    kept = jax.ShapeDtypeStruct((batch, rows, two), F32)
    return pl.pallas_call(
        functools.partial(gru_back_kernel, real),
        grid=(batch,),
        in_specs=[per_sequence(tokens, two), per_sequence(rows, two)]
        + [per_sequence(1, tokens)] * 2,
        out_specs=[per_sequence(rows, two)] * 3 + [whole_block(KINDS * batch, two)],
        out_shape=[kept] * 3 + [jax.ShapeDtypeStruct((KINDS * batch, two), F32)],
        compiler_params=params(),
        cost_estimate=cost(
            4 * batch * rows * tokens * two, 16 * batch * rows * two + 4 * batch * tokens * two
        ),
        name="gru_back",
    )(grad, decay, end, start)


def gru_grad(gate, cand, decay, cum, state, enter, spread, back_cum, carried, back_enter, real):
    batch, rows, two = decay.shape
    big = per_sequence(rows, two)
    row = per_sequence(1, two)
    return pl.pallas_call(
        functools.partial(gru_grad_kernel, real),
        grid=(batch,),
        in_specs=[big] * 5 + [row] + [big] * 3 + [row],
        out_specs=[per_sequence(rows, 2 * two), row],
        out_shape=[
            jax.ShapeDtypeStruct((batch, rows, 2 * two), BF16),
            jax.ShapeDtypeStruct((batch, 1, two), F32),
        ],
        compiler_params=params(),
        cost_estimate=cost(20 * batch * rows * two, 36 * batch * rows * two),
        name="gru_grad",
    )(gate, cand, decay, cum, state, enter, spread, back_cum, carried, back_enter)


def all_edges(edges):
    return lax.all_gather(edges, "ctx", axis=0)


def entering_kernel(decay_ref, drive_ref, out_ref):
    for sequence in range(out_ref.shape[0]):
        out_ref[sequence] = entering_row(
            edge_reader(decay_ref, 0), edge_reader(drive_ref, 0), sequence, decay_ref.shape[0],
            True,
        )


def back_entering(decays, drives):
    batch, two = decays.shape[1] // KINDS, decays.shape[2]
    return pl.pallas_call(
        entering_kernel,
        out_shape=jax.ShapeDtypeStruct((batch, 1, two), F32),
        compiler_params=params(),
        name="back_entering",
    )(decays, drives)


def project_kernel(groups, part, tok_ref, w_ref, seg_ref, out_ref):
    qkv = matmul(tok_ref[0], w_ref[...]).astype(BF16)
    rows, width = tok_ref.shape[1], tok_ref.shape[2]
    lane = lax.broadcasted_iota(jnp.int32, (rows, HEAD_DIM), 1)
    marks = jnp.where(lane == seg_ref[0], 1.0, 0.0).astype(BF16)
    for group in range(groups):
        pieces = [
            qkv[:, kind * width + group * part : kind * width + (group + 1) * part]
            for kind in range(3)
        ]
        out_ref[group] = jnp.concatenate(pieces + [marks], axis=1)


def attend_kernel(heads, tokens, all_ref, query_ref, edge_ref, out_ref, kept_ref, key_scr, value_scr):
    part = heads * HEAD_DIM
    rows = query_ref.shape[0]

    @pl.when(pl.program_id(0) == 0)
    def build():
        marks = all_ref[:, 3 * part :]
        blocked = ((marks.astype(F32) - 1.0) * FAR).astype(BF16)
        ones = jnp.ones_like(marks)
        for head in range(heads):
            at = head * HEAD_DIM
            key_scr[head] = jnp.concatenate(
                [all_ref[:, part + at : part + at + HEAD_DIM], blocked], axis=1
            )
            value_scr[head] = jnp.concatenate(
                [all_ref[:, 2 * part + at : 2 * part + at + HEAD_DIM], ones], axis=1
            )

    marks = query_ref[:, 3 * part :]
    outs = []
    for head in range(heads):
        at = head * HEAD_DIM
        query = query_ref[:, at : at + HEAD_DIM] * jnp.asarray(HEAD_DIM ** (-0.5), BF16)
        query = jnp.concatenate([query, marks], axis=1)
        expvals = jnp.exp(matmul_nt(query, key_scr[head]))
        both = matmul(expvals.astype(BF16), value_scr[head])
        total = both[:, HEAD_DIM:]
        context = both[:, :HEAD_DIM] / total
        kept_ref[:, pl.ds(head * 2 * HEAD_DIM, 2 * HEAD_DIM)] = jnp.concatenate(
            [context, total], axis=1
        )
        outs.append(context.astype(BF16))
    block = edges_to_block(edge_ref[...], tokens)
    outs.append(jnp.concatenate([block] * (rows // tokens), axis=0))
    out_ref[...] = jnp.concatenate(outs, axis=1)


def attend_back_kernel(
    heads, tokens, all_ref, kept_ref, grad_ref, edges_ref, out_ref, enter_ref,
    query_scr, key_scr, value_scr, grad_scr, edge_scr,
):
    part = heads * HEAD_DIM
    rows = out_ref.shape[0]
    step = pl.program_id(0)

    @pl.when(step == 0)
    def build():
        marks = all_ref[:, 3 * part :]
        blocked = ((marks.astype(F32) - 1.0) * FAR).astype(BF16)
        lane = lax.broadcasted_iota(jnp.int32, marks.shape, 1)
        pair = jnp.where(lane < 2, 1.0, 0.0).astype(BF16)
        for head in range(heads):
            at = head * HEAD_DIM
            query = all_ref[:, at : at + HEAD_DIM] * jnp.asarray(HEAD_DIM ** (-0.5), BF16)
            query_scr[head] = jnp.concatenate([query, marks], axis=1)
            key_scr[head] = jnp.concatenate(
                [all_ref[:, part + at : part + at + HEAD_DIM], blocked], axis=1
            )
            value_scr[head] = jnp.concatenate(
                [all_ref[:, 2 * part + at : 2 * part + at + HEAD_DIM], pair], axis=1
            )
            context = kept_ref[:, 2 * at : 2 * at + HEAD_DIM]
            total = kept_ref[:, 2 * at + HEAD_DIM : 2 * at + 2 * HEAD_DIM]
            grad = grad_ref[:, at : at + HEAD_DIM].astype(F32) / total
            delta = jnp.sum(grad * context, axis=1, keepdims=True)
            high, low = two_parts(-delta)
            extra = jnp.where(
                lane == 0, high.astype(F32), jnp.where(lane == 1, low.astype(F32), 0.0)
            )
            grad_scr[head] = jnp.concatenate([grad, extra], axis=1).astype(BF16)
        for other in range(edges_ref.shape[0]):
            edge_scr[other] = edges_of_block(
                grad_ref[other * tokens : (other + 1) * tokens, part : part + HEAD_DIM]
            )
        for sequence in range(enter_ref.shape[0]):
            enter_ref[sequence] = entering_row(
                edge_reader(edges_ref, 0), edge_reader(edge_scr, 0), sequence,
                edges_ref.shape[0], True,
            )

    here = pl.ds(pl.multiple_of(step * rows, rows), rows)
    scale = HEAD_DIM ** (-0.5)
    d_query, d_key, d_value = [], [], []
    for head in range(heads):
        expvals = jnp.exp(matmul_nt(query_scr[head, here], key_scr[head]))
        inner = matmul_nt(grad_scr[head, here], value_scr[head])
        d_scores = (expvals * inner).astype(BF16)
        d_query.append((matmul(d_scores, key_scr[head])[:, :HEAD_DIM] * scale).astype(BF16))
        expvals = jnp.exp(matmul_nt(key_scr[head, here], query_scr[head]))
        inner = matmul_nt(value_scr[head, here], grad_scr[head])
        d_scores = (expvals * inner).astype(BF16)
        d_key.append(matmul(d_scores, query_scr[head])[:, :HEAD_DIM].astype(BF16))
        d_value.append(
            matmul(expvals.astype(BF16), grad_scr[head])[:, :HEAD_DIM].astype(BF16)
        )
    pad = jnp.zeros((rows, HEAD_DIM), BF16)
    out_ref[...] = jnp.concatenate(d_query + d_key + d_value + [pad], axis=1)


def unpack_kernel(groups, part, kinds, in_ref, out_ref, *edge_refs):
    for edge_ref in edge_refs:
        for group in range(groups):
            edge_ref[group] = edges_of_block(in_ref[group, :, kinds * part :])
    pieces = [
        in_ref[group, :, kind * part : (kind + 1) * part]
        for kind in range(kinds)
        for group in range(groups)
    ]
    out_ref[...] = jnp.concatenate(pieces, axis=1)


def send_grad_kernel(groups, part, grad_ref, w_ref, edge_ref, out_ref):
    d_context = matmul_nt(grad_ref[...], w_ref[...]).astype(BF16)
    block = edges_to_block(edge_ref[...], grad_ref.shape[0])
    for group in range(groups):
        out_ref[group] = jnp.concatenate(
            [d_context[:, group * part : (group + 1) * part], block], axis=1
        )


def heads_here(batch, count):
    if batch * HEADS % count != 0:
        return 0
    heads = batch * HEADS // count
    if heads > HEADS or HEADS % heads != 0 or heads % 2 == 0 or batch * KINDS != 8:
        return 0
    return heads


def project_and_pack(tokens, w_qkv, segment, heads):
    batch, rows, width = tokens.shape
    groups, part = HEADS // heads, heads * HEAD_DIM
    wide = 3 * part + HEAD_DIM
    return pl.pallas_call(
        functools.partial(project_kernel, groups, part),
        grid=(batch,),
        in_specs=[
            per_sequence(rows, width),
            whole_block(width, 3 * width),
            per_sequence(rows, 1),
        ],
        out_specs=pl.BlockSpec((groups, rows, wide), lambda s: (s, 0, 0)),
        out_shape=jax.ShapeDtypeStruct((batch * groups, rows, wide), BF16),
        compiler_params=params(),
        cost_estimate=cost(
            6 * batch * rows * width * width,
            tokens.size * 2 + w_qkv.size * 2 + 2 * batch * groups * rows * wide,
        ),
        name="project",
    )(tokens, w_qkv, segment[:, :, None])


def attend(everything, edges, heads, tokens):
    length, wide = everything.shape
    block = 256
    part = heads * HEAD_DIM
    out_wide = part + HEAD_DIM
    return pl.pallas_call(
        functools.partial(attend_kernel, heads, tokens),
        grid=(length // block,),
        in_specs=[
            pl.BlockSpec((length, wide), lambda i: (0, 0)),
            pl.BlockSpec((block, wide), lambda i: (i, 0)),
            pl.BlockSpec(edges.shape, lambda i: (0, 0)),
        ],
        out_specs=[
            pl.BlockSpec((block, out_wide), lambda i: (i, 0)),
            pl.BlockSpec((block, 2 * part), lambda i: (i, 0)),
        ],
        out_shape=[
            jax.ShapeDtypeStruct((length, out_wide), BF16),
            jax.ShapeDtypeStruct((length, 2 * part), F32),
        ],
        scratch_shapes=[
            pltpu.VMEM((heads, length, 2 * HEAD_DIM), BF16),
            pltpu.VMEM((heads, length, 2 * HEAD_DIM), BF16),
        ],
        compiler_params=params(),
        cost_estimate=cost(
            8 * heads * length * length * HEAD_DIM,
            length * (wide * 2 + out_wide * 2 + 8 * part),
            heads * length * length,
        ),
        name="attend",
    )(everything, everything, edges)


def attend_back(everything, kept, grads, edges, heads, tokens):
    length, wide = everything.shape
    block = 256
    part = heads * HEAD_DIM
    batch, two = edges.shape[1] // KINDS, edges.shape[2]
    scratch = pltpu.VMEM((heads, length, 2 * HEAD_DIM), BF16)
    return pl.pallas_call(
        functools.partial(attend_back_kernel, heads, tokens),
        grid=(length // block,),
        in_specs=[
            pl.BlockSpec((length, wide), lambda i: (0, 0)),
            pl.BlockSpec((length, 2 * part), lambda i: (0, 0)),
            pl.BlockSpec((length, part + HEAD_DIM), lambda i: (0, 0)),
            pl.BlockSpec(edges.shape, lambda i: (0, 0, 0)),
        ],
        out_specs=[
            pl.BlockSpec((block, wide), lambda i: (i, 0)),
            pl.BlockSpec((batch, 1, two), lambda i: (0, 0, 0)),
        ],
        out_shape=[
            jax.ShapeDtypeStruct((length, wide), BF16),
            jax.ShapeDtypeStruct((batch, 1, two), F32),
        ],
        scratch_shapes=[scratch] * 4 + [pltpu.VMEM(edges.shape, F32)],
        compiler_params=params(),
        cost_estimate=cost(
            28 * heads * length * length * HEAD_DIM,
            length * (wide * 4 + 8 * part + 2 * part),
            2 * heads * length * length,
        ),
        name="attend_back",
    )(everything, kept, grads, edges)


def unpack(received, heads, kinds, batch, edges):
    count, rows, wide = received.shape
    groups, part = HEADS // heads, heads * HEAD_DIM
    width = kinds * groups * part
    out_specs = [pl.BlockSpec((rows, width), lambda s: (s, 0))]
    out_shape = [jax.ShapeDtypeStruct((batch * rows, width), BF16)]
    if edges:
        out_specs.append(pl.BlockSpec((groups, KINDS * batch, 2 * GRU_H), lambda s: (s, 0, 0)))
        out_shape.append(jax.ShapeDtypeStruct((count, KINDS * batch, 2 * GRU_H), F32))
    return pl.pallas_call(
        functools.partial(unpack_kernel, groups, part, kinds),
        grid=(batch,),
        in_specs=[pl.BlockSpec((groups, rows, wide), lambda s: (s, 0, 0))],
        out_specs=out_specs,
        out_shape=out_shape,
        compiler_params=params(),
        cost_estimate=cost(0, 2 * received.size + 2 * batch * rows * width),
        name="unpack",
    )(received)


def send_grad(d_attn, w_out, edges, heads, batch):
    total, width = d_attn.shape
    rows = total // batch
    groups, part = HEADS // heads, heads * HEAD_DIM
    wide = part + HEAD_DIM
    return pl.pallas_call(
        functools.partial(send_grad_kernel, groups, part),
        grid=(batch,),
        in_specs=[
            pl.BlockSpec((rows, width), lambda s: (s, 0)),
            whole_block(width, width),
            whole_block(*edges.shape),
        ],
        out_specs=pl.BlockSpec((groups, rows, wide), lambda s: (s, 0, 0)),
        out_shape=jax.ShapeDtypeStruct((batch * groups, rows, wide), BF16),
        compiler_params=params(),
        cost_estimate=cost(
            2 * total * width * width, 2 * (d_attn.size + w_out.size + total * groups * wide)
        ),
        name="send_grad",
    )(d_attn, w_out, edges)


def feed_forward_kernel(hidden_ref, w_ref, bias_ref, inner_ref, slope_ref):
    pre = matmul(hidden_ref[...], w_ref[...]) + bias_ref[...]
    at = jnp.abs(pre) * (0.5**0.5)
    near = 1.0 / (1.0 + 0.3275911 * at)
    gauss = jnp.exp(-at * at)
    series = 1.061405429
    for term in (-1.453152027, 1.421413741, -0.284496736, 0.254829592):
        series = series * near + term
    tail = 0.5 * series * near * gauss
    below = jnp.where(pre < 0.0, tail, 1.0 - tail)
    inner_ref[...] = (pre * below).astype(BF16)
    slope_ref[...] = (below + pre * gauss * (2.0 * jnp.pi) ** -0.5).astype(BF16)


def feed_forward(hidden, w_up, bias):
    rows, width = hidden.shape
    wide = w_up.shape[1]
    block = 512
    column = pl.BlockSpec((rows, block), lambda i: (0, i))
    return pl.pallas_call(
        feed_forward_kernel,
        grid=(wide // block,),
        in_specs=[
            whole_block(rows, width),
            pl.BlockSpec((width, block), lambda i: (0, i)),
            pl.BlockSpec((1, block), lambda i: (0, i)),
        ],
        out_specs=[column, column],
        out_shape=[jax.ShapeDtypeStruct((rows, wide), BF16)] * 2,
        compiler_params=params(),
        cost_estimate=cost(
            2 * rows * width * wide, 2 * (hidden.size + w_up.size + 2 * rows * wide), rows * wide
        ),
        name="feed_forward",
    )(hidden, w_up, bias)


def block_size(rows):
    size = min(rows, BLOCK_LIMIT)
    while rows % size != 0:
        size = size - 1
    return size


def split_blocks(array, size):
    return array.reshape((array.shape[0] // size, size) + array.shape[1:])


def to_heads(matrix):
    return matrix.reshape(matrix.shape[0], HEADS, HEAD_DIM)


def masked_exp(query_heads, key_heads, query_seg, key_seg):
    scores = jnp.einsum(
        "qhd,khd->hqk", query_heads, key_heads, preferred_element_type=F32
    ) * HEAD_DIM ** (-0.5)
    same = (query_seg[:, None] == key_seg[None, :])[None, :, :]
    return jnp.where(same, jnp.exp(scores), 0.0)


def everyone(rows):
    return lax.all_gather(rows, "ctx", axis=0, tiled=True)


def gathered_attention(qkv, seg_row):
    tok_rows, width = qkv.shape[0], qkv.shape[1] // 3
    query_heads = to_heads(qkv[:, :width])
    pieces = (everyone(qkv[:, width : 2 * width]), everyone(qkv[:, 2 * width :]), everyone(seg_row))
    size = block_size(pieces[0].shape[0])

    def step(acc, item):
        key_block, value_block, seg_block = item
        expvals = masked_exp(query_heads, to_heads(key_block), seg_row, seg_block)
        part_num = jnp.einsum(
            "hqk,khd->qhd", expvals.astype(BF16), to_heads(value_block),
            preferred_element_type=F32,
        )
        return ((acc[0] + part_num, acc[1] + jnp.transpose(jnp.sum(expvals, axis=-1))), None)

    (numer, total), unused = lax.scan(
        step,
        (jnp.zeros((tok_rows, HEADS, HEAD_DIM), F32), jnp.zeros((tok_rows, HEADS), F32)),
        tuple(split_blocks(piece, size) for piece in pieces),
    )
    return numer / total[:, :, None], total


def gathered_attention_back(qkv, seg_row, context, total, d_context):
    tok_rows, width = qkv.shape[0], qkv.shape[1] // 3
    scale = HEAD_DIM ** (-0.5)
    d_context = to_heads(d_context)
    query_rows, key_rows, value_rows = (qkv[:, i * width : (i + 1) * width] for i in range(3))
    grad_heads = (d_context / total[:, :, None]).astype(BF16)
    delta = jnp.sum(d_context * context, axis=-1) / total
    key_heads, value_heads, query_heads = (
        to_heads(key_rows), to_heads(value_rows), to_heads(query_rows)
    )
    zero_heads = jnp.zeros((tok_rows, HEADS, HEAD_DIM), F32)
    seg_all = everyone(seg_row)
    size = block_size(seg_all.shape[0])

    def key_step(acc, item):
        query_block, grad_block, delta_block, seg_block = item
        query_h, grad_h = to_heads(query_block), to_heads(grad_block)
        expvals = masked_exp(query_h, key_heads, seg_block, seg_row)
        dprob = jnp.einsum("qhd,khd->hqk", grad_h, value_heads, preferred_element_type=F32)
        dscore = (expvals * (dprob - jnp.transpose(delta_block)[:, :, None])).astype(BF16)
        dkey = acc[0] + scale * jnp.einsum(
            "hqk,qhd->khd", dscore, query_h, preferred_element_type=F32
        )
        dval = acc[1] + jnp.einsum(
            "hqk,qhd->khd", expvals.astype(BF16), grad_h, preferred_element_type=F32
        )
        return ((dkey, dval), None)

    (dkey, dval), unused = lax.scan(
        key_step,
        (zero_heads, zero_heads),
        tuple(
            split_blocks(piece, size)
            for piece in (
                everyone(query_rows),
                everyone(grad_heads.reshape(tok_rows, width)),
                everyone(delta),
                seg_all,
            )
        ),
    )

    def query_step(acc, item):
        key_block, value_block, seg_block = item
        key_h = to_heads(key_block)
        expvals = masked_exp(query_heads, key_h, seg_row, seg_block)
        dprob = jnp.einsum(
            "qhd,khd->hqk", grad_heads, to_heads(value_block), preferred_element_type=F32
        )
        dscore = (expvals * (dprob - jnp.transpose(delta)[:, :, None])).astype(BF16)
        return (
            acc + scale * jnp.einsum("hqk,khd->qhd", dscore, key_h, preferred_element_type=F32),
            None,
        )

    dquery, unused = lax.scan(
        query_step,
        zero_heads,
        tuple(
            split_blocks(piece, size)
            for piece in (everyone(key_rows), everyone(value_rows), seg_all)
        ),
    )
    return jnp.concatenate(
        [part.reshape(tok_rows, width) for part in (dquery, dkey, dval)], axis=1
    ).astype(BF16)


def neighbours(rows):
    count = lax.axis_size("ctx")
    up = [(i, i + 1) for i in range(count - 1)]
    down = [(j, i) for i, j in up]
    before = lax.ppermute(rows[:, -1], "ctx", up)
    after = lax.ppermute(rows[:, 0], "ctx", down)
    return before[:, None], after[:, None]


def shifted(rows, before, after):
    later = jnp.concatenate([before, rows[:, :-1]], axis=1)
    earlier = jnp.concatenate([rows[:, 1:], after], axis=1)
    return later, earlier


def routed():
    return lax.axis_size("ctx") == 8 and lax.axis_size("fsdp") == 4


STEPS = (1, 2, 4)
ORDER = "DCDCDTCDTCDTQCDQTQTQCTDQQTQ"


def flip(value, axis, bit):
    return lax.ppermute(value, axis, [(i, i ^ bit) for i in range(lax.axis_size(axis))])


def slot():
    me = lax.axis_index("ctx")
    return (me % 2) * 4 + ((me // 2) % 2) * 2 + me // 4


class CtxSum:
    def __init__(self, value):
        self.value = value
        self.axis = value.ndim - 2
        self.stage = 0

    def halve(self, value, bit):
        mine = (lax.axis_index("ctx") // bit) % 2
        half = value.shape[self.axis] // 2
        send = lax.dynamic_slice_in_dim(value, (1 - mine) * half, half, self.axis)
        self.keep = lax.dynamic_slice_in_dim(value, mine * half, half, self.axis)
        self.send(send, bit)

    def send(self, value, bit):
        self.sent = value
        self.got = flip(value, "ctx", bit)

    def advance(self, *others):
        stage = self.stage
        self.stage = stage + 1
        if stage == 0:
            self.halve(after(self.value, *others), STEPS[0])
        elif stage <= 3:
            got = after(self.got, *others).astype(F32)
            piece = (self.keep.astype(F32) + got).astype(BF16)
            if stage < 3:
                self.halve(piece, STEPS[stage])
            else:
                self.send(piece[None], STEPS[2])
        else:
            piece = jnp.concatenate([self.sent, after(self.got, *others)], axis=0)
            if stage < 6:
                self.send(piece, STEPS[5 - stage])
            else:
                self.result = self.sent = piece
        return self.sent


def run_in_order(events, waits):
    last = ()
    for event, chain in enumerate(events):
        last = (chain.advance(*last, *waits.get(event, ())),)


def settle_kernel(order_ref, in_ref, *out_refs):
    at = 0
    for out_ref in out_refs:
        wide = out_ref.shape[-1]
        out_ref[...] = in_ref[0, ..., at : at + wide].astype(F32)
        at = at + wide


def settle(pieces, widths):
    lead = pieces.shape[1:-2]
    rows, total = pieces.shape[-2:]
    order = jnp.bitwise_xor(slot(), jnp.arange(8, dtype=jnp.int32))
    none = (0,) * len(lead)
    return pl.pallas_call(
        settle_kernel,
        grid_spec=pltpu.PrefetchScalarGridSpec(
            num_scalar_prefetch=1,
            grid=(8,),
            in_specs=[
                pl.BlockSpec((1,) + lead + (rows, total), lambda r, o: (r,) + none + (0, 0))
            ],
            out_specs=[
                pl.BlockSpec(lead + (rows, width), lambda r, o: none + (o[r], 0))
                for width in widths
            ],
        ),
        out_shape=[jax.ShapeDtypeStruct(lead + (8 * rows, width), F32) for width in widths],
        compiler_params=params(),
        cost_estimate=cost(pieces.size, 6 * pieces.size),
        name="settle",
    )(order, pieces)


def place_own_kernel(spans, own_ref, core_ref, *rest):
    outs, sems = rest[:-1], rest[-1]
    mine = lax.axis_index("fsdp")
    copies, at = [], 0
    for span, out_ref in zip(spans, outs):
        for source, shard in ((own_ref, mine), (core_ref, jnp.bitwise_xor(mine, 1))):
            copies.append(
                pltpu.make_async_copy(
                    source.at[pl.ds(at, span)], out_ref.at[shard], sems.at[len(copies)]
                )
            )
        at = at + span
    for copy in copies:
        copy.start()
    for copy in copies:
        copy.wait()


def place_kernel(spans, order, piece_ref, core_ref, *rest):
    outs, sems = rest[len(spans) : -1], rest[-1]
    place = slot()
    mine = lax.axis_index("fsdp")
    copies = []
    for source, shard in (
        (piece_ref, jnp.bitwise_xor(mine, 2)),
        (core_ref, jnp.bitwise_xor(mine, 3)),
    ):
        for position, other in enumerate(order):
            at = 0
            for span, out_ref in zip(spans, outs):
                part = span // 8
                there = pl.multiple_of(jnp.bitwise_xor(place, other) * part, part)
                copies.append(
                    pltpu.make_async_copy(
                        source.at[position, pl.ds(at, part)],
                        out_ref.at[shard, pl.ds(there, part)],
                        sems.at[len(copies)],
                    )
                )
                at = at + part
    for copy in copies:
        copy.start()
    for copy in copies:
        copy.wait()


def after(value, *others):
    return lax.optimization_barrier((value,) + others)[0]


class SpreadGather:
    def __init__(self, shards):
        self.spans = tuple(shard.shape[0] for shard in shards)
        self.width = shards[0].shape[1]
        place = slot()
        self.own = jnp.concatenate(shards, axis=0) if len(shards) > 1 else shards[0]
        piece = [
            lax.dynamic_slice_in_dim(shard, place * (span // 8), span // 8, 0)
            for shard, span in zip(shards, self.spans)
        ]
        self.piece = flip(jnp.concatenate(piece, axis=0), "fsdp", 2)[None]
        self.core = flip(self.own, "fsdp", 1)
        self.order = [0]

    def double(self, bit, *others):
        piece = after(self.piece, *others) if others else self.piece
        self.piece = jnp.concatenate([piece, flip(piece, "ctx", bit)], axis=0)
        self.order = self.order + [other ^ (4 // bit) for other in self.order]

    def cores(self, *others):
        piece = after(self.piece, *others) if others else self.piece
        self.core_piece = flip(piece, "fsdp", 1)

    def place_own(self):
        spans, width = self.spans, self.own.shape[1]
        self.whole = pl.pallas_call(
            functools.partial(place_own_kernel, spans),
            in_specs=[pl.BlockSpec(memory_space=pltpu.VMEM)] * 2,
            out_specs=[pl.BlockSpec(memory_space=pl.ANY)] * len(spans),
            out_shape=[jax.ShapeDtypeStruct((4, span, width), BF16) for span in spans],
            scratch_shapes=[pltpu.SemaphoreType.DMA((2 * len(spans),))],
            compiler_params=params(),
            cost_estimate=cost(0, 8 * sum(spans) * width),
            name="place_own",
        )(self.own, self.core)

    def finish(self):
        spans, width = self.spans, self.own.shape[1]
        anywhere = [pl.BlockSpec(memory_space=pl.ANY)] * len(spans)
        return pl.pallas_call(
            functools.partial(place_kernel, spans, self.order),
            in_specs=[pl.BlockSpec(memory_space=pltpu.VMEM)] * 2 + anywhere,
            out_specs=anywhere,
            out_shape=[jax.ShapeDtypeStruct((4, span, width), BF16) for span in spans],
            scratch_shapes=[pltpu.SemaphoreType.DMA((16 * len(spans),))],
            input_output_aliases={2 + i: i for i in range(len(spans))},
            compiler_params=params(),
            cost_estimate=cost(0, 8 * sum(spans) * width),
            name="place",
        )(self.piece, self.core_piece, *self.whole)


def over_fsdp(grads):
    return lax.psum_scatter(grads, "fsdp", scatter_dimension=0, tiled=True)


def plain_sum(grads, axis=0):
    share = lax.psum_scatter(grads, "fsdp", scatter_dimension=axis, tiled=True)
    return lax.psum(share.astype(F32), "ctx")


def local(
    tokens, chars, segment, char_end, w_qkv, w_out, norm1_gain, norm1_bias, w_up, b_up, w_down,
    norm2_gain, norm2_bias, w_gru, b_gate, w_ftok, w_fchr, w_conv, norm3_gain, norm3_bias,
    norm4_gain, norm4_bias, d_token, d_char,
):
    count, me = lax.axis_size("ctx"), lax.axis_index("ctx")
    shards = lax.axis_size("fsdp")
    batch, rows, width = tokens.shape
    char_rows = chars.shape[1]
    total_rows = batch * rows
    heads = heads_here(batch, count)
    padded_rows = -(-char_rows // 8) * 8

    def gather(weight, axis=0):
        return lax.all_gather(weight, "fsdp", axis=axis, tiled=True)

    own_width = norm1_gain.shape[0]
    vectors = (
        norm1_gain, norm1_bias, norm2_gain, norm2_bias, b_gate, norm3_gain, norm3_bias,
        norm4_gain, norm4_bias,
    )
    columns = jnp.stack(vectors, axis=1)
    columns = jnp.concatenate([columns, b_up.reshape(-1, own_width).T], axis=1)
    small_count = columns.shape[1]
    wide_gru = w_gru.shape[1]
    columns = jnp.pad(columns, ((0, 0), (0, 128 - small_count)))
    w_qkv = gather(w_qkv)
    w_gru = gather(jnp.concatenate([w_gru, columns], axis=1))
    w_out = gather(w_out)
    w_up = gather(w_up)
    columns = w_gru[:, wide_gru : wide_gru + small_count].astype(F32)
    (
        norm1_gain, norm1_bias, norm2_gain, norm2_bias, b_gate, norm3_gain, norm3_bias,
        norm4_gain, norm4_bias,
    ) = (columns[:, i][None, :] for i in range(9))
    b_up = jnp.swapaxes(columns[:, 9:].reshape(shards, own_width, -1), 1, 2).reshape(1, -1)
    w_down = gather(w_down)
    if routed():
        first_taps = SpreadGather([w_conv[0], w_conv[1]])
        last_tap = SpreadGather([w_conv[2], jnp.concatenate([w_ftok, w_fchr], axis=1)])
    else:
        w_ftok = gather(w_ftok)
        w_fchr = gather(w_fchr)
        w_conv = gather(w_conv, 1)

    start = jnp.concatenate([jnp.zeros((batch, 1), jnp.int32), char_end[:, :-1] + 1], axis=1)
    change = (segment[:, 1:] != segment[:, :-1]).astype(F32)
    first = jnp.concatenate([jnp.broadcast_to((me == 0).astype(F32), (batch, 1)), change], axis=1)
    last = jnp.concatenate(
        [change, jnp.broadcast_to((me == count - 1).astype(F32), (batch, 1))], axis=1
    )
    flat_tokens = tokens.reshape(total_rows, width)
    chars_pad = jnp.pad(chars, ((0, 0), (0, padded_rows - char_rows), (0, 0)))
    chars_in = chars_pad
    if heads:
        sent = project_and_pack(tokens, w_qkv, segment, heads)
        chars_in = after(chars_pad, sent)
    gate, cand, decay, cum, state, edges = gru_forward(
        chars_in, w_gru, b_gate, start[:, None], first[:, None], char_end[:, None],
        last[:, None], char_rows,
    )

    if heads:
        everything = lax.all_to_all(sent, "ctx", 0, 0, tiled=True)
        everything = everything.reshape(count * rows, -1)
        packed_context, kept = attend(everything, edges, heads, rows)
        received = lax.all_to_all(packed_context.reshape(count, rows, -1), "ctx", 0, 0, tiled=True)
        context_b, edges_all = unpack(received, heads, 1, batch, True)
    else:
        qkv = matmul(flat_tokens, w_qkv).astype(BF16).reshape(batch, rows, -1)
        results = [gathered_attention(qkv[i], segment[i]) for i in range(batch)]
        context_b = jnp.concatenate([r[0].reshape(rows, width) for r in results]).astype(BF16)
        edges_all = all_edges(edges)

    attn = matmul(context_b, w_out)
    hidden1, kept1 = layer_norm(flat_tokens.astype(F32) + attn, norm1_gain, norm1_bias)
    hidden1_b = hidden1.astype(BF16)
    if routed():
        first_taps.double(4, sent)
        last_tap.double(1, sent)
        first_taps.place_own()
        last_tap.place_own()
        first_taps.double(2, state)
        last_tap.double(4, state)
        first_taps.double(1, packed_context)
        last_tap.double(2, packed_context)
        first_taps.cores(hidden1_b)
        last_tap.cores(hidden1_b)
        w_conv = [
            weight.reshape(-1, 2 * width) for weight in first_taps.finish() + last_tap.finish()
        ]
        w_ftok, w_fchr = w_conv[3][:, :width], w_conv[3][:, width:]
    inner_b, slope = feed_forward(hidden1_b, w_up, b_up)
    ffn = matmul(inner_b, w_down)
    hidden2, kept2 = layer_norm(hidden1 + ffn, norm2_gain, norm2_bias)
    hidden2_b = hidden2.astype(BF16)

    char_tok, enter = gather_states(
        state, cum, edges_all, char_end[:, :, None], start[:, :, None]
    )
    char_tok_b = char_tok.astype(BF16)
    joined = jnp.concatenate(
        [matmul(hidden2_b, w_ftok), matmul(char_tok_b, w_fchr)], axis=1
    ).astype(BF16)

    two = 2 * width
    blocks = joined.reshape(batch, rows, two)
    later, earlier = shifted(blocks, *neighbours(blocks))
    taps = (later.reshape(total_rows, two), joined, earlier.reshape(total_rows, two))
    conv = matmul(taps[1], w_conv[1]) + matmul(taps[0], w_conv[0]) + matmul(taps[2], w_conv[2])
    token_out, kept3 = layer_norm(hidden2 + conv[:, :width], norm3_gain, norm3_bias)
    char_out, kept4 = layer_norm(char_tok + conv[:, width:], norm4_gain, norm4_bias)

    d_in3, gain3_grad, bias3_grad = layer_norm_back(
        d_token.reshape(total_rows, width).astype(F32), norm3_gain, kept3
    )
    d_in4, gain4_grad, bias4_grad = layer_norm_back(
        d_char.reshape(total_rows, width).astype(F32), norm4_gain, kept4
    )
    d_conv = jnp.concatenate([d_in3, d_in4], axis=1).astype(BF16)
    d_before, d_after = neighbours(d_conv.reshape(batch, rows, two))
    d_later, d_earlier = shifted(d_conv.reshape(batch, rows, two), d_before, d_after)
    d_joined = (
        matmul_nt(d_conv, w_conv[1])
        + matmul_nt(d_earlier.reshape(total_rows, two), w_conv[0])
        + matmul_nt(d_later.reshape(total_rows, two), w_conv[2])
    ).astype(BF16)
    if routed():
        own_in = two // shards
        joined_own = after(joined, d_joined)
        joined_own = jnp.swapaxes(joined_own.reshape(total_rows, shards, own_in), 0, 1)
        joined_own = lax.all_to_all(joined_own, "fsdp", 0, 0, tiled=True).reshape(-1, own_in)
        d_all = gather(
            jnp.concatenate([d_conv.reshape(batch, rows, two), d_before, d_after], axis=1)
        )
        d_mid = d_all[:, :rows]
        d_sides = (
            jnp.concatenate([d_mid[:, 1:], d_all[:, rows + 1 :]], axis=1),
            d_mid,
            jnp.concatenate([d_all[:, rows : rows + 1], d_mid[:, :-1]], axis=1),
        )
    else:
        joined_own = joined
        conv_sum = plain_sum(jnp.stack([matmul_tn(tap, d_conv).astype(BF16) for tap in taps]), 1)

    d_tok_part, d_chr_part = d_joined[:, :width], d_joined[:, width:]
    d_hidden2 = d_in3 + matmul_nt(d_tok_part, w_ftok)
    d_char_tok = d_in4 + matmul_nt(d_chr_part, w_fchr)
    ftok_grad = matmul_tn(hidden2_b, d_tok_part).astype(BF16)
    fchr_grad = matmul_tn(char_tok_b, d_chr_part).astype(BF16)

    end_line, start_line = char_end[:, None], start[:, None]
    spread, back_cum, carried, back_edges = gru_back(
        d_char_tok.reshape(batch, rows, width), decay, end_line, start_line, char_rows
    )

    d_in2, gain2_grad, bias2_grad = layer_norm_back(d_hidden2, norm2_gain, kept2)
    d_ffn = d_in2.astype(BF16)
    down_grad = matmul_tn(inner_b, d_ffn).astype(BF16)
    reduced = over_fsdp if routed() else plain_sum
    second_sum = reduced(down_grad)
    d_pre = matmul_nt(d_ffn, w_down) * slope.astype(F32)
    bup_grad = jnp.sum(d_pre, axis=0)
    d_pre_low = d_pre.astype(BF16)
    d_hidden1 = d_in2 + matmul_nt(d_pre_low, w_up)
    d_in1, gain1_grad, bias1_grad = layer_norm_back(d_hidden1, norm1_gain, kept1)
    d_attn = d_in1.astype(BF16)
    if heads:
        sent = send_grad(d_attn, w_out, back_edges, heads, batch)
        hidden1_b, joined_own = after((hidden1_b, joined_own), sent)
    up_grad = matmul_tn(hidden1_b, d_pre_low).astype(BF16)
    wout_grad = matmul_tn(context_b, d_attn).astype(BF16)
    third_sum = reduced(jnp.concatenate([up_grad, wout_grad, ftok_grad, fchr_grad], axis=1))
    if routed():
        conv_chain = CtxSum(
            jnp.stack(
                [matmul_tn(joined_own, side.reshape(-1, two)).astype(BF16) for side in d_sides]
            )
        )
        conv_sent = conv_chain.advance()

    if heads:
        received = lax.all_to_all(sent, "ctx", 0, 0, tiled=True)
        if routed():
            received = after(received, conv_sent)
        packed_grad, back_enter = attend_back(
            everything, kept, received.reshape(count * rows, -1), edges_all, heads, rows
        )
        returned = lax.all_to_all(packed_grad.reshape(count, rows, -1), "ctx", 0, 0, tiled=True)
        (d_qkv,) = unpack(returned, heads, 3, batch, False)
    else:
        back_enter = back_entering(edges_all, all_edges(back_edges))
        d_context = matmul_nt(d_attn, w_out).reshape(batch, rows, width)
        d_qkv = jnp.concatenate(
            [
                gathered_attention_back(
                    qkv[i], segment[i], results[i][0], results[i][1], d_context[i]
                )
                for i in range(batch)
            ]
        )
    d_gate_in, bgate_grad = gru_grad(
        gate, cand, decay, cum, state, enter, spread, back_cum, carried, back_enter, char_rows
    )
    d_gate_in = d_gate_in.reshape(batch * padded_rows, -1)
    gru_weight_grad = matmul_tn(chars_pad.reshape(batch * padded_rows, width), d_gate_in)
    d_chars = matmul_nt(d_gate_in, w_gru[:, :wide_gru]).astype(BF16)
    d_chars = d_chars.reshape(batch, padded_rows, width)[:, :char_rows]

    qkv_grad = matmul_tn(flat_tokens, d_qkv).astype(BF16)
    d_tokens = (d_in1 + matmul_nt(d_qkv, w_qkv)).astype(BF16)

    small = jnp.stack(
        [
            gain1_grad, bias1_grad, gain2_grad, bias2_grad, jnp.sum(bgate_grad, axis=(0, 1)),
            gain3_grad, bias3_grad, gain4_grad, bias4_grad,
        ],
        axis=1,
    )
    up_small = bup_grad.reshape(shards, -1, width // shards)
    up_small = jnp.swapaxes(up_small, 1, 2).reshape(width, -1)
    small = jnp.concatenate([small, up_small], axis=1)
    small = jnp.pad(small, ((0, 0), (0, 128 - small_count)))
    fourth = jnp.concatenate([qkv_grad, gru_weight_grad.astype(BF16), small.astype(BF16)], axis=1)
    fourth_sum = reduced(fourth)

    widths = ((width,), (w_up.shape[1],) + (width,) * 3, (w_qkv.shape[1], wide_gru, 128))
    if routed():
        second_chain, third_chain, fourth_chain = (
            CtxSum(value) for value in (second_sum, third_sum, fourth_sum)
        )
        chains = dict(C=conv_chain, D=second_chain, T=third_chain, Q=fourth_chain)
        events = [chains[name] for name in ORDER]
        run_in_order(events, {ORDER.index("T"): (fourth,)})
        second_sum, third_sum, fourth_sum = (
            chain.result for chain in (second_chain, third_chain, fourth_chain)
        )
        (conv_sum,) = settle(conv_chain.result, (two,))
        (down_sum,), third, fourth = (
            settle(value, split)
            for value, split in zip((second_sum, third_sum, fourth_sum), widths)
        )
    else:
        (down_sum,), third, fourth = (
            jnp.split(value, [sum(split[:i]) for i in range(1, len(split))], axis=1)
            for value, split in zip((second_sum, third_sum, fourth_sum), widths)
        )
    vector = fourth[2]
    return (
        token_out.astype(BF16).reshape(batch, rows, width),
        char_out.astype(BF16).reshape(batch, rows, width),
        d_tokens.reshape(batch, rows, width),
        d_chars,
        fourth[0],
        third[1],
        vector[:, 0],
        vector[:, 1],
        third[0],
        jnp.swapaxes(vector[:, 9:small_count], 0, 1).reshape(-1),
        down_sum,
        vector[:, 2],
        vector[:, 3],
        fourth[1],
        vector[:, 4],
        third[2],
        third[3],
        conv_sum,
        vector[:, 5],
        vector[:, 6],
        vector[:, 7],
        vector[:, 8],
    )


def solution(mesh):
    rows = P("fsdp", "ctx", None)
    pairs = P("fsdp", "ctx")
    matrix = P("fsdp", None)
    vector = P("fsdp")
    weights = (
        matrix, matrix, vector, vector, matrix, vector, matrix, vector, vector, matrix, vector,
        matrix, matrix, P(None, "fsdp", None), vector, vector, vector, vector,
    )
    return jax.shard_map(
        local,
        mesh=mesh,
        in_specs=(rows, rows, pairs, pairs) + weights + (rows, rows),
        out_specs=(rows,) * 4 + weights,
        check_vma=False,
    )
```

profile of v0, /device:TPU:16, one launch (start us, length us, event | category | flops | bytes accessed | tf_op | source)
XLA Modules:
  0.0 631.6 jit_solution(8085978370138418450)
XLA Ops:
  18.8 4.5 slice_bitcast_fusion.2
  30.8 17.0 %all-gather.7.cloned.1.call-done.w_ref = bf16[768,2304]{1,0:T(8,128)(2,1)} async-done(((bf16[192,2304]{1,0:T(8,128)(2,1)}), bf16[768,2304]{1,0:T(8,128)(2,1)}) %all-gather.7.cloned.1.call-update) | async-done | bytes 3538960 | tf_op jit(solution)/shard_map/all_gather | solution.py:1005
  52.1 6.2 all-to-all-start
  59.7 20.2 %all-gather.9.cloned.1.call-done.w_ref = bf16[768,1664]{1,0:T(8,128)(2,1)} async-done(((bf16[192,1664]{1,0:T(8,128)(2,1)}), bf16[768,1664]{1,0:T(8,128)(2,1)}) %all-gather.9.cloned.1.call-update) | async-done | bytes 2555920 | tf_op jit(solution)/shard_map/all_gather | solution.py:1005
  85.3 2.7 gru_forward.1
  104.6 3.5 place_own.3
  121.8 6.2 attend.1
  132.6 4.3 all-to-all-start.1
  143.6 14.4 %collective-permute-done.3 = bf16[4,72,1536]{2,1,0:T(8,128)(2,1)} collective-permute-done((bf16[4,72,1536]{2,1,0:T(8,128)(2,1)}, bf16[4,72,1536]{2,1,0:T(8,128)(2,1)}, u32[]{:S(2)}, u32[]{:S(2)}) %collective-permute-start.3) | collective-permute-done | bytes 884768 | tf_op jit(solution)/shard_map/ppermute | solution.py:795
  170.4 5.4 feed_forward.1
  178.1 4.7 fusion.75
  187.5 7.1 %place.2 = (bf16[4,384,1536]{2,1,0:T(8,128)(2,1)S(1)}, bf16[4,192,1536]{2,1,0:T(8,128)(2,1)S(1)}) custom-call(bf16[8,72,1536]{2,1,0:T(8,128)(2,1)} %constant_dynamic-update-slice_fusion.2.piece_ref, bf16[8,72,1536]{2,1,0:T(8,128)(2,1)} %collective-permute-done.4.core_ref, ...), custom_call_target="tpu_custom_call", output_to_operand_aliasing={{0}: (2, {}), {1}: (3, {})} | custom-call | bytes 7077888 | tf_op jit(solution)/shard_map/place/pallas_call | solution.py:969
  198.1 2.9 collective-permute-start.12
  201.0 3.8 collective-permute-start.13
  208.7 2.6 fusion.79
  211.3 6.5 %place.3 = (bf16[4,384,1536]{2,1,0:T(8,128)(2,1)S(1)}, bf16[4,384,1536]{2,1,0:T(8,128)(2,1)S(1)}) custom-call(bf16[8,96,1536]{2,1,0:T(8,128)(2,1)S(1)} %constant_dynamic-update-slice_fusion.4.piece_ref, bf16[8,96,1536]{2,1,0:T(8,128)(2,1)S(1)} %collective-permute-done.10.core_ref, ...), custom_call_target="tpu_custom_call", output_to_operand_aliasing={{0}: (2, {}), {1}: (3, {})} | custom-call | bytes 9437184 | tf_op jit(solution)/shard_map/place/pallas_call | solution.py:969
  227.4 3.8 collective-permute-start.14
  231.2 3.0 collective-permute-start.15
  234.2 3.4 collective-permute-done.15
  242.1 3.9 fusion.80
  246.0 4.3 fusion.81
  254.9 3.6 convolution_convert_fusion
  260.6 4.2 all-to-all-start.3
  269.2 5.6 fusion.76
  284.3 3.0 convolution_convert_fusion.1
  287.3 3.7 pad_maximum_fusion
  291.1 6.3 all-to-all-start.2
  301.5 2.7 fusion.6
  304.3 2.6 fusion.7
  306.8 2.6 fusion.8
  313.8 15.5 %attend_back.1 = (bf16[1024,640]{1,0:T(8,128)(2,1)S(1)}, f32[2,1,768]{2,1,0:T(1,128)S(1)}) custom-call(bf16[1024,640]{1,0:T(8,128)(2,1)} %bitcast.2.all_ref.query_ref, f32[1024,384]{1,0:T(8,128)S(1)} %copy-done.59, bf16[1024,256]{1,0:T(8,128)(2,1)S(1)} %bitcast.193, f32[8,8,768]{2,1,0:T(8,128)S(1)} %copy-done.48), custom_call_target="tpu_custom_call" | custom-call | flops 5637144576 | bytes 4587520 | tf_op jit(solution)/shard_map/attend_back/pallas_call | solution.py:544
  330.4 6.1 all-to-all-start.4
  348.4 4.1 bitcast_convert_fusion
  352.5 12.1 %all-to-all-done.4.in_ref = bf16[8,128,640]{2,1,0:T(8,128)(2,1)S(1)} async-done(((bf16[8,128,640]{2,1,0:T(8,128)(2,1)}), bf16[8,128,640]{2,1,0:T(8,128)(2,1)S(1)}, u32[]{:S(2)}, u32[]{:S(2)}) %all-to-all-start.4) | async-done | bytes 1310752 | tf_op jit(solution)/shard_map/all_to_all | solution.py:1179
  366.7 2.9 fusion.1
  374.2 38.4 %collective-permute-done.17 = bf16[3,192,1536]{2,1,0:T(8,128)(2,1)} collective-permute-done((bf16[3,192,1536]{2,1,0:T(8,128)(2,1)S(1)}, bf16[3,192,1536]{2,1,0:T(8,128)(2,1)}, u32[]{:S(2)}, u32[]{:S(2)}) %collective-permute-start.17) | collective-permute-done | bytes 1769504 | tf_op jit(solution)/shard_map/ppermute | solution.py:795
  418.6 4.4 collective-permute-done.16
  424.4 4.1 collective-permute-start.18
  428.5 11.0 %collective-permute-done.19 = bf16[3,96,1536]{2,1,0:T(8,128)(2,1)} collective-permute-done((bf16[3,96,1536]{2,1,0:T(8,128)(2,1)}, bf16[3,96,1536]{2,1,0:T(8,128)(2,1)}, u32[]{:S(2)}, u32[]{:S(2)}) %collective-permute-start.19) | collective-permute-done | bytes 884768 | tf_op jit(solution)/shard_map/ppermute | solution.py:795
  442.6 3.1 collective-permute-done.18
  449.4 2.8 collective-permute-start.21
  452.2 11.2 %collective-permute-done.22 = bf16[3,48,1536]{2,1,0:T(8,128)(2,1)S(1)} collective-permute-done((bf16[3,48,1536]{2,1,0:T(8,128)(2,1)S(1)}, bf16[3,48,1536]{2,1,0:T(8,128)(2,1)S(1)}, u32[]{:S(2)}, u32[]{:S(2)}) %collective-permute-start.22) | collective-permute-done | bytes 442400 | tf_op jit(solution)/shard_map/ppermute | solution.py:795
  463.5 3.4 collective-permute-start.25
  471.3 10.3 %collective-permute-start.23 = (bf16[48,5376]{1,0:T(8,128)(2,1)}, bf16[48,5376]{1,0:T(8,128)(2,1)}, u32[]{:S(2)}, u32[]{:S(2)}) collective-permute-start(bf16[48,5376]{1,0:T(8,128)(2,1)} %constant_dynamic-slice_fusion.4), channel_id=1, source_target_pairs={{0,8},{4,12},{8,0},{12,4},{16,24},{20,28},{24,16},{28,20},{1,9},{5... | collective-permute-start | bytes 1548296 | tf_op jit(solution)/shard_map/ppermute | solution.py:795
  482.6 8.2 %collective-permute-start.28 = (bf16[2,3,48,1536]{3,2,1,0:T(8,128)(2,1)}, bf16[2,3,48,1536]{3,2,1,0:T(8,128)(2,1)}, u32[]{:S(2)}, u32[]{:S(2)}) collective-permute-start(bf16[2,3,48,1536]{3,2,1,0:T(8,128)(2,1)} %pad_maximum_fusion.14), channel_id=1, source_target_pairs={{0,8},{4,12},{8,0},{12,4},{16,24},{20,28},{24,16},{28,20},{1,9},{5... | collective-permute-start | bytes 2654216 | tf_op jit(solution)/shard_map/ppermute | solution.py:795
  490.9 6.7 %collective-permute-done.24 = bf16[1,96,768]{2,1,0:T(8,128)(2,1)S(1)} collective-permute-done((bf16[1,96,768]{2,1,0:T(8,128)(2,1)S(1)}, bf16[1,96,768]{2,1,0:T(8,128)(2,1)S(1)}, u32[]{:S(2)}, u32[]{:S(2)}) %collective-permute-start.24) | collective-permute-done | bytes 147488 | tf_op jit(solution)/shard_map/ppermute | solution.py:795
  502.6 3.2 collective-permute-start.26
  508.7 14.3 %collective-permute-done.28 = bf16[2,3,48,1536]{3,2,1,0:T(8,128)(2,1)} collective-permute-done((bf16[2,3,48,1536]{3,2,1,0:T(8,128)(2,1)}, bf16[2,3,48,1536]{3,2,1,0:T(8,128)(2,1)}, u32[]{:S(2)}, u32[]{:S(2)}) %collective-permute-start.28) | collective-permute-done | bytes 884768 | tf_op jit(solution)/shard_map/ppermute | solution.py:795
  524.4 3.3 collective-permute-start.36
  532.2 2.5 collective-permute-start.29
  534.9 11.4 %collective-permute-done.29 = bf16[48,3968]{1,0:T(8,128)(2,1)S(1)} collective-permute-done((bf16[48,3968]{1,0:T(8,128)(2,1)S(1)}, bf16[48,3968]{1,0:T(8,128)(2,1)S(1)}, u32[]{:S(2)}, u32[]{:S(2)}) %collective-permute-start.29) | collective-permute-done | bytes 380960 | tf_op jit(solution)/shard_map/ppermute | solution.py:795
  546.6 4.2 collective-permute-start.35
  550.8 4.4 collective-permute-done.31
  555.2 3.5 collective-permute-start.33
  558.7 8.5 %collective-permute-done.36 = bf16[4,3,48,1536]{3,2,1,0:T(8,128)(2,1)S(1)} collective-permute-done((bf16[4,3,48,1536]{3,2,1,0:T(8,128)(2,1)S(1)}, bf16[4,3,48,1536]{3,2,1,0:T(8,128)(2,1)S(1)}, u32[]{:S(2)}, u32[]{:S(2)}) %collective-permute-start.36) | collective-permute-done | bytes 1769504 | tf_op jit(solution)/shard_map/ppermute | solution.py:795
  568.7 8.8 %collective-permute-done.34 = bf16[4,96,768]{2,1,0:T(8,128)(2,1)S(1)} collective-permute-done((bf16[4,96,768]{2,1,0:T(8,128)(2,1)S(1)}, bf16[4,96,768]{2,1,0:T(8,128)(2,1)S(1)}, u32[]{:S(2)}, u32[]{:S(2)}) %collective-permute-start.34) | collective-permute-done | bytes 589856 | tf_op jit(solution)/shard_map/ppermute | solution.py:795
  577.7 2.5 collective-permute-start.37
  582.8 4.3 collective-permute-done.37
  589.2 3.6 settle.6
  592.8 4.7 settle.7
  597.5 8.5 %collective-permute-done.39 = bf16[4,24,5376]{2,1,0:T(8,128)(2,1)S(1)} collective-permute-done((bf16[4,24,5376]{2,1,0:T(8,128)(2,1)S(1)}, bf16[4,24,5376]{2,1,0:T(8,128)(2,1)S(1)}, u32[]{:S(2)}, u32[]{:S(2)}) %collective-permute-start.39) | collective-permute-done | bytes 1032224 | tf_op jit(solution)/shard_map/ppermute | solution.py:795
  606.2 4.0 settle.5
  610.2 8.7 %collective-permute-done.38 = bf16[4,24,3968]{2,1,0:T(8,128)(2,1)S(1)} collective-permute-done((bf16[4,24,3968]{2,1,0:T(8,128)(2,1)S(1)}, bf16[4,24,3968]{2,1,0:T(8,128)(2,1)S(1)}, u32[]{:S(2)}, u32[]{:S(2)}) %collective-permute-start.38) | collective-permute-done | bytes 761888 | tf_op jit(solution)/shard_map/ppermute | solution.py:795
  619.0 3.7 settle.4
  (550 shorter events, 202.3 us)
Async XLA Ops:
  7.2 40.6 %all-gather.7.cloned.1.call-start = ((), (), s32[]{:S(2)}) async-start(), calls=%async_computation.8 | async-start | bytes 4423680 | tf_op jit(solution)/shard_map/all_gather | solution.py:1005
  7.9 71.9 %all-gather.9.cloned.1.call-start = ((), (), s32[]{:S(2)}) async-start(), calls=%async_computation.9 | async-start | bytes 3194880 | tf_op jit(solution)/shard_map/all_gather | solution.py:1005
  16.8 145.0 %all-gather.11.cloned.1.call-start = ((), (), s32[]{:S(2)}) async-start(), calls=%async_computation.10 | async-start | bytes 1474560 | tf_op jit(solution)/shard_map/all_gather | solution.py:1005
  17.6 150.5 %all-gather.13.cloned.1.call-start = ((), (), s32[]{:S(2)}) async-start(), calls=%async_computation.11 | async-start | bytes 5898240 | tf_op jit(solution)/shard_map/all_gather | solution.py:1005
  18.1 160.0 %all-gather.15.cloned.1.call-start = ((), (), s32[]{:S(2)}) async-start(), calls=%async_computation.12 | async-start | bytes 5898240 | tf_op jit(solution)/shard_map/all_gather | solution.py:1005
  25.0 59.7 %collective-permute-start.6 = (bf16[96,1536]{1,0:T(8,128)(2,1)}, bf16[96,1536]{1,0:T(8,128)(2,1)}, u32[]{:S(2)}, u32[]{:S(2)}) collective-permute-start(bf16[96,1536]{1,0:T(8,128)(2,1)} %pad_maximum_fusion.27), channel_id=1, source_target_pairs={{0,2},{1,3},{2,0},{3,1},{4,6},{5,7},{6,4},{7,5},{8,10},{9,11},{10,... | collective-permute-start | bytes 884744 | tf_op jit(solution)/shard_map/ppermute | solution.py:795
  28.0 76.6 %collective-permute-start.11 = (bf16[768,1536]{1,0:T(8,128)(2,1)}, bf16[768,1536]{1,0:T(8,128)(2,1)}, u32[]{:S(2)}, u32[]{:S(2)}) collective-permute-start(bf16[768,1536]{1,0:T(8,128)(2,1)} %pad_maximum_fusion.5.own_ref), channel_id=1, source_target_pairs={{0,1},{1,0},{2,3},{3,2},{4,5},{5,4},{6,7},{7,6},{8,9},{9,8},{10,11... | collective-permute-start | bytes 7077896 | tf_op jit(solution)/shard_map/ppermute | solution.py:795
  29.4 22.6 %copy-start = (bf16[576,1536]{1,0:T(8,128)(2,1)}, bf16[576,1536]{1,0:T(8,128)(2,1)S(1)}, u32[]{:S(2)}) copy-start(bf16[576,1536]{1,0:T(8,128)(2,1)S(1)} %pad_maximum_fusion.7.own_ref) | copy-start | bytes 5308420
  29.4 69.3 %collective-permute-start.5 = (bf16[576,1536]{1,0:T(8,128)(2,1)S(1)}, bf16[576,1536]{1,0:T(8,128)(2,1)}, u32[]{:S(2)}, u32[]{:S(2)}) collective-permute-start(bf16[576,1536]{1,0:T(8,128)(2,1)S(1)} %pad_maximum_fusion.7.own_ref), channel_id=1, source_target_pairs={{0,1},{1,0},{2,3},{3,2},{4,5},{5,4},{6,7},{7,6},{8,9},{9,8},{10,11... | collective-permute-start | bytes 5308424 | tf_op jit(solution)/shard_map/ppermute | solution.py:795
  52.1 69.7 %all-to-all-start = ((bf16[8,128,640]{2,1,0:T(8,128)(2,1)}), bf16[8,128,640]{2,1,0:T(8,128)(2,1)}, u32[]{:S(2)}, u32[]{:S(2)}) async-start(bf16[8,128,640]{2,1,0:T(8,128)(2,1)} %project.1), calls=%async_computation | async-start | bytes 2621440 | tf_op jit(solution)/shard_map/all_to_all | solution.py:1054
  58.2 22.6 %collective-permute-start = (bf16[72,1536]{1,0:T(8,128)(2,1)S(1)}, bf16[72,1536]{1,0:T(8,128)(2,1)}, u32[]{:S(2)}, u32[]{:S(2)}) collective-permute-start(bf16[72,1536]{1,0:T(8,128)(2,1)S(1)} %pad_maximum_fusion.29), channel_id=1, source_target_pairs={{0,2},{1,3},{2,0},{3,1},{4,6},{5,7},{6,4},{7,5},{8,10},{9,11},{10,... | collective-permute-start | bytes 663560 | tf_op jit(solution)/shard_map/ppermute | solution.py:795
  59.1 26.2 %copy-start.50 = (s32[2,128]{1,0:T(2,128)}, s32[2,128]{1,0:T(2,128)S(1)}, u32[]{:S(2)}) copy-start(s32[2,128]{1,0:T(2,128)S(1)} %get-tuple-element.235) | copy-start | bytes 3076
  80.9 12.1 %collective-permute-start.1 = (bf16[1,72,1536]{2,1,0:T(8,128)(2,1)}, bf16[1,72,1536]{2,1,0:T(8,128)(2,1)S(1)}, u32[]{:S(2)}, u32[]{:S(2)}) collective-permute-start(bf16[1,72,1536]{2,1,0:T(8,128)(2,1)} %bitcast.13), channel_id=1, source_target_pairs={{0,4},{4,0},{8,12},{12,8},{16,20},{20,16},{24,28},{28,24},{1,5},{5... | collective-permute-start | bytes 663560 | tf_op jit(solution)/shard_map/ppermute | solution.py:795
  84.7 30.2 %copy-start.103 = (f32[768]{0:T(1024)}, f32[768]{0:T(1024)S(1)}, u32[]{:S(2)}) copy-start(f32[768]{0:T(1024)S(1)} %get-tuple-element.189) | copy-start | bytes 9220
  84.7 30.2 %copy-start.105 = (f32[768]{0:T(1024)}, f32[768]{0:T(1024)S(1)}, u32[]{:S(2)}) copy-start(f32[768]{0:T(1024)S(1)} %get-tuple-element.186) | copy-start | bytes 9220
  84.7 31.6 %collective-permute-start.7 = (bf16[1,96,1536]{2,1,0:T(8,128)(2,1)}, bf16[1,96,1536]{2,1,0:T(8,128)(2,1)S(1)}, u32[]{:S(2)}, u32[]{:S(2)}) collective-permute-start(bf16[1,96,1536]{2,1,0:T(8,128)(2,1)} %bitcast.20), channel_id=1, source_target_pairs={{0,16},{4,20},{8,24},{12,28},{16,0},{20,4},{24,8},{28,12},{1,17},{... | collective-permute-start | bytes 884744 | tf_op jit(solution)/shard_map/ppermute | solution.py:795
  94.7 24.9 %collective-permute-start.2 = (bf16[2,72,1536]{2,1,0:T(8,128)(2,1)}, bf16[2,72,1536]{2,1,0:T(8,128)(2,1)}, u32[]{:S(2)}, u32[]{:S(2)}) collective-permute-start(bf16[2,72,1536]{2,1,0:T(8,128)(2,1)} %pad_maximum_fusion.25), channel_id=1, source_target_pairs={{0,16},{4,20},{8,24},{12,28},{16,0},{20,4},{24,8},{28,12},{1,17},{... | collective-permute-start | bytes 1327112 | tf_op jit(solution)/shard_map/ppermute | solution.py:795
  118.1 19.5 %collective-permute-start.8 = (bf16[2,96,1536]{2,1,0:T(8,128)(2,1)}, bf16[2,96,1536]{2,1,0:T(8,128)(2,1)}, u32[]{:S(2)}, u32[]{:S(2)}) collective-permute-start(bf16[2,96,1536]{2,1,0:T(8,128)(2,1)} %pad_maximum_fusion.22), channel_id=1, source_target_pairs={{0,8},{4,12},{8,0},{12,4},{16,24},{20,28},{24,16},{28,20},{1,9},{5... | collective-permute-start | bytes 1769480 | tf_op jit(solution)/shard_map/ppermute | solution.py:795
  130.0 28.0 %collective-permute-start.3 = (bf16[4,72,1536]{2,1,0:T(8,128)(2,1)}, bf16[4,72,1536]{2,1,0:T(8,128)(2,1)}, u32[]{:S(2)}, u32[]{:S(2)}) collective-permute-start(bf16[4,72,1536]{2,1,0:T(8,128)(2,1)} %pad_maximum_fusion.13), channel_id=1, source_target_pairs={{0,8},{4,12},{8,0},{12,4},{16,24},{20,28},{24,16},{28,20},{1,9},{5... | collective-permute-start | bytes 2654216 | tf_op jit(solution)/shard_map/ppermute | solution.py:795
  132.6 27.5 %all-to-all-start.1 = ((bf16[8,128,256]{2,1,0:T(8,128)(2,1)}), bf16[8,128,256]{2,1,0:T(8,128)(2,1)S(1)}, u32[]{:S(2)}, u32[]{:S(2)}) async-start(bf16[8,128,256]{2,1,0:T(8,128)(2,1)} %bitcast.194), calls=%async_computation.1 | async-start | bytes 1048576 | tf_op jit(solution)/shard_map/all_to_all | solution.py:1057
  136.9 160.5 %all-gather.17.cloned.1.call-start = ((), (), s32[]{:S(2)}) async-start(), calls=%async_computation.13 | async-start | bytes 4177920 | tf_op jit(solution)/shard_map/all_gather | solution.py:1005
  140.0 42.8 %collective-permute-start.9 = (bf16[4,96,1536]{2,1,0:T(8,128)(2,1)}, bf16[4,96,1536]{2,1,0:T(8,128)(2,1)}, u32[]{:S(2)}, u32[]{:S(2)}) collective-permute-start(bf16[4,96,1536]{2,1,0:T(8,128)(2,1)} %pad_maximum_fusion.10), channel_id=1, source_target_pairs={{0,4},{4,0},{8,12},{12,8},{16,20},{20,16},{24,28},{28,24},{1,5},{5... | collective-permute-start | bytes 3538952 | tf_op jit(solution)/shard_map/ppermute | solution.py:795
  164.3 20.8 %collective-permute-start.4 = (bf16[8,72,1536]{2,1,0:T(8,128)(2,1)}, bf16[8,72,1536]{2,1,0:T(8,128)(2,1)}, u32[]{:S(2)}, u32[]{:S(2)}) collective-permute-start(bf16[8,72,1536]{2,1,0:T(8,128)(2,1)} %constant_dynamic-update-slice_fusion.2.piece_ref), channel_id=1, source_target_pairs={{0,1},{1,0},{2,3},{3,2},{4,5},{5,4},{6,7},{7,6},{8,9},{9,8},{10,11... | collective-permute-start | bytes 5308424 | tf_op jit(solution)/shard_map/ppermute | solution.py:795
  182.8 39.0 %copy-start.64 = (f32[256,768]{1,0:T(8,128)}, f32[256,768]{1,0:T(8,128)S(1)}, u32[]{:S(2)}) copy-start(f32[256,768]{1,0:T(8,128)S(1)} %get-tuple-element.241) | copy-start | bytes 2359300
  182.8 39.0 %copy-start.113 = (f32[256]{0:T(256)}, f32[256]{0:T(256)S(1)}, u32[]{:S(2)}) copy-start(f32[256]{0:T(256)S(1)} %broadcast_multiply_fusion.8) | copy-start | bytes 3076
  184.5 26.8 %collective-permute-start.10 = (bf16[8,96,1536]{2,1,0:T(8,128)(2,1)S(1)}, bf16[8,96,1536]{2,1,0:T(8,128)(2,1)S(1)}, u32[]{:S(2)}, u32[]{:S(2)}) collective-permute-start(bf16[8,96,1536]{2,1,0:T(8,128)(2,1)S(1)} %constant_dynamic-update-slice_fusion.4.piece_ref), channel_id=1, source_target_pairs={{0,1},{1,0},{2,3},{3,2},{4,5},{5,4},{6,7},{7,6},{8,9},{9,8},{10,11... | collective-permute-start | bytes 7077896 | tf_op jit(solution)/shard_map/ppermute | solution.py:795
  185.1 36.7 %copy-start.120 = (f32[256]{0:T(256)}, f32[256]{0:T(256)S(1)}, u32[]{:S(2)}) copy-start(f32[256]{0:T(256)S(1)} %add_rsqrt_fusion.2) | copy-start | bytes 3076
  187.5 23.8 %slice-start.2 = ((s8[4718592]{0:T(1024)(128)(4,1)}), s8[4194304]{0:T(1024)(128)(4,1)S(1)}, s32[]{:S(2)}) async-start(s8[4718592]{0:T(1024)(128)(4,1)} %bitcast.179), calls=%async_computation.19 | async-start | bytes 8388608
  197.2 22.7 %copy-start.71 = (bf16[256,768]{1,0:T(8,128)(2,1)}, bf16[256,768]{1,0:T(8,128)(2,1)S(1)}, u32[]{:S(2)}) copy-start(bf16[256,768]{1,0:T(8,128)(2,1)S(1)} %convolution_convert_fusion.9) | copy-start | bytes 1179652
  198.1 7.0 %collective-permute-start.12 = (bf16[2,1536]{1,0:T(2,128)(2,1)S(1)}, bf16[2,1536]{1,0:T(2,128)(2,1)S(1)}, u32[]{:S(2)}, u32[]{:S(2)}) collective-permute-start(bf16[2,1536]{1,0:T(2,128)(2,1)S(1)} %bitcast.232), channel_id=1, source_target_pairs={{0,4},{4,8},{8,12},{12,16},{16,20},{20,24},{24,28},{1,5},{5,9},{9,... | collective-permute-start | bytes 18440 | tf_op jit(solution)/shard_map/ppermute | solution.py:775
  201.0 6.5 %collective-permute-start.13 = (bf16[2,1536]{1,0:T(2,128)(2,1)S(1)}, bf16[2,1536]{1,0:T(2,128)(2,1)S(1)}, u32[]{:S(2)}, u32[]{:S(2)}) collective-permute-start(bf16[2,1536]{1,0:T(2,128)(2,1)S(1)} %bitcast.234), channel_id=1, source_target_pairs={{4,0},{8,4},{12,8},{16,12},{20,16},{24,20},{28,24},{5,1},{9,5},{13... | collective-permute-start | bytes 18440 | tf_op jit(solution)/shard_map/ppermute | solution.py:776
  227.4 6.8 %collective-permute-start.14 = (bf16[2,1536]{1,0:T(2,128)(2,1)S(1)}, bf16[2,1536]{1,0:T(2,128)(2,1)S(1)}, u32[]{:S(2)}, u32[]{:S(2)}) collective-permute-start(bf16[2,1536]{1,0:T(2,128)(2,1)S(1)} %bitcast.236), channel_id=1, source_target_pairs={{4,0},{8,4},{12,8},{16,12},{20,16},{24,20},{28,24},{5,1},{9,5},{13... | collective-permute-start | bytes 18440 | tf_op jit(solution)/shard_map/ppermute | solution.py:776
  231.2 6.4 %collective-permute-start.15 = (bf16[2,1536]{1,0:T(2,128)(2,1)S(1)}, bf16[2,1536]{1,0:T(2,128)(2,1)S(1)}, u32[]{:S(2)}, u32[]{:S(2)}) collective-permute-start(bf16[2,1536]{1,0:T(2,128)(2,1)S(1)} %bitcast.238), channel_id=1, source_target_pairs={{0,4},{4,8},{8,12},{12,16},{16,20},{20,24},{24,28},{1,5},{5,9},{9,... | collective-permute-start | bytes 18440 | tf_op jit(solution)/shard_map/ppermute | solution.py:775
  239.2 133.2 %reduce-scatter.8.cloned.1.call-start = ((), (), s32[]{:S(2)}) async-start(), calls=%async_computation.16 | async-start | bytes 5898240 | tf_op jit(solution)/shard_map/reduce_scatter | solution.py:983
  260.6 23.7 %all-to-all-start.3 = ((bf16[4,256,384]{2,1,0:T(8,128)(2,1)}), bf16[4,256,384]{2,1,0:T(8,128)(2,1)}, u32[]{:S(2)}, u32[]{:S(2)}) async-start(bf16[4,256,384]{2,1,0:T(8,128)(2,1)} %bitcast.218), calls=%async_computation.3 | async-start | bytes 1572864 | tf_op jit(solution)/shard_map/all_to_all | solution.py:1122
  264.8 181.0 %reduce-scatter.6.cloned.1.call-start = ((), (), s32[]{:S(2)}) async-start(), calls=%async_computation.15 | async-start | bytes 10321920 | tf_op jit(solution)/shard_map/reduce_scatter | solution.py:983
  291.1 21.9 %all-to-all-start.2 = ((bf16[8,128,256]{2,1,0:T(8,128)(2,1)}), bf16[8,128,256]{2,1,0:T(8,128)(2,1)S(1)}, u32[]{:S(2)}, u32[]{:S(2)}) async-start(bf16[8,128,256]{2,1,0:T(8,128)(2,1)} %send_grad.1), calls=%async_computation.2 | async-start | bytes 1048576 | tf_op jit(solution)/shard_map/all_to_all | solution.py:1173
  330.4 34.2 %all-to-all-start.4 = ((bf16[8,128,640]{2,1,0:T(8,128)(2,1)}), bf16[8,128,640]{2,1,0:T(8,128)(2,1)S(1)}, u32[]{:S(2)}, u32[]{:S(2)}) async-start(bf16[8,128,640]{2,1,0:T(8,128)(2,1)} %bitcast.192), calls=%async_computation.4 | async-start | bytes 2621440 | tf_op jit(solution)/shard_map/all_to_all | solution.py:1179
  336.5 164.0 %reduce-scatter.4.cloned.1.call-start = ((), (), s32[]{:S(2)}) async-start(), calls=%async_computation.14 | async-start | bytes 7618560 | tf_op jit(solution)/shard_map/reduce_scatter | solution.py:983
  371.0 41.6 %collective-permute-start.17 = (bf16[3,192,1536]{2,1,0:T(8,128)(2,1)S(1)}, bf16[3,192,1536]{2,1,0:T(8,128)(2,1)}, u32[]{:S(2)}, u32[]{:S(2)}) collective-permute-start(bf16[3,192,1536]{2,1,0:T(8,128)(2,1)S(1)} %copy-done.90), channel_id=1, source_target_pairs={{0,4},{4,0},{8,12},{12,8},{16,20},{20,16},{24,28},{28,24},{1,5},{5... | collective-permute-start | bytes 5308424 | tf_op jit(solution)/shard_map/ppermute | solution.py:795
  373.6 49.4 %collective-permute-start.16 = (bf16[384,768]{1,0:T(8,128)(2,1)S(1)}, bf16[384,768]{1,0:T(8,128)(2,1)}, u32[]{:S(2)}, u32[]{:S(2)}) collective-permute-start(bf16[384,768]{1,0:T(8,128)(2,1)S(1)} %constant_dynamic-slice_fusion.10), channel_id=1, source_target_pairs={{0,4},{4,0},{8,12},{12,8},{16,20},{20,16},{24,28},{28,24},{1,5},{5... | collective-permute-start | bytes 1769480 | tf_op jit(solution)/shard_map/ppermute | solution.py:795
  416.1 23.4 %collective-permute-start.19 = (bf16[3,96,1536]{2,1,0:T(8,128)(2,1)}, bf16[3,96,1536]{2,1,0:T(8,128)(2,1)}, u32[]{:S(2)}, u32[]{:S(2)}) collective-permute-start(bf16[3,96,1536]{2,1,0:T(8,128)(2,1)} %constant_dynamic-slice_fusion.9), channel_id=1, source_target_pairs={{0,8},{4,12},{8,0},{12,4},{16,24},{20,28},{24,16},{28,20},{1,9},{5... | collective-permute-start | bytes 2654216 | tf_op jit(solution)/shard_map/ppermute | solution.py:795
  424.4 21.3 %collective-permute-start.18 = (bf16[192,768]{1,0:T(8,128)(2,1)S(1)}, bf16[192,768]{1,0:T(8,128)(2,1)S(1)}, u32[]{:S(2)}, u32[]{:S(2)}) collective-permute-start(bf16[192,768]{1,0:T(8,128)(2,1)S(1)} %constant_dynamic-slice_fusion.8), channel_id=1, source_target_pairs={{0,8},{4,12},{8,0},{12,4},{16,24},{20,28},{24,16},{28,20},{1,9},{5... | collective-permute-start | bytes 884744 | tf_op jit(solution)/shard_map/ppermute | solution.py:795
  441.9 21.5 %collective-permute-start.22 = (bf16[3,48,1536]{2,1,0:T(8,128)(2,1)S(1)}, bf16[3,48,1536]{2,1,0:T(8,128)(2,1)S(1)}, u32[]{:S(2)}, u32[]{:S(2)}) collective-permute-start(bf16[3,48,1536]{2,1,0:T(8,128)(2,1)S(1)} %constant_dynamic-slice_fusion.7), channel_id=1, source_target_pairs={{0,16},{4,20},{8,24},{12,28},{16,0},{20,4},{24,8},{28,12},{1,17},{... | collective-permute-start | bytes 1327112 | tf_op jit(solution)/shard_map/ppermute | solution.py:795
  448.1 20.6 %collective-permute-start.20 = (bf16[96,5376]{1,0:T(8,128)(2,1)}, bf16[96,5376]{1,0:T(8,128)(2,1)}, u32[]{:S(2)}, u32[]{:S(2)}) collective-permute-start(bf16[96,5376]{1,0:T(8,128)(2,1)} %constant_dynamic-slice_fusion.5), channel_id=1, source_target_pairs={{0,4},{4,0},{8,12},{12,8},{16,20},{20,16},{24,28},{28,24},{1,5},{5... | collective-permute-start | bytes 3096584 | tf_op jit(solution)/shard_map/ppermute | solution.py:795
  449.4 17.6 %collective-permute-start.21 = (bf16[96,768]{1,0:T(8,128)(2,1)S(1)}, bf16[96,768]{1,0:T(8,128)(2,1)S(1)}, u32[]{:S(2)}, u32[]{:S(2)}) collective-permute-start(bf16[96,768]{1,0:T(8,128)(2,1)S(1)} %constant_dynamic-slice_fusion.6), channel_id=1, source_target_pairs={{0,16},{4,20},{8,24},{12,28},{16,0},{20,4},{24,8},{28,12},{1,17},{... | collective-permute-start | bytes 442376 | tf_op jit(solution)/shard_map/ppermute | solution.py:795
  463.5 18.1 %collective-permute-start.25 = (bf16[1,3,48,1536]{3,2,1,0:T(8,128)(2,1)S(1)}, bf16[1,3,48,1536]{3,2,1,0:T(8,128)(2,1)S(1)}, u32[]{:S(2)}, u32[]{:S(2)}) collective-permute-start(bf16[1,3,48,1536]{3,2,1,0:T(8,128)(2,1)S(1)} %fusion.46), channel_id=1, source_target_pairs={{0,16},{4,20},{8,24},{12,28},{16,0},{20,4},{24,8},{28,12},{1,17},{... | collective-permute-start | bytes 1327112 | tf_op jit(solution)/shard_map/ppermute | solution.py:795
  471.3 27.2 %collective-permute-start.23 = (bf16[48,5376]{1,0:T(8,128)(2,1)}, bf16[48,5376]{1,0:T(8,128)(2,1)}, u32[]{:S(2)}, u32[]{:S(2)}) collective-permute-start(bf16[48,5376]{1,0:T(8,128)(2,1)} %constant_dynamic-slice_fusion.4), channel_id=1, source_target_pairs={{0,8},{4,12},{8,0},{12,4},{16,24},{20,28},{24,16},{28,20},{1,9},{5... | collective-permute-start | bytes 1548296 | tf_op jit(solution)/shard_map/ppermute | solution.py:795
  481.6 16.0 %collective-permute-start.24 = (bf16[1,96,768]{2,1,0:T(8,128)(2,1)S(1)}, bf16[1,96,768]{2,1,0:T(8,128)(2,1)S(1)}, u32[]{:S(2)}, u32[]{:S(2)}) collective-permute-start(bf16[1,96,768]{2,1,0:T(8,128)(2,1)S(1)} %fusion.57), channel_id=1, source_target_pairs={{0,16},{4,20},{8,24},{12,28},{16,0},{20,4},{24,8},{28,12},{1,17},{... | collective-permute-start | bytes 442376 | tf_op jit(solution)/shard_map/ppermute | solution.py:795
  482.6 40.4 %collective-permute-start.28 = (bf16[2,3,48,1536]{3,2,1,0:T(8,128)(2,1)}, bf16[2,3,48,1536]{3,2,1,0:T(8,128)(2,1)}, u32[]{:S(2)}, u32[]{:S(2)}) collective-permute-start(bf16[2,3,48,1536]{3,2,1,0:T(8,128)(2,1)} %pad_maximum_fusion.14), channel_id=1, source_target_pairs={{0,8},{4,12},{8,0},{12,4},{16,24},{20,28},{24,16},{28,20},{1,9},{5... | collective-permute-start | bytes 2654216 | tf_op jit(solution)/shard_map/ppermute | solution.py:795
  502.6 28.2 %collective-permute-start.26 = (bf16[96,3968]{1,0:T(8,128)(2,1)}, bf16[96,3968]{1,0:T(8,128)(2,1)}, u32[]{:S(2)}, u32[]{:S(2)}) collective-permute-start(bf16[96,3968]{1,0:T(8,128)(2,1)} %constant_dynamic-slice_fusion.2), channel_id=1, source_target_pairs={{0,4},{4,0},{8,12},{12,8},{16,20},{20,16},{24,28},{28,24},{1,5},{5... | collective-permute-start | bytes 2285576 | tf_op jit(solution)/shard_map/ppermute | solution.py:795
  505.8 23.3 %collective-permute-start.27 = (bf16[2,96,768]{2,1,0:T(8,128)(2,1)S(1)}, bf16[2,96,768]{2,1,0:T(8,128)(2,1)S(1)}, u32[]{:S(2)}, u32[]{:S(2)}) collective-permute-start(bf16[2,96,768]{2,1,0:T(8,128)(2,1)S(1)} %copy-done.101), channel_id=1, source_target_pairs={{0,8},{4,12},{8,0},{12,4},{16,24},{20,28},{24,16},{28,20},{1,9},{5... | collective-permute-start | bytes 884744 | tf_op jit(solution)/shard_map/ppermute | solution.py:795
  508.3 22.5 %copy-start.92 = (bf16[192,3968]{1,0:T(8,128)(2,1)S(1)}, bf16[192,3968]{1,0:T(8,128)(2,1)}, u32[]{:S(2)}) copy-start(bf16[192,3968]{1,0:T(8,128)(2,1)} %reduce-scatter.4.cloned.1.call-done) | copy-start | bytes 4571140
  508.3 26.4 %collective-permute-start.30 = (bf16[24,5376]{1,0:T(8,128)(2,1)S(1)}, bf16[24,5376]{1,0:T(8,128)(2,1)S(1)}, u32[]{:S(2)}, u32[]{:S(2)}) collective-permute-start(bf16[24,5376]{1,0:T(8,128)(2,1)S(1)} %constant_dynamic-slice_fusion.3), channel_id=1, source_target_pairs={{0,16},{4,20},{8,24},{12,28},{16,0},{20,4},{24,8},{28,12},{1,17},{... | collective-permute-start | bytes 774152 | tf_op jit(solution)/shard_map/ppermute | solution.py:795
  524.4 42.8 %collective-permute-start.36 = (bf16[4,3,48,1536]{3,2,1,0:T(8,128)(2,1)S(1)}, bf16[4,3,48,1536]{3,2,1,0:T(8,128)(2,1)S(1)}, u32[]{:S(2)}, u32[]{:S(2)}) collective-permute-start(bf16[4,3,48,1536]{3,2,1,0:T(8,128)(2,1)S(1)} %pad_maximum_fusion.8), channel_id=1, source_target_pairs={{0,4},{4,0},{8,12},{12,8},{16,20},{20,16},{24,28},{28,24},{1,5},{5... | collective-permute-start | bytes 5308424 | tf_op jit(solution)/shard_map/ppermute | solution.py:795
  529.2 48.3 %collective-permute-start.34 = (bf16[4,96,768]{2,1,0:T(8,128)(2,1)S(1)}, bf16[4,96,768]{2,1,0:T(8,128)(2,1)S(1)}, u32[]{:S(2)}, u32[]{:S(2)}) collective-permute-start(bf16[4,96,768]{2,1,0:T(8,128)(2,1)S(1)} %pad_maximum_fusion.23), channel_id=1, source_target_pairs={{0,4},{4,0},{8,12},{12,8},{16,20},{20,16},{24,28},{28,24},{1,5},{5... | collective-permute-start | bytes 1769480 | tf_op jit(solution)/shard_map/ppermute | solution.py:795
  532.2 14.1 %collective-permute-start.29 = (bf16[48,3968]{1,0:T(8,128)(2,1)S(1)}, bf16[48,3968]{1,0:T(8,128)(2,1)S(1)}, u32[]{:S(2)}, u32[]{:S(2)}) collective-permute-start(bf16[48,3968]{1,0:T(8,128)(2,1)S(1)} %constant_dynamic-slice_fusion.1), channel_id=1, source_target_pairs={{0,8},{4,12},{8,0},{12,4},{16,24},{20,28},{24,16},{28,20},{1,9},{5... | collective-permute-start | bytes 1142792 | tf_op jit(solution)/shard_map/ppermute | solution.py:795
  534.8 11.7 %collective-permute-start.32 = (bf16[1,24,5376]{2,1,0:T(8,128)(2,1)S(1)}, bf16[1,24,5376]{2,1,0:T(8,128)(2,1)S(1)}, u32[]{:S(2)}, u32[]{:S(2)}) collective-permute-start(bf16[1,24,5376]{2,1,0:T(8,128)(2,1)S(1)} %fusion.51), channel_id=1, source_target_pairs={{0,16},{4,20},{8,24},{12,28},{16,0},{20,4},{24,8},{28,12},{1,17},{... | collective-permute-start | bytes 774152 | tf_op jit(solution)/shard_map/ppermute | solution.py:795
  546.5 8.7 %collective-permute-start.31 = (bf16[24,3968]{1,0:T(8,128)(2,1)S(1)}, bf16[24,3968]{1,0:T(8,128)(2,1)S(1)}, u32[]{:S(2)}, u32[]{:S(2)}) collective-permute-start(bf16[24,3968]{1,0:T(8,128)(2,1)S(1)} %constant_dynamic-slice_fusion), channel_id=1, source_target_pairs={{0,16},{4,20},{8,24},{12,28},{16,0},{20,4},{24,8},{28,12},{1,17},{... | collective-permute-start | bytes 571400 | tf_op jit(solution)/shard_map/ppermute | solution.py:795
  546.6 22.0 %collective-permute-start.35 = (bf16[2,24,5376]{2,1,0:T(8,128)(2,1)S(1)}, bf16[2,24,5376]{2,1,0:T(8,128)(2,1)S(1)}, u32[]{:S(2)}, u32[]{:S(2)}) collective-permute-start(bf16[2,24,5376]{2,1,0:T(8,128)(2,1)S(1)} %pad_maximum_fusion.24), channel_id=1, source_target_pairs={{0,8},{4,12},{8,0},{12,4},{16,24},{20,28},{24,16},{28,20},{1,9},{5... | collective-permute-start | bytes 1548296 | tf_op jit(solution)/shard_map/ppermute | solution.py:795
  555.2 22.5 %collective-permute-start.33 = (bf16[1,24,3968]{2,1,0:T(8,128)(2,1)S(1)}, bf16[1,24,3968]{2,1,0:T(8,128)(2,1)S(1)}, u32[]{:S(2)}, u32[]{:S(2)}) collective-permute-start(bf16[1,24,3968]{2,1,0:T(8,128)(2,1)S(1)} %fusion.56), channel_id=1, source_target_pairs={{0,16},{4,20},{8,24},{12,28},{16,0},{20,4},{24,8},{28,12},{1,17},{... | collective-permute-start | bytes 571400 | tf_op jit(solution)/shard_map/ppermute | solution.py:795
  577.7 9.4 %collective-permute-start.37 = (bf16[2,24,3968]{2,1,0:T(8,128)(2,1)S(1)}, bf16[2,24,3968]{2,1,0:T(8,128)(2,1)S(1)}, u32[]{:S(2)}, u32[]{:S(2)}) collective-permute-start(bf16[2,24,3968]{2,1,0:T(8,128)(2,1)S(1)} %pad_maximum_fusion.26), channel_id=1, source_target_pairs={{0,8},{4,12},{8,0},{12,4},{16,24},{20,28},{24,16},{28,20},{1,9},{5... | collective-permute-start | bytes 1142792 | tf_op jit(solution)/shard_map/ppermute | solution.py:795
  580.3 25.7 %collective-permute-start.39 = (bf16[4,24,5376]{2,1,0:T(8,128)(2,1)S(1)}, bf16[4,24,5376]{2,1,0:T(8,128)(2,1)S(1)}, u32[]{:S(2)}, u32[]{:S(2)}) collective-permute-start(bf16[4,24,5376]{2,1,0:T(8,128)(2,1)S(1)} %pad_maximum_fusion.12), channel_id=1, source_target_pairs={{0,4},{4,0},{8,12},{12,8},{16,20},{20,16},{24,28},{28,24},{1,5},{5... | collective-permute-start | bytes 3096584 | tf_op jit(solution)/shard_map/ppermute | solution.py:795
  587.2 31.6 %collective-permute-start.38 = (bf16[4,24,3968]{2,1,0:T(8,128)(2,1)S(1)}, bf16[4,24,3968]{2,1,0:T(8,128)(2,1)S(1)}, u32[]{:S(2)}, u32[]{:S(2)}) collective-permute-start(bf16[4,24,3968]{2,1,0:T(8,128)(2,1)S(1)} %pad_maximum_fusion.21), channel_id=1, source_target_pairs={{0,4},{4,0},{8,12},{12,8},{16,20},{20,16},{24,28},{28,24},{1,5},{5... | collective-permute-start | bytes 2285576 | tf_op jit(solution)/shard_map/ppermute | solution.py:795
  (134 other events, 494.7 us)
Sparse Core Ops, SparseCore 0:
  9.6 38.1 all-gather.6
  49.9 29.9 all-gather.8
  81.4 17.4 all-gather.10
  100.3 37.4 all-gather.12
  139.2 37.4 all-gather.14
  239.4 29.7 all-gather.16
  271.7 49.1 reduce-scatter.7
  323.7 70.9 reduce-scatter.5
  398.0 57.0 reduce-scatter.3
where the time goes:
time: 641 us; the launch traced here: 632 us
  waiting for transfers between devices  219 us (34%)
  starting transfers between devices  113 us (18%)
  local copies, waits for them, and re-layouts  97.9 us (15%)
  Pallas kernels  73.7 us (11%)
  matrix products  58.9 us (9%)
  other arithmetic  52.1 us (8%)
  between operations  16.4 us (3%)
    ppermute x36, waiting for transfers between devices, flip(): lax.ppermute(value, axis, [(i, i ^ bit) for i in range(lax.axis_size(axis...  162 us
    ppermute x36, starting transfers between devices, flip(): lax.ppermute(value, axis, [(i, i ^ bit) for i in range(lax.axis_size(axis...  71.8 us
    unnamed x295, local copies, waits for them, and re-layouts  60.9 us
    all_gather x6, waiting for transfers between devices, gather(): return lax.all_gather(weight, 'fsdp', axis=axis, tiled=True)  37.2 us
    dot_general x9, matrix products, matmul_nt(): lax.dot_general(left, right, (((1,), (1,)), ((), ())), preferred_element_...  23.5 us
    dot_general x10, matrix products, matmul_tn(): lax.dot_general(left, right, (((0,), (0,)), ((), ())), preferred_element_...  22.4 us
    pallas_call x4, Pallas kernels, settle(): pl.pallas_call(settle_kernel, grid_spec=pltpu.PrefetchScalarGridSpec(num_...  16 us
    pallas_call x1, Pallas kernels, attend_back(): pl.pallas_call(functools.partial(attend_back_kernel, heads, tokens), grid...  15.5 us
  transfers between devices with their start and end apart: 54, of which 23 were waited for; matrix products, arithmetic and copies ran while one was open for 23% of the time, Pallas kernels for 10%

commit v1 on v0

--- a/solution.py
+++ b/solution.py
@@ -55,7 +55,7 @@
 
 def cost(flops, moved, transcendentals=0):
     return pl.CostEstimate(
-        flops=int(flops), bytes_accessed=int(moved), transcendentals=int(transcendentals)
+        flops=1, bytes_accessed=1, transcendentals=0
     )
 
 
@@ -335,45 +335,54 @@
     )(decays, drives)
 
 
-def project_kernel(groups, part, tok_ref, w_ref, seg_ref, out_ref):
-    qkv = matmul(tok_ref[0], w_ref[...]).astype(BF16)
-    rows, width = tok_ref.shape[1], tok_ref.shape[2]
-    lane = lax.broadcasted_iota(jnp.int32, (rows, HEAD_DIM), 1)
-    marks = jnp.where(lane == seg_ref[0], 1.0, 0.0).astype(BF16)
-    for group in range(groups):
-        pieces = [
-            qkv[:, kind * width + group * part : kind * width + (group + 1) * part]
-            for kind in range(3)
-        ]
-        out_ref[group] = jnp.concatenate(pieces + [marks], axis=1)
-
-
-def attend_kernel(heads, tokens, all_ref, query_ref, edge_ref, out_ref, kept_ref, key_scr, value_scr):
+def attend_kernel(
+    heads, tokens, tok_ref, own_ref, core_ref, far_ref, far_core_ref, edge_ref, out_ref, kept_ref,
+    query_ref, key_ref, value_ref, w_ref,
+):
     part = heads * HEAD_DIM
-    rows = query_ref.shape[0]
-
-    @pl.when(pl.program_id(0) == 0)
+    rows = out_ref.shape[0]
+    step = pl.program_id(0)
+
+    @pl.when(step == 0)
     def build():
-        marks = all_ref[:, 3 * part :]
-        blocked = ((marks.astype(F32) - 1.0) * FAR).astype(BF16)
-        ones = jnp.ones_like(marks)
-        for head in range(heads):
-            at = head * HEAD_DIM
-            key_scr[head] = jnp.concatenate(
-                [all_ref[:, part + at : part + at + HEAD_DIM], blocked], axis=1
-            )
-            value_scr[head] = jnp.concatenate(
-                [all_ref[:, 2 * part + at : 2 * part + at + HEAD_DIM], ones], axis=1
-            )
-
-    marks = query_ref[:, 3 * part :]
+        eye = jnp.where(
+            lax.broadcasted_iota(jnp.int32, (HEAD_DIM, HEAD_DIM), 0)
+            == lax.broadcasted_iota(jnp.int32, (HEAD_DIM, HEAD_DIM), 1),
+            1.0,
+            0.0,
+        ).astype(BF16)
+        number = lax.broadcasted_iota(jnp.int32, (HEAD_DIM, tokens), 0).astype(F32)
+        shard = own_ref.shape[0]
+        for other, piece_ref in enumerate((own_ref, core_ref, far_ref, far_core_ref)):
+            at = jnp.bitwise_xor(lax.axis_index("fsdp"), other) * shard
+            w_ref[pl.ds(pl.multiple_of(at, shard), shard)] = piece_ref[...]
+        ones = jnp.ones((tokens, HEAD_DIM), BF16)
+
+        def block(source, carry):
+            qkv = matmul(tok_ref[source, :tokens], w_ref[...])
+            ids = tok_ref[source, tokens:].astype(F32)[0:1, :tokens]
+            marks = matmul_tn(jnp.where(number == ids, 1.0, 0.0).astype(BF16), eye)
+            blocked = ((marks - 1.0) * FAR).astype(BF16)
+            marks = marks.astype(BF16)
+            here = pl.ds(pl.multiple_of(source * tokens, tokens), tokens)
+            for head in range(heads):
+                query, key, value = (
+                    qkv[:, kind * part + head * HEAD_DIM : kind * part + (head + 1) * HEAD_DIM]
+                    for kind in range(3)
+                )
+                query = query.astype(BF16) * jnp.asarray(HEAD_DIM ** (-0.5), BF16)
+                query_ref[head, here] = jnp.concatenate([query, marks], axis=1)
+                key_ref[head, here] = jnp.concatenate([key.astype(BF16), blocked], axis=1)
+                value_ref[head, here] = jnp.concatenate([value.astype(BF16), ones], axis=1)
+            return carry
+
+        lax.fori_loop(0, tok_ref.shape[0], block, 0)
+
+    here = pl.ds(pl.multiple_of(step * rows, rows), rows)
     outs = []
     for head in range(heads):
-        at = head * HEAD_DIM
-        query = query_ref[:, at : at + HEAD_DIM] * jnp.asarray(HEAD_DIM ** (-0.5), BF16)
-        query = jnp.concatenate([query, marks], axis=1)
-        expvals = jnp.exp(matmul_nt(query, key_scr[head]))
-        both = matmul(expvals.astype(BF16), value_scr[head])
+        expvals = jnp.exp(matmul_nt(query_ref[head, here], key_ref[head]))
+        both = matmul(expvals.astype(BF16), value_ref[head])
         total = both[:, HEAD_DIM:]
         context = both[:, :HEAD_DIM] / total
         kept_ref[:, pl.ds(head * 2 * HEAD_DIM, 2 * HEAD_DIM)] = jnp.concatenate(
@@ -386,8 +395,8 @@
 
 
 def attend_back_kernel(
-    heads, tokens, all_ref, kept_ref, grad_ref, edges_ref, out_ref, enter_ref,
-    query_scr, key_scr, value_scr, grad_scr, edge_scr,
+    heads, tokens, tok_ref, w_ref, query_ref, key_ref, value_ref, kept_ref, grad_ref, edges_ref,
+    out_ref, w_grad_ref, enter_ref, grad_scr, edge_scr,
 ):
     part = heads * HEAD_DIM
     rows = out_ref.shape[0]
@@ -395,20 +404,9 @@
 
     @pl.when(step == 0)
     def build():
-        marks = all_ref[:, 3 * part :]
-        blocked = ((marks.astype(F32) - 1.0) * FAR).astype(BF16)
-        lane = lax.broadcasted_iota(jnp.int32, marks.shape, 1)
-        pair = jnp.where(lane < 2, 1.0, 0.0).astype(BF16)
+        lane = lax.broadcasted_iota(jnp.int32, (grad_ref.shape[0], HEAD_DIM), 1)
         for head in range(heads):
             at = head * HEAD_DIM
-            query = all_ref[:, at : at + HEAD_DIM] * jnp.asarray(HEAD_DIM ** (-0.5), BF16)
-            query_scr[head] = jnp.concatenate([query, marks], axis=1)
-            key_scr[head] = jnp.concatenate(
-                [all_ref[:, part + at : part + at + HEAD_DIM], blocked], axis=1
-            )
-            value_scr[head] = jnp.concatenate(
-                [all_ref[:, 2 * part + at : 2 * part + at + HEAD_DIM], pair], axis=1
-            )
             context = kept_ref[:, 2 * at : 2 * at + HEAD_DIM]
             total = kept_ref[:, 2 * at + HEAD_DIM : 2 * at + 2 * HEAD_DIM]
             grad = grad_ref[:, at : at + HEAD_DIM].astype(F32) / total
@@ -427,36 +425,52 @@
                 edge_reader(edges_ref, 0), edge_reader(edge_scr, 0), sequence,
                 edges_ref.shape[0], True,
             )
+        w_grad_ref[...] = jnp.zeros_like(w_grad_ref)
 
     here = pl.ds(pl.multiple_of(step * rows, rows), rows)
     scale = HEAD_DIM ** (-0.5)
     d_query, d_key, d_value = [], [], []
     for head in range(heads):
-        expvals = jnp.exp(matmul_nt(query_scr[head, here], key_scr[head]))
-        inner = matmul_nt(grad_scr[head, here], value_scr[head])
+        expvals = jnp.exp(matmul_nt(query_ref[head, here], key_ref[head]))
+        inner = matmul_nt(grad_scr[head, here], value_ref[head])
         d_scores = (expvals * inner).astype(BF16)
-        d_query.append((matmul(d_scores, key_scr[head])[:, :HEAD_DIM] * scale).astype(BF16))
-        expvals = jnp.exp(matmul_nt(key_scr[head, here], query_scr[head]))
-        inner = matmul_nt(value_scr[head, here], grad_scr[head])
+        d_query.append((matmul(d_scores, key_ref[head])[:, :HEAD_DIM] * scale).astype(BF16))
+        expvals = jnp.exp(matmul_nt(key_ref[head, here], query_ref[head]))
+        inner = matmul_nt(value_ref[head, here], grad_scr[head])
         d_scores = (expvals * inner).astype(BF16)
-        d_key.append(matmul(d_scores, query_scr[head])[:, :HEAD_DIM].astype(BF16))
+        d_key.append(matmul(d_scores, query_ref[head])[:, :HEAD_DIM].astype(BF16))
         d_value.append(
             matmul(expvals.astype(BF16), grad_scr[head])[:, :HEAD_DIM].astype(BF16)
         )
-    pad = jnp.zeros((rows, HEAD_DIM), BF16)
-    out_ref[...] = jnp.concatenate(d_query + d_key + d_value + [pad], axis=1)
-
-
-def unpack_kernel(groups, part, kinds, in_ref, out_ref, *edge_refs):
-    for edge_ref in edge_refs:
-        for group in range(groups):
-            edge_ref[group] = edges_of_block(in_ref[group, :, kinds * part :])
-    pieces = [
-        in_ref[group, :, kind * part : (kind + 1) * part]
-        for kind in range(kinds)
-        for group in range(groups)
-    ]
-    out_ref[...] = jnp.concatenate(pieces, axis=1)
+    d_qkv = jnp.concatenate(d_query + d_key + d_value, axis=1)
+    out_ref[...] = matmul_nt(d_qkv, w_ref[...]).astype(BF16)
+    blocks = rows // tokens
+    tok = jnp.concatenate(
+        [tok_ref[step * blocks + block, :tokens] for block in range(blocks)], axis=0
+    )
+    w_grad_ref[...] += matmul_tn(tok, d_qkv)
+
+
+def unpack_kernel(groups, part, in_ref, out_ref, edge_ref):
+    for group in range(groups):
+        edge_ref[group] = edges_of_block(in_ref[group, :, part:])
+    out_ref[...] = jnp.concatenate([in_ref[group, :, :part] for group in range(groups)], axis=1)
+
+
+def spread_columns_kernel(heads, in_ref, out_ref):
+    groups, part = in_ref.shape[0], heads * HEAD_DIM
+    width = groups * part
+    mine = lax.rem(lax.axis_index("ctx"), groups)
+    for case in range(groups):
+
+        @pl.when(mine == case)
+        def place():
+            for kind in range(3):
+                pieces = [
+                    in_ref[case ^ group, :, kind * part : (kind + 1) * part].astype(F32)
+                    for group in range(groups)
+                ]
+                out_ref[:, pl.ds(kind * width, width)] = jnp.concatenate(pieces, axis=1)
 
 
 def send_grad_kernel(groups, part, grad_ref, w_ref, edge_ref, out_ref):
@@ -469,7 +483,7 @@
 
 
 def heads_here(batch, count):
-    if batch * HEADS % count != 0:
+    if batch * HEADS % count != 0 or not routed():
         return 0
     heads = batch * HEADS // count
     if heads > HEADS or HEADS % heads != 0 or heads % 2 == 0 or batch * KINDS != 8:
@@ -477,117 +491,117 @@
     return heads
 
 
-def project_and_pack(tokens, w_qkv, segment, heads):
-    batch, rows, width = tokens.shape
-    groups, part = HEADS // heads, heads * HEAD_DIM
-    wide = 3 * part + HEAD_DIM
-    return pl.pallas_call(
-        functools.partial(project_kernel, groups, part),
-        grid=(batch,),
-        in_specs=[
-            per_sequence(rows, width),
-            whole_block(width, 3 * width),
-            per_sequence(rows, 1),
-        ],
-        out_specs=pl.BlockSpec((groups, rows, wide), lambda s: (s, 0, 0)),
-        out_shape=jax.ShapeDtypeStruct((batch * groups, rows, wide), BF16),
-        compiler_params=params(),
-        cost_estimate=cost(
-            6 * batch * rows * width * width,
-            tokens.size * 2 + w_qkv.size * 2 + 2 * batch * groups * rows * wide,
-        ),
-        name="project",
-    )(tokens, w_qkv, segment[:, :, None])
-
-
-def attend(everything, edges, heads, tokens):
-    length, wide = everything.shape
+def attend(tokens_all, w_pieces, edges, heads, tokens):
+    count, rows, width = tokens_all.shape
+    length = count * tokens
     block = 256
     part = heads * HEAD_DIM
     out_wide = part + HEAD_DIM
+    wide = jax.ShapeDtypeStruct((heads, length, 2 * HEAD_DIM), BF16)
     return pl.pallas_call(
         functools.partial(attend_kernel, heads, tokens),
         grid=(length // block,),
         in_specs=[
-            pl.BlockSpec((length, wide), lambda i: (0, 0)),
-            pl.BlockSpec((block, wide), lambda i: (i, 0)),
-            pl.BlockSpec(edges.shape, lambda i: (0, 0)),
-        ],
+            pl.BlockSpec((count, rows, width), lambda i: (0, 0, 0)),
+        ]
+        + [pl.BlockSpec(w_pieces[0].shape, lambda i: (0, 0))] * 4
+        + [pl.BlockSpec(edges.shape, lambda i: (0, 0))],
         out_specs=[
             pl.BlockSpec((block, out_wide), lambda i: (i, 0)),
             pl.BlockSpec((block, 2 * part), lambda i: (i, 0)),
-        ],
+        ]
+        + [pl.BlockSpec(wide.shape, lambda i: (0, 0, 0))] * 3
+        + [pl.BlockSpec((width, 3 * part), lambda i: (0, 0))],
         out_shape=[
             jax.ShapeDtypeStruct((length, out_wide), BF16),
             jax.ShapeDtypeStruct((length, 2 * part), F32),
-        ],
-        scratch_shapes=[
-            pltpu.VMEM((heads, length, 2 * HEAD_DIM), BF16),
-            pltpu.VMEM((heads, length, 2 * HEAD_DIM), BF16),
+            wide,
+            wide,
+            wide,
+            jax.ShapeDtypeStruct((width, 3 * part), BF16),
         ],
         compiler_params=params(),
         cost_estimate=cost(
             8 * heads * length * length * HEAD_DIM,
-            length * (wide * 2 + out_wide * 2 + 8 * part),
+            length * (width * 2 + out_wide * 2 + 8 * part),
             heads * length * length,
         ),
         name="attend",
-    )(everything, everything, edges)
-
-
-def attend_back(everything, kept, grads, edges, heads, tokens):
-    length, wide = everything.shape
+    )(tokens_all, *w_pieces, edges)
+
+
+def attend_back(tokens_all, w_heads, saved, kept, grads, edges, heads, tokens):
+    count, rows, width = tokens_all.shape
+    length = count * tokens
     block = 256
     part = heads * HEAD_DIM
     batch, two = edges.shape[1] // KINDS, edges.shape[2]
-    scratch = pltpu.VMEM((heads, length, 2 * HEAD_DIM), BF16)
+    wide = (heads, length, 2 * HEAD_DIM)
     return pl.pallas_call(
         functools.partial(attend_back_kernel, heads, tokens),
         grid=(length // block,),
         in_specs=[
-            pl.BlockSpec((length, wide), lambda i: (0, 0)),
+            pl.BlockSpec((count, rows, width), lambda i: (0, 0, 0)),
+            pl.BlockSpec(w_heads.shape, lambda i: (0, 0)),
+        ]
+        + [pl.BlockSpec(wide, lambda i: (0, 0, 0))] * 3
+        + [
             pl.BlockSpec((length, 2 * part), lambda i: (0, 0)),
             pl.BlockSpec((length, part + HEAD_DIM), lambda i: (0, 0)),
             pl.BlockSpec(edges.shape, lambda i: (0, 0, 0)),
         ],
         out_specs=[
-            pl.BlockSpec((block, wide), lambda i: (i, 0)),
+            pl.BlockSpec((block, width), lambda i: (i, 0)),
+            pl.BlockSpec(w_heads.shape, lambda i: (0, 0)),
             pl.BlockSpec((batch, 1, two), lambda i: (0, 0, 0)),
         ],
         out_shape=[
-            jax.ShapeDtypeStruct((length, wide), BF16),
+            jax.ShapeDtypeStruct((length, width), BF16),
+            jax.ShapeDtypeStruct(w_heads.shape, F32),
             jax.ShapeDtypeStruct((batch, 1, two), F32),
         ],
-        scratch_shapes=[scratch] * 4 + [pltpu.VMEM(edges.shape, F32)],
+        scratch_shapes=[pltpu.VMEM(wide, BF16), pltpu.VMEM(edges.shape, F32)],
         compiler_params=params(),
         cost_estimate=cost(
             28 * heads * length * length * HEAD_DIM,
-            length * (wide * 4 + 8 * part + 2 * part),
+            length * (width * 4 + 8 * part + 2 * part),
             2 * heads * length * length,
         ),
         name="attend_back",
-    )(everything, kept, grads, edges)
-
-
-def unpack(received, heads, kinds, batch, edges):
+    )(tokens_all, w_heads, *saved, kept, grads, edges)
+
+
+def unpack(received, heads, batch):
     count, rows, wide = received.shape
     groups, part = HEADS // heads, heads * HEAD_DIM
-    width = kinds * groups * part
-    out_specs = [pl.BlockSpec((rows, width), lambda s: (s, 0))]
-    out_shape = [jax.ShapeDtypeStruct((batch * rows, width), BF16)]
-    if edges:
-        out_specs.append(pl.BlockSpec((groups, KINDS * batch, 2 * GRU_H), lambda s: (s, 0, 0)))
-        out_shape.append(jax.ShapeDtypeStruct((count, KINDS * batch, 2 * GRU_H), F32))
-    return pl.pallas_call(
-        functools.partial(unpack_kernel, groups, part, kinds),
+    width = groups * part
+    return pl.pallas_call(
+        functools.partial(unpack_kernel, groups, part),
         grid=(batch,),
         in_specs=[pl.BlockSpec((groups, rows, wide), lambda s: (s, 0, 0))],
-        out_specs=out_specs,
-        out_shape=out_shape,
+        out_specs=[
+            pl.BlockSpec((rows, width), lambda s: (s, 0)),
+            pl.BlockSpec((groups, KINDS * batch, 2 * GRU_H), lambda s: (s, 0, 0)),
+        ],
+        out_shape=[
+            jax.ShapeDtypeStruct((batch * rows, width), BF16),
+            jax.ShapeDtypeStruct((count, KINDS * batch, 2 * GRU_H), F32),
+        ],
         compiler_params=params(),
         cost_estimate=cost(0, 2 * received.size + 2 * batch * rows * width),
         name="unpack",
     )(received)
+
+
+def spread_columns(pieces, heads):
+    groups, rows, wide = pieces.shape
+    return pl.pallas_call(
+        functools.partial(spread_columns_kernel, heads),
+        out_shape=jax.ShapeDtypeStruct((rows, groups * wide), F32),
+        compiler_params=params(),
+        cost_estimate=cost(1, 1),
+        name="spread_columns",
+    )(pieces)
 
 
 def send_grad(d_attn, w_out, edges, heads, batch):
@@ -650,6 +664,145 @@
     )(hidden, w_up, bias)
 
 
+def gradients_kernel(
+    blocks, hidden1_ref, context_ref, hidden2_ref, char_ref, pre_ref, attn_ref, joined_ref, out_ref
+):
+    step = pl.program_id(0)
+    width = hidden2_ref.shape[1]
+
+    def put(at, left_ref, right):
+        @pl.when((step < blocks) if at is None else (step == blocks + at))
+        def store():
+            out_ref[...] = matmul_tn(left_ref[...], right()).astype(BF16)
+
+    put(None, hidden1_ref, lambda: pre_ref[...])
+    put(0, context_ref, lambda: attn_ref[...])
+    put(1, hidden2_ref, lambda: joined_ref[:, :width])
+    put(2, char_ref, lambda: joined_ref[:, width:])
+
+
+def gradients(hidden1, context, hidden2, chars, d_pre, d_attn, d_joined):
+    rows, width = hidden1.shape
+    blocks = d_pre.shape[1] // width
+    whole = whole_block(rows, width)
+    return pl.pallas_call(
+        functools.partial(gradients_kernel, blocks),
+        grid=(blocks + 3,),
+        in_specs=[whole] * 4
+        + [
+            pl.BlockSpec((rows, width), lambda i: (0, jnp.minimum(i, blocks - 1))),
+            whole,
+            whole_block(rows, 2 * width),
+        ],
+        out_specs=pl.BlockSpec((width, width), lambda i: (0, i)),
+        out_shape=jax.ShapeDtypeStruct((width, (blocks + 3) * width), BF16),
+        compiler_params=params(),
+        cost_estimate=cost(1, 1),
+        name="gradients",
+    )(hidden1, context, hidden2, chars, d_pre, d_attn, d_joined)
+
+
+def down_grad_kernel(own_ref, core_ref, far_ref, far_core_ref, grad_ref, out_ref):
+    total = jnp.zeros(out_ref.shape, F32)
+    for other, inner_ref in enumerate((own_ref, core_ref, far_ref, far_core_ref)):
+        source = jnp.bitwise_xor(lax.axis_index("fsdp"), other)
+        total = total + matmul_tn(inner_ref[...], grad_ref[source])
+    out_ref[...] = total.astype(BF16)
+
+
+def down_gradient(inner, grads):
+    return pl.pallas_call(
+        down_grad_kernel,
+        out_shape=jax.ShapeDtypeStruct((inner[0].shape[1], grads.shape[2]), BF16),
+        compiler_params=params(),
+        cost_estimate=cost(1, 1),
+        name="down_gradient",
+    )(*inner, grads)
+
+
+def conv_grad_kernel(
+    own_ref, core_ref, far_ref, far_core_ref, grad_ref, keep_ref, send_ref, side_scr
+):
+    tap = pl.program_id(0)
+    refs = (own_ref, core_ref, far_ref, far_core_ref)
+    batch = grad_ref.shape[0] // len(refs)
+    rows = side_scr.shape[0] // batch
+    shape = (rows, grad_ref.shape[2])
+    row = lax.broadcasted_iota(jnp.int32, shape, 0)
+    total = jnp.zeros((own_ref.shape[1], grad_ref.shape[2]), F32)
+    for other, joined_ref in enumerate(refs):
+        first = jnp.bitwise_xor(lax.axis_index("fsdp"), other) * batch
+        for block in range(batch):
+            here = pl.ds(block * rows, rows)
+            grad = grad_ref[first + block].astype(F32)
+            mid = grad[:rows]
+
+            @pl.when(tap == 0)
+            def earlier():
+                moved = pltpu.roll(mid, rows - 1, 0)
+                last = jnp.broadcast_to(grad[rows + 1 : rows + 2], shape)
+                side_scr[here] = jnp.where(row == rows - 1, last, moved).astype(BF16)
+
+            @pl.when(tap == 1)
+            def same():
+                side_scr[here] = mid.astype(BF16)
+
+            @pl.when(tap == 2)
+            def later():
+                moved = pltpu.roll(mid, 1, 0)
+                before = jnp.broadcast_to(grad[rows : rows + 1], shape)
+                side_scr[here] = jnp.where(row == 0, before, moved).astype(BF16)
+
+        total = total + matmul_tn(joined_ref[...], side_scr[...])
+    half = keep_ref.shape[1]
+    halves = (total[:half].astype(BF16), total[half:].astype(BF16))
+    for mine in (0, 1):
+
+        @pl.when(lax.rem(lax.axis_index("ctx"), 2) == mine)
+        def store():
+            keep_ref[0] = halves[mine]
+            send_ref[0] = halves[1 - mine]
+
+
+def conv_gradient(joined, grads, rows, part):
+    count, tall, wide = grads.shape
+    wide = wide // 2
+    own = joined[0].shape
+    out = jax.ShapeDtypeStruct((3, own[1] // 2, wide), BF16)
+    return pl.pallas_call(
+        conv_grad_kernel,
+        grid=(3,),
+        in_specs=[pl.BlockSpec(own, lambda k: (0, 0))] * 4
+        + [pl.BlockSpec((count, tall, wide), lambda k: (0, 0, part))],
+        out_specs=[pl.BlockSpec((1,) + out.shape[1:], lambda k: (k, 0, 0))] * 2,
+        out_shape=[out, out],
+        scratch_shapes=[pltpu.VMEM((own[0], wide), BF16)],
+        compiler_params=params(),
+        cost_estimate=cost(1, 1),
+        name="conv_gradient",
+    )(*joined, grads)
+
+
+def last_grads_kernel(chars_ref, gates_ref, small_ref, heads_ref, out_ref):
+    wide = gates_ref.shape[1]
+    narrow = small_ref.shape[1]
+    out_ref[:, :wide] = matmul_tn(chars_ref[...], gates_ref[...]).astype(BF16)
+    out_ref[:, wide : wide + narrow] = small_ref[...].astype(BF16)
+    out_ref[:, wide + narrow :] = heads_ref[...].astype(BF16)
+
+
+def last_gradients(chars, d_gates, small, heads_grad):
+    width = chars.shape[1]
+    wide = d_gates.shape[1] + small.shape[1] + heads_grad.shape[1]
+    return pl.pallas_call(
+        last_grads_kernel,
+        out_shape=jax.ShapeDtypeStruct((width, wide), BF16),
+        compiler_params=params(),
+        cost_estimate=cost(1, 1),
+        name="last_gradients",
+    )(chars, d_gates, small, heads_grad)
+
+
 def block_size(rows):
     size = min(rows, BLOCK_LIMIT)
     while rows % size != 0:
@@ -788,23 +941,44 @@
 
 
 STEPS = (1, 2, 4)
-ORDER = "DCDCDTCDTCDTQCDQTQTQCTDQQTQ"
+OTHER_STEPS = (1, 4, 2)
+ORDER = "DABXDABTABXDTABDXTGKDTGKDTGKABTGKDGGTG"
 
 
 def flip(value, axis, bit):
     return lax.ppermute(value, axis, [(i, i ^ bit) for i in range(lax.axis_size(axis))])
 
 
-def slot():
+def slot(steps=STEPS):
     me = lax.axis_index("ctx")
-    return (me % 2) * 4 + ((me // 2) % 2) * 2 + me // 4
+    first, second, third = ((me // bit) % 2 for bit in steps)
+    return first * 4 + second * 2 + third
+
+
+def own_columns(value):
+    count, mine = lax.axis_size("fsdp"), lax.axis_index("fsdp")
+    wide = value.shape[1] // count
+    pieces = []
+    for other in range(count):
+        piece = lax.dynamic_slice_in_dim(value, jnp.bitwise_xor(mine, other) * wide, wide, 1)
+        pieces.append(flip(piece, "fsdp", other) if other else piece)
+    return pieces
 
 
 class CtxSum:
-    def __init__(self, value):
+    def __init__(self, value, steps=STEPS):
         self.value = value
         self.axis = value.ndim - 2
         self.stage = 0
+        self.steps = steps
+
+    @classmethod
+    def begun(cls, keep, send, steps=STEPS):
+        chain = cls(keep, steps)
+        chain.keep = keep
+        chain.send(send, steps[0])
+        chain.stage = 1
+        return chain
 
     def halve(self, value, bit):
         mine = (lax.axis_index("ctx") // bit) % 2
@@ -821,27 +995,78 @@
         stage = self.stage
         self.stage = stage + 1
         if stage == 0:
-            self.halve(after(self.value, *others), STEPS[0])
+            self.halve(after(self.value, *others), self.steps[0])
         elif stage <= 3:
             got = after(self.got, *others).astype(F32)
             piece = (self.keep.astype(F32) + got).astype(BF16)
             if stage < 3:
-                self.halve(piece, STEPS[stage])
+                self.halve(piece, self.steps[stage])
             else:
-                self.send(piece[None], STEPS[2])
+                self.send(piece[None], self.steps[2])
         else:
             piece = jnp.concatenate([self.sent, after(self.got, *others)], axis=0)
             if stage < 6:
-                self.send(piece, STEPS[5 - stage])
+                self.send(piece, self.steps[5 - stage])
             else:
                 self.result = self.sent = piece
         return self.sent
 
 
-def run_in_order(events, waits):
-    last = ()
-    for event, chain in enumerate(events):
-        last = (chain.advance(*last, *waits.get(event, ())),)
+class HeadSum(CtxSum):
+    def advance(self, *others):
+        stage = self.stage
+        self.stage = stage + 1
+        if stage == 0:
+            self.send(after(self.value, *others), 4)
+        elif stage == 1:
+            piece = self.sent.astype(F32) + after(self.got, *others).astype(F32)
+            self.send(piece.astype(BF16)[None], 1)
+        else:
+            piece = jnp.concatenate([self.sent, after(self.got, *others)], axis=0)
+            if stage == 2:
+                self.send(piece, 2)
+            else:
+                self.result = self.sent = piece
+        return self.sent
+
+
+class TokenSum(CtxSum):
+    def advance(self, *others):
+        me = lax.axis_index("ctx")
+        stage = self.stage
+        self.stage = stage + 1
+        if stage == 0:
+            piece = after(self.value, *others)
+        else:
+            got = after(self.got, *others).astype(F32)
+            if stage == 3:
+                keep = self.keep.astype(F32)
+                ordered = (jnp.concatenate([keep, got]), jnp.concatenate([got, keep]))
+                self.result = self.sent = jnp.where(me // 4 == 0, *ordered)
+                return self.sent
+            piece = (self.keep.astype(F32) + got).astype(BF16)
+            piece = jnp.squeeze(piece, axis=3 - stage)
+        bit = STEPS[stage]
+        mine = (me // bit) % 2
+        axis = 2 - stage
+        self.keep = lax.dynamic_slice_in_dim(piece, mine, 1, axis)
+        self.send(lax.dynamic_slice_in_dim(piece, 1 - mine, 1, axis), bit)
+        return self.sent
+
+
+def run_in_order(chains, finish, ready):
+    last, done = (), {}
+    for event, name in enumerate(ORDER):
+        chain = chains[name]
+        others = last
+        if event == ORDER.index("T"):
+            others = others + (ready,)
+        if event == len(ORDER) - 3:
+            others = others + tuple(done["D"]) + (done["K"],)
+        last = (chain.advance(*others),)
+        if hasattr(chain, "result"):
+            done[name] = finish[name](chain.result)
+    return done
 
 
 def settle_kernel(order_ref, in_ref, *out_refs):
@@ -850,6 +1075,35 @@
         wide = out_ref.shape[-1]
         out_ref[...] = in_ref[0, ..., at : at + wide].astype(F32)
         at = at + wide
+
+
+def settle_half_kernel(order_ref, in_ref, *refs):
+    refs[-1][...] = in_ref[0].astype(F32)
+
+
+def settle_half(pieces, steps, part, whole=None):
+    lead = pieces.shape[1:-2]
+    rows, width = pieces.shape[-2:]
+    none = (0,) * len(lead)
+    order = jnp.bitwise_xor(slot(steps), jnp.arange(8, dtype=jnp.int32))
+    given = [] if whole is None else [whole]
+    return pl.pallas_call(
+        settle_half_kernel,
+        grid_spec=pltpu.PrefetchScalarGridSpec(
+            num_scalar_prefetch=1,
+            grid=(8,),
+            in_specs=[
+                pl.BlockSpec((1,) + lead + (rows, width), lambda r, o: (r,) + none + (0, 0))
+            ]
+            + [pl.BlockSpec(memory_space=pl.ANY)] * len(given),
+            out_specs=pl.BlockSpec(lead + (rows, width), lambda r, o: none + (o[r], part)),
+        ),
+        out_shape=jax.ShapeDtypeStruct(lead + (8 * rows, 2 * width), F32),
+        input_output_aliases={2: 0} if given else {},
+        compiler_params=params(),
+        cost_estimate=cost(1, 1),
+        name="settle_half",
+    )(order, pieces, *given)
 
 
 def settle(pieces, widths):
@@ -877,50 +1131,58 @@
     )(order, pieces)
 
 
+def move(sources, stages, targets, arrived, left):
+    ins = [
+        pltpu.make_async_copy(source, stage, arrived.at[i])
+        for i, (source, stage) in enumerate(zip(sources, stages))
+    ]
+    for copy in ins:
+        copy.start()
+    outs = []
+    for i, (copy, stage, target) in enumerate(zip(ins, stages, targets)):
+        copy.wait()
+        outs.append(pltpu.make_async_copy(stage, target, left.at[i]))
+        outs[-1].start()
+    for copy in outs:
+        copy.wait()
+
+
 def place_own_kernel(spans, own_ref, core_ref, *rest):
-    outs, sems = rest[:-1], rest[-1]
+    outs, (own_scr, core_scr, arrived, left) = rest[:-4], rest[-4:]
     mine = lax.axis_index("fsdp")
-    copies, at = [], 0
+    sources, stages, targets, at = [], [], [], 0
     for span, out_ref in zip(spans, outs):
-        for source, shard in ((own_ref, mine), (core_ref, jnp.bitwise_xor(mine, 1))):
-            copies.append(
-                pltpu.make_async_copy(
-                    source.at[pl.ds(at, span)], out_ref.at[shard], sems.at[len(copies)]
-                )
-            )
+        there = pl.ds(at, span)
+        for ref, scr, shard in (
+            (own_ref, own_scr, mine),
+            (core_ref, core_scr, jnp.bitwise_xor(mine, 1)),
+        ):
+            sources.append(ref.at[there])
+            stages.append(scr.at[there])
+            targets.append(out_ref.at[shard])
         at = at + span
-    for copy in copies:
-        copy.start()
-    for copy in copies:
-        copy.wait()
+    move(sources, stages, targets, arrived, left)
 
 
 def place_kernel(spans, order, piece_ref, core_ref, *rest):
-    outs, sems = rest[len(spans) : -1], rest[-1]
+    outs, (piece_scr, core_scr, arrived, left) = rest[len(spans) : -4], rest[-4:]
     place = slot()
     mine = lax.axis_index("fsdp")
-    copies = []
-    for source, shard in (
-        (piece_ref, jnp.bitwise_xor(mine, 2)),
-        (core_ref, jnp.bitwise_xor(mine, 3)),
+    sources, stages, targets = [], [], []
+    for ref, scr, shard in (
+        (piece_ref, piece_scr, jnp.bitwise_xor(mine, 2)),
+        (core_ref, core_scr, jnp.bitwise_xor(mine, 3)),
     ):
         for position, other in enumerate(order):
             at = 0
             for span, out_ref in zip(spans, outs):
                 part = span // 8
                 there = pl.multiple_of(jnp.bitwise_xor(place, other) * part, part)
-                copies.append(
-                    pltpu.make_async_copy(
-                        source.at[position, pl.ds(at, part)],
-                        out_ref.at[shard, pl.ds(there, part)],
-                        sems.at[len(copies)],
-                    )
-                )
+                sources.append(ref.at[position, pl.ds(at, part)])
+                stages.append(scr.at[position, pl.ds(at, part)])
+                targets.append(out_ref.at[shard, pl.ds(there, part)])
                 at = at + part
-    for copy in copies:
-        copy.start()
-    for copy in copies:
-        copy.wait()
+    move(sources, stages, targets, arrived, left)
 
 
 def after(value, *others):
@@ -937,41 +1199,48 @@
             lax.dynamic_slice_in_dim(shard, place * (span // 8), span // 8, 0)
             for shard, span in zip(shards, self.spans)
         ]
-        self.piece = flip(jnp.concatenate(piece, axis=0), "fsdp", 2)[None]
+        self.base = None
+        self.got = flip(jnp.concatenate(piece, axis=0), "fsdp", 2)[None]
         self.core = flip(self.own, "fsdp", 1)
         self.order = [0]
 
+    def take(self, others):
+        got = after(self.got, *others) if others else self.got
+        return got if self.base is None else jnp.concatenate([self.base, got], axis=0)
+
     def double(self, bit, *others):
-        piece = after(self.piece, *others) if others else self.piece
-        self.piece = jnp.concatenate([piece, flip(piece, "ctx", bit)], axis=0)
+        self.base = self.take(others)
+        self.got = flip(self.base, "ctx", bit)
         self.order = self.order + [other ^ (4 // bit) for other in self.order]
 
     def cores(self, *others):
-        piece = after(self.piece, *others) if others else self.piece
-        self.core_piece = flip(piece, "fsdp", 1)
-
-    def place_own(self):
+        self.piece = self.take(others)
+        self.core_piece = flip(self.piece, "fsdp", 1)
+
+    def place_own(self, *others):
         spans, width = self.spans, self.own.shape[1]
         self.whole = pl.pallas_call(
             functools.partial(place_own_kernel, spans),
-            in_specs=[pl.BlockSpec(memory_space=pltpu.VMEM)] * 2,
+            in_specs=[pl.BlockSpec(memory_space=pl.ANY)] * 2,
             out_specs=[pl.BlockSpec(memory_space=pl.ANY)] * len(spans),
             out_shape=[jax.ShapeDtypeStruct((4, span, width), BF16) for span in spans],
-            scratch_shapes=[pltpu.SemaphoreType.DMA((2 * len(spans),))],
+            scratch_shapes=[pltpu.VMEM(self.own.shape, BF16)] * 2
+            + [pltpu.SemaphoreType.DMA((2 * len(spans),))] * 2,
             compiler_params=params(),
             cost_estimate=cost(0, 8 * sum(spans) * width),
             name="place_own",
-        )(self.own, self.core)
+        )(after(self.own, *others), self.core)
 
     def finish(self):
         spans, width = self.spans, self.own.shape[1]
         anywhere = [pl.BlockSpec(memory_space=pl.ANY)] * len(spans)
         return pl.pallas_call(
             functools.partial(place_kernel, spans, self.order),
-            in_specs=[pl.BlockSpec(memory_space=pltpu.VMEM)] * 2 + anywhere,
+            in_specs=[pl.BlockSpec(memory_space=pl.ANY)] * 2 + anywhere,
             out_specs=anywhere,
             out_shape=[jax.ShapeDtypeStruct((4, span, width), BF16) for span in spans],
-            scratch_shapes=[pltpu.SemaphoreType.DMA((16 * len(spans),))],
+            scratch_shapes=[pltpu.VMEM(self.piece.shape, BF16)] * 2
+            + [pltpu.SemaphoreType.DMA((16 * len(spans),))] * 2,
             input_output_aliases={2 + i: i for i in range(len(spans))},
             compiler_params=params(),
             cost_estimate=cost(0, 8 * sum(spans) * width),
@@ -1014,7 +1283,19 @@
     small_count = columns.shape[1]
     wide_gru = w_gru.shape[1]
     columns = jnp.pad(columns, ((0, 0), (0, 128 - small_count)))
-    w_qkv = gather(w_qkv)
+    width_qkv = w_qkv.shape[1]
+    if heads:
+        group, part = me % (HEADS // heads), heads * HEAD_DIM
+        w_heads = jnp.concatenate(
+            [
+                lax.dynamic_slice_in_dim(w_qkv, kind * width + group * part, part, 1)
+                for kind in range(3)
+            ],
+            axis=1,
+        )
+        w_pieces = [w_heads] + [flip(w_heads, "fsdp", other) for other in (1, 2, 3)]
+    else:
+        w_qkv = gather(w_qkv)
     w_gru = gather(jnp.concatenate([w_gru, columns], axis=1))
     w_out = gather(w_out)
     w_up = gather(w_up)
@@ -1041,21 +1322,27 @@
     )
     flat_tokens = tokens.reshape(total_rows, width)
     chars_pad = jnp.pad(chars, ((0, 0), (0, padded_rows - char_rows), (0, 0)))
-    chars_in = chars_pad
+    if routed():
+        first_taps.double(4)
+        last_tap.double(1)
+    gate, cand, decay, cum, state, edges = gru_forward(
+        chars_pad, w_gru, b_gate, start[:, None], first[:, None], char_end[:, None],
+        last[:, None], char_rows,
+    )
+
     if heads:
-        sent = project_and_pack(tokens, w_qkv, segment, heads)
-        chars_in = after(chars_pad, sent)
-    gate, cand, decay, cum, state, edges = gru_forward(
-        chars_in, w_gru, b_gate, start[:, None], first[:, None], char_end[:, None],
-        last[:, None], char_rows,
-    )
-
-    if heads:
-        everything = lax.all_to_all(sent, "ctx", 0, 0, tiled=True)
-        everything = everything.reshape(count * rows, -1)
-        packed_context, kept = attend(everything, edges, heads, rows)
+        ids = segment.astype(BF16)[:, None, :]
+        ids = jnp.pad(ids, ((0, 0), (0, 7), (0, width - rows)))
+        sent = jnp.repeat(jnp.concatenate([tokens, ids], axis=1), HEADS // heads, axis=0)
+        tokens_all = lax.all_to_all(sent, "ctx", 0, 0, tiled=True)
+        packed_context, kept, *saved, w_heads = attend(tokens_all, w_pieces, edges, heads, rows)
+        first_taps.double(2, state)
+        last_tap.double(4, state)
+        first_taps.place_own(packed_context)
+        last_tap.place_own(packed_context)
         received = lax.all_to_all(packed_context.reshape(count, rows, -1), "ctx", 0, 0, tiled=True)
-        context_b, edges_all = unpack(received, heads, 1, batch, True)
+        received = after(received, *first_taps.whole, *last_tap.whole)
+        context_b, edges_all = unpack(received, heads, batch)
     else:
         qkv = matmul(flat_tokens, w_qkv).astype(BF16).reshape(batch, rows, -1)
         results = [gathered_attention(qkv[i], segment[i]) for i in range(batch)]
@@ -1065,25 +1352,19 @@
     attn = matmul(context_b, w_out)
     hidden1, kept1 = layer_norm(flat_tokens.astype(F32) + attn, norm1_gain, norm1_bias)
     hidden1_b = hidden1.astype(BF16)
+    inner_b, slope = feed_forward(hidden1_b, w_up, b_up)
+    ffn = matmul(inner_b, w_down)
+    hidden2, kept2 = layer_norm(hidden1 + ffn, norm2_gain, norm2_bias)
+    hidden2_b = hidden2.astype(BF16)
     if routed():
-        first_taps.double(4, sent)
-        last_tap.double(1, sent)
-        first_taps.place_own()
-        last_tap.place_own()
-        first_taps.double(2, state)
-        last_tap.double(4, state)
-        first_taps.double(1, packed_context)
-        last_tap.double(2, packed_context)
-        first_taps.cores(hidden1_b)
-        last_tap.cores(hidden1_b)
+        first_taps.double(1, context_b)
+        last_tap.double(2, context_b)
+        first_taps.cores(inner_b)
+        last_tap.cores(inner_b)
         w_conv = [
             weight.reshape(-1, 2 * width) for weight in first_taps.finish() + last_tap.finish()
         ]
         w_ftok, w_fchr = w_conv[3][:, :width], w_conv[3][:, width:]
-    inner_b, slope = feed_forward(hidden1_b, w_up, b_up)
-    ffn = matmul(inner_b, w_down)
-    hidden2, kept2 = layer_norm(hidden1 + ffn, norm2_gain, norm2_bias)
-    hidden2_b = hidden2.astype(BF16)
 
     char_tok, enter = gather_states(
         state, cum, edges_all, char_end[:, :, None], start[:, :, None]
@@ -1094,6 +1375,10 @@
     ).astype(BF16)
 
     two = 2 * width
+    if routed():
+        inner_own = own_columns(inner_b)
+        joined = after(joined, *inner_own[1:])
+        joined_own = own_columns(joined)
     blocks = joined.reshape(batch, rows, two)
     later, earlier = shifted(blocks, *neighbours(blocks))
     taps = (later.reshape(total_rows, two), joined, earlier.reshape(total_rows, two))
@@ -1109,6 +1394,8 @@
     )
     d_conv = jnp.concatenate([d_in3, d_in4], axis=1).astype(BF16)
     d_before, d_after = neighbours(d_conv.reshape(batch, rows, two))
+    if routed():
+        d_conv = after(d_conv, *joined_own[1:])
     d_later, d_earlier = shifted(d_conv.reshape(batch, rows, two), d_before, d_after)
     d_joined = (
         matmul_nt(d_conv, w_conv[1])
@@ -1116,28 +1403,15 @@
         + matmul_nt(d_later.reshape(total_rows, two), w_conv[2])
     ).astype(BF16)
     if routed():
-        own_in = two // shards
-        joined_own = after(joined, d_joined)
-        joined_own = jnp.swapaxes(joined_own.reshape(total_rows, shards, own_in), 0, 1)
-        joined_own = lax.all_to_all(joined_own, "fsdp", 0, 0, tiled=True).reshape(-1, own_in)
         d_all = gather(
             jnp.concatenate([d_conv.reshape(batch, rows, two), d_before, d_after], axis=1)
         )
-        d_mid = d_all[:, :rows]
-        d_sides = (
-            jnp.concatenate([d_mid[:, 1:], d_all[:, rows + 1 :]], axis=1),
-            d_mid,
-            jnp.concatenate([d_all[:, rows : rows + 1], d_mid[:, :-1]], axis=1),
-        )
     else:
-        joined_own = joined
         conv_sum = plain_sum(jnp.stack([matmul_tn(tap, d_conv).astype(BF16) for tap in taps]), 1)
 
     d_tok_part, d_chr_part = d_joined[:, :width], d_joined[:, width:]
     d_hidden2 = d_in3 + matmul_nt(d_tok_part, w_ftok)
     d_char_tok = d_in4 + matmul_nt(d_chr_part, w_fchr)
-    ftok_grad = matmul_tn(hidden2_b, d_tok_part).astype(BF16)
-    fchr_grad = matmul_tn(char_tok_b, d_chr_part).astype(BF16)
 
     end_line, start_line = char_end[:, None], start[:, None]
     spread, back_cum, carried, back_edges = gru_back(
@@ -1146,9 +1420,11 @@
 
     d_in2, gain2_grad, bias2_grad = layer_norm_back(d_hidden2, norm2_gain, kept2)
     d_ffn = d_in2.astype(BF16)
-    down_grad = matmul_tn(inner_b, d_ffn).astype(BF16)
     reduced = over_fsdp if routed() else plain_sum
-    second_sum = reduced(down_grad)
+    if routed():
+        d_ffn_all = gather(d_ffn[None])
+    else:
+        second_sum = plain_sum(matmul_tn(inner_b, d_ffn).astype(BF16))
     d_pre = matmul_nt(d_ffn, w_down) * slope.astype(F32)
     bup_grad = jnp.sum(d_pre, axis=0)
     d_pre_low = d_pre.astype(BF16)
@@ -1157,27 +1433,25 @@
     d_attn = d_in1.astype(BF16)
     if heads:
         sent = send_grad(d_attn, w_out, back_edges, heads, batch)
-        hidden1_b, joined_own = after((hidden1_b, joined_own), sent)
-    up_grad = matmul_tn(hidden1_b, d_pre_low).astype(BF16)
-    wout_grad = matmul_tn(context_b, d_attn).astype(BF16)
-    third_sum = reduced(jnp.concatenate([up_grad, wout_grad, ftok_grad, fchr_grad], axis=1))
-    if routed():
-        conv_chain = CtxSum(
-            jnp.stack(
-                [matmul_tn(joined_own, side.reshape(-1, two)).astype(BF16) for side in d_sides]
-            )
-        )
-        conv_sent = conv_chain.advance()
+        conv_pieces = [after(joined_own[0], sent)] + joined_own[1:]
+        first_chain = CtxSum.begun(*conv_gradient(conv_pieces, d_all, rows, 0))
+        other_chain = CtxSum.begun(*conv_gradient(conv_pieces, d_all, rows, 1), OTHER_STEPS)
+        hidden1_b = after(hidden1_b, first_chain.sent, other_chain.sent)
+    third_sum = reduced(
+        gradients(hidden1_b, context_b, hidden2_b, char_tok_b, d_pre_low, d_attn, d_joined)
+    )
 
     if heads:
         received = lax.all_to_all(sent, "ctx", 0, 0, tiled=True)
-        if routed():
-            received = after(received, conv_sent)
-        packed_grad, back_enter = attend_back(
-            everything, kept, received.reshape(count * rows, -1), edges_all, heads, rows
-        )
-        returned = lax.all_to_all(packed_grad.reshape(count, rows, -1), "ctx", 0, 0, tiled=True)
-        (d_qkv,) = unpack(returned, heads, 3, batch, False)
+        d_tok_part, heads_grad, back_enter = attend_back(
+            tokens_all, w_heads, saved, kept, received.reshape(count * rows, -1), edges_all,
+            heads, rows,
+        )
+        token_chain = TokenSum(d_tok_part.reshape(2, 2, 2, rows, width))
+        last = other_chain.advance(first_chain.advance(heads_grad))
+        last = token_chain.advance(last)
+        gate = after(gate, last)
+        second_chain = CtxSum(down_gradient(inner_own, d_ffn_all))
     else:
         back_enter = back_entering(edges_all, all_edges(back_edges))
         d_context = matmul_nt(d_attn, w_out).reshape(batch, rows, width)
@@ -1193,12 +1467,12 @@
         gate, cand, decay, cum, state, enter, spread, back_cum, carried, back_enter, char_rows
     )
     d_gate_in = d_gate_in.reshape(batch * padded_rows, -1)
-    gru_weight_grad = matmul_tn(chars_pad.reshape(batch * padded_rows, width), d_gate_in)
     d_chars = matmul_nt(d_gate_in, w_gru[:, :wide_gru]).astype(BF16)
     d_chars = d_chars.reshape(batch, padded_rows, width)[:, :char_rows]
 
-    qkv_grad = matmul_tn(flat_tokens, d_qkv).astype(BF16)
-    d_tokens = (d_in1 + matmul_nt(d_qkv, w_qkv)).astype(BF16)
+    if not heads:
+        heads_grad = matmul_tn(flat_tokens, d_qkv)
+        d_tokens = matmul_nt(d_qkv, w_qkv)
 
     small = jnp.stack(
         [
@@ -1211,37 +1485,50 @@
     up_small = jnp.swapaxes(up_small, 1, 2).reshape(width, -1)
     small = jnp.concatenate([small, up_small], axis=1)
     small = jnp.pad(small, ((0, 0), (0, 128 - small_count)))
-    fourth = jnp.concatenate([qkv_grad, gru_weight_grad.astype(BF16), small.astype(BF16)], axis=1)
+    fourth = last_gradients(
+        chars_pad.reshape(batch * padded_rows, width), d_gate_in, small, heads_grad
+    )
     fourth_sum = reduced(fourth)
 
-    widths = ((width,), (w_up.shape[1],) + (width,) * 3, (w_qkv.shape[1], wide_gru, 128))
+    widths = ((width,), (w_up.shape[1],) + (width,) * 3, (wide_gru, 128, width_qkv))
     if routed():
-        second_chain, third_chain, fourth_chain = (
-            CtxSum(value) for value in (second_sum, third_sum, fourth_sum)
-        )
-        chains = dict(C=conv_chain, D=second_chain, T=third_chain, Q=fourth_chain)
-        events = [chains[name] for name in ORDER]
-        run_in_order(events, {ORDER.index("T"): (fourth,)})
-        second_sum, third_sum, fourth_sum = (
-            chain.result for chain in (second_chain, third_chain, fourth_chain)
-        )
-        (conv_sum,) = settle(conv_chain.result, (two,))
-        (down_sum,), third, fourth = (
-            settle(value, split)
-            for value, split in zip((second_sum, third_sum, fourth_sum), widths)
-        )
+        own_wide = wide_gru + 128
+        chains = dict(
+            A=first_chain,
+            B=other_chain,
+            D=second_chain,
+            X=token_chain,
+            T=CtxSum(third_sum),
+            G=CtxSum(fourth_sum[:, :own_wide]),
+            K=HeadSum(fourth_sum[:, own_wide:]),
+        )
+        finish = dict(
+            A=lambda value: settle_half(value, STEPS, 0),
+            B=lambda value: value,
+            D=lambda value: settle(value, widths[0]),
+            T=lambda value: settle(value, widths[1]),
+            G=lambda value: settle(value, widths[2][:2]),
+            K=lambda value: spread_columns(value, heads),
+            X=lambda value: value.reshape(total_rows, width),
+        )
+        done = run_in_order(chains, finish, fourth)
+        (down_sum,), third = done["D"], done["T"]
+        conv_sum = settle_half(done["B"], OTHER_STEPS, 1, done["A"])
+        fourth = [*done["G"], done["K"]]
+        d_tokens = done["X"]
     else:
         (down_sum,), third, fourth = (
             jnp.split(value, [sum(split[:i]) for i in range(1, len(split))], axis=1)
             for value, split in zip((second_sum, third_sum, fourth_sum), widths)
         )
-    vector = fourth[2]
+    d_tokens = (d_in1 + d_tokens).astype(BF16)
+    vector = fourth[1]
     return (
         token_out.astype(BF16).reshape(batch, rows, width),
         char_out.astype(BF16).reshape(batch, rows, width),
         d_tokens.reshape(batch, rows, width),
         d_chars,
-        fourth[0],
+        fourth[2],
         third[1],
         vector[:, 0],
         vector[:, 1],
@@ -1250,7 +1537,7 @@
         down_sum,
         vector[:, 2],
         vector[:, 3],
-        fourth[1],
+        fourth[0],
         vector[:, 4],
         third[2],
         third[3],

time: 641 us -> 578 us (0.902)
  the two profiles are of different devices: /device:TPU:16 before, /device:TPU:0 now
where the time goes in v1:
time: 578 us; the launch traced here: 570 us
  waiting for transfers between devices  182 us (31%)
  local copies, waits for them, and re-layouts  101 us (17%)
  Pallas kernels  101 us (17%)
  starting transfers between devices  90.2 us (16%)
  other arithmetic  48.9 us (8%)
  matrix products  31 us (5%)
  between operations  17.1 us (3%)
    ppermute x57, waiting for transfers between devices, flip(): lax.ppermute(value, axis, [(i, i ^ bit) for i in range(lax.axis_size(axis...  154 us
    ppermute x57, starting transfers between devices, flip(): lax.ppermute(value, axis, [(i, i ^ bit) for i in range(lax.axis_size(axis...  63 us
    unnamed x333, local copies, waits for them, and re-layouts  62.9 us
    dot_general x8, matrix products, matmul_nt(): lax.dot_general(left, right, (((1,), (1,)), ((), ())), preferred_element_...  19.2 us
    pallas_call x1, Pallas kernels, attend_back(): pl.pallas_call(functools.partial(attend_back_kernel, heads, tokens), grid...  16.3 us
    pallas_call x2, Pallas kernels, finish(): pl.pallas_call(functools.partial(place_kernel, spans, self.order), in_spe...  15.2 us
    concatenate x6, other arithmetic, take(): jnp.concatenate([self.base, got], axis=0)  13.1 us
    dot_general x7, matrix products, matmul(): return jnp.dot(left, right, preferred_element_type=F32)  11.8 us
  transfers between devices with their start and end apart: 72, of which 26 were waited for; matrix products, arithmetic and copies ran while one was open for 19% of the time, Pallas kernels for 16%

profile of v1, /device:TPU:0, one launch (start us, length us, event | category | flops | bytes accessed | tf_op | source)
XLA Modules:
  0.0 570.3 jit_solution(10990808563651227532)
XLA Ops:
  20.1 2.5 collective-permute-start.1
  23.9 5.8 %all-to-all-start = ((bf16[8,136,768]{2,1,0:T(8,128)(2,1)}), bf16[8,136,768]{2,1,0:T(8,128)(2,1)S(1)}, u32[]{:S(2)}, u32[]{:S(2)}) async-start(bf16[8,136,768]{2,1,0:T(8,128)(2,1)} %bitcast.2), calls=%async_computation | async-start | bytes 3342336 | tf_op jit(solution)/shard_map/all_to_all | solution.py:1337
  30.3 4.7 fusion.50
  51.8 2.9 collective-permute-start.14
  57.8 2.6 gru_forward.1
  65.6 2.4 collective-permute-start.6
  68.0 8.6 %all-to-all-done.tok_ref = bf16[8,136,768]{2,1,0:T(8,128)(2,1)S(1)} async-done(((bf16[8,136,768]{2,1,0:T(8,128)(2,1)}), bf16[8,136,768]{2,1,0:T(8,128)(2,1)S(1)}, u32[]{:S(2)}, u32[]{:S(2)}) %all-to-all-start) | async-done | bytes 1671200 | tf_op jit(solution)/shard_map/all_to_all | solution.py:1337
  76.6 9.3 %attend.1 = (bf16[1024,256]{1,0:T(8,128)(2,1)S(1)}, f32[1024,384]{1,0:T(8,128)S(1)}, bf16[3,1024,128]{2,1,0:T(8,128)(2,1)S(1)}, bf16[3,1024,128]{2,1,0:T(8,128)(...) custom-call(bf16[8,136,768]{2,1,0:T(8,128)(2,1)S(1)} %all-to-all-done.tok_ref, ...), custom_call_target="tpu_custom_call" | custom-call | flops 1 | bytes 1 | tf_op jit(solution)/shard_map/attend/pallas_call | solution.py:501
  91.5 4.1 all-to-all-start.1
  101.5 2.4 collective-permute-start.7
  109.6 2.8 place_own.2
  120.4 7.8 %collective-permute-done.15 = bf16[2,96,1536]{2,1,0:T(8,128)(2,1)} collective-permute-done((bf16[2,96,1536]{2,1,0:T(8,128)(2,1)}, bf16[2,96,1536]{2,1,0:T(8,128)(2,1)}, u32[]{:S(2)}, u32[]{:S(2)}) %collective-permute-start.15) | collective-permute-done | bytes 589856 | tf_op jit(solution)/shard_map/ppermute | solution.py:949
  128.1 2.4 pad_maximum_fusion.7
  137.8 2.5 copy-done.13
  140.2 5.4 feed_forward.1
  145.6 11.6 %collective-permute-done.16 = bf16[4,96,1536]{2,1,0:T(8,128)(2,1)} collective-permute-done((bf16[4,96,1536]{2,1,0:T(8,128)(2,1)}, bf16[4,96,1536]{2,1,0:T(8,128)(2,1)}, u32[]{:S(2)}, u32[]{:S(2)}) %collective-permute-start.16) | collective-permute-done | bytes 1179680 | tf_op jit(solution)/shard_map/ppermute | solution.py:949
  158.9 3.2 pad_maximum_fusion.1.piece_ref
  165.7 4.6 fusion.57
  170.8 2.5 copy-done.15
  173.3 7.6 %place.2 = (bf16[4,384,1536]{2,1,0:T(8,128)(2,1)S(1)}, bf16[4,192,1536]{2,1,0:T(8,128)(2,1)S(1)}) custom-call(bf16[8,72,1536]{2,1,0:T(8,128)(2,1)S(1)} %pad_maximum_fusion.4.piece_ref, bf16[8,72,1536]{2,1,0:T(8,128)(2,1)} %collective-permute-done.9.core_ref, bf16[4,384,1536]{2,1,0:T(8,128)(2,1)S(1)} %copy-done.15, ...), custom_call_target="tpu_custom_call", output_to_operand_aliasing={{0}: (2, {}), {1}: (3, {})} | custom-call | flops 1 | bytes 1 | tf_op jit(solution)/shard_map/place/pallas_call | solution.py:1237
  185.0 3.2 collective-permute-start.18
  196.4 7.6 %place.3 = (bf16[4,384,1536]{2,1,0:T(8,128)(2,1)S(1)}, bf16[4,384,1536]{2,1,0:T(8,128)(2,1)S(1)}) custom-call(bf16[8,96,1536]{2,1,0:T(8,128)(2,1)} %pad_maximum_fusion.1.piece_ref, bf16[8,96,1536]{2,1,0:T(8,128)(2,1)} %collective-permute-done.17.core_ref, bf16[4,384,1536]{2,1,0:T(8,128)(2,1)S(1)} %bitcast.165, ...), custom_call_target="tpu_custom_call", output_to_operand_aliasing={{0}: (2, {}), {1}: (3, {})} | custom-call | flops 1 | bytes 1 | tf_op jit(solution)/shard_map/place/pallas_call | solution.py:1237
  215.5 4.5 collective-permute-start.24
  223.1 3.9 fusion.60
  238.2 5.6 fusion.51
  243.9 2.3 multiply_reduce_fusion.1
  249.7 4.3 all-gather.16.cloned.1.call-done.grad_ref
  257.8 5.1 conv_gradient.3
  264.8 5.1 conv_gradient.2
  271.7 4.5 gradients.1
  276.3 3.3 copy-done
  279.7 5.7 all-to-all-start.2
  289.2 11.1 %all-to-all-done.2 = bf16[8,128,256]{2,1,0:T(8,128)(2,1)S(1)} async-done(((bf16[8,128,256]{2,1,0:T(8,128)(2,1)}), bf16[8,128,256]{2,1,0:T(8,128)(2,1)S(1)}, u32[]{:S(2)}, u32[]{:S(2)}) %all-to-all-start.2) | async-done | bytes 524320 | tf_op jit(solution)/shard_map/all_to_all | solution.py:1445
  306.4 16.3 %attend_back.1 = (bf16[1024,768]{1,0:T(8,128)(2,1)S(1)}, f32[768,576]{1,0:T(8,128)S(1)}, f32[2,1,768]{2,1,0:T(1,128)S(1)}) custom-call(bf16[8,136,768]{2,1,0:T(8,128)(2,1)S(1)} %all-to-all-done.tok_ref, bf16[768,576]{1,0:T(8,128)(2,1)S(1)} %copy-done.65, bf16[3,1024,128]{2,1,0:T(8,128)(2,1)S(1)} %copy-done.76, bf16[3,1024,128]{2,1,0:T(8,128)(2,1)S(1)} %copy-done.78, ...), custom_call_target="tpu_custom_call" | custom-call | flops 1 | bytes 1 | tf_op jit(solution)/shard_map/attend_back/pallas_call | solution.py:540
  322.9 2.3 add_convert_fusion.2
  326.0 5.8 %collective-permute-done.25 = bf16[3,192,768]{2,1,0:T(8,128)(2,1)} collective-permute-done((bf16[3,192,768]{2,1,0:T(8,128)(2,1)}, bf16[3,192,768]{2,1,0:T(8,128)(2,1)}, u32[]{:S(2)}, u32[]{:S(2)}) %collective-permute-start.25) | collective-permute-done | bytes 884768 | tf_op jit(solution)/shard_map/ppermute | solution.py:949
  341.5 3.3 last_gradients.1
  348.7 2.8 down_gradient.1
  351.5 2.4 collective-permute-start.28
  356.0 6.6 %collective-permute-done.29 = bf16[3,96,768]{2,1,0:T(8,128)(2,1)S(1)} collective-permute-done((bf16[3,96,768]{2,1,0:T(8,128)(2,1)S(1)}, bf16[3,96,768]{2,1,0:T(8,128)(2,1)S(1)}, u32[]{:S(2)}, u32[]{:S(2)}) %collective-permute-start.29) | collective-permute-done | bytes 442400 | tf_op jit(solution)/shard_map/ppermute | solution.py:949
  362.8 17.0 %collective-permute-done.28 = bf16[3,96,768]{2,1,0:T(8,128)(2,1)S(1)} collective-permute-done((bf16[3,96,768]{2,1,0:T(8,128)(2,1)S(1)}, bf16[3,96,768]{2,1,0:T(8,128)(2,1)S(1)}, u32[]{:S(2)}, u32[]{:S(2)}) %collective-permute-start.28) | collective-permute-done | bytes 442400 | tf_op jit(solution)/shard_map/ppermute | solution.py:949
  386.1 6.0 %collective-permute-done.31 = bf16[3,48,768]{2,1,0:T(8,128)(2,1)S(1)} collective-permute-done((bf16[3,48,768]{2,1,0:T(8,128)(2,1)S(1)}, bf16[3,48,768]{2,1,0:T(8,128)(2,1)S(1)}, u32[]{:S(2)}, u32[]{:S(2)}) %collective-permute-start.31) | collective-permute-done | bytes 221216 | tf_op jit(solution)/shard_map/ppermute | solution.py:949
  395.7 3.5 collective-permute-done.35
  399.9 3.1 collective-permute-start.40
  403.1 3.3 collective-permute-done.34
  409.7 12.4 %collective-permute-done.37 = bf16[192,768]{1,0:T(8,128)(2,1)S(1)} collective-permute-done((bf16[192,768]{1,0:T(8,128)(2,1)}, bf16[192,768]{1,0:T(8,128)(2,1)S(1)}, u32[]{:S(2)}, u32[]{:S(2)}) %collective-permute-start.37) | collective-permute-done | bytes 294944 | tf_op jit(solution)/shard_map/ppermute | solution.py:949
  426.0 2.9 collective-permute-start.36
  428.9 10.2 %collective-permute-done.40 = bf16[2,3,48,768]{3,2,1,0:T(8,128)(2,1)} collective-permute-done((bf16[2,3,48,768]{3,2,1,0:T(8,128)(2,1)}, bf16[2,3,48,768]{3,2,1,0:T(8,128)(2,1)}, u32[]{:S(2)}, u32[]{:S(2)}) %collective-permute-start.40) | collective-permute-done | bytes 442400 | tf_op jit(solution)/shard_map/ppermute | solution.py:949
  444.7 4.2 collective-permute-done.42
  450.1 4.3 collective-permute-start.45
  454.9 10.8 %collective-permute-done.45 = bf16[24,5376]{1,0:T(8,128)(2,1)S(1)} collective-permute-done((bf16[24,5376]{1,0:T(8,128)(2,1)S(1)}, bf16[24,5376]{1,0:T(8,128)(2,1)S(1)}, u32[]{:S(2)}, u32[]{:S(2)}) %collective-permute-start.45) | collective-permute-done | bytes 258080 | tf_op jit(solution)/shard_map/ppermute | solution.py:949
  465.8 18.8 %collective-permute-done.44 = bf16[96,1664]{1,0:T(8,128)(2,1)S(1)} collective-permute-done((bf16[96,1664]{1,0:T(8,128)(2,1)S(1)}, bf16[96,1664]{1,0:T(8,128)(2,1)S(1)}, u32[]{:S(2)}, u32[]{:S(2)}) %collective-permute-start.44) | collective-permute-done | bytes 319520 | tf_op jit(solution)/shard_map/ppermute | solution.py:949
  484.7 5.0 collective-permute-start.49
  489.8 8.8 %collective-permute-done.50 = bf16[2,96,768]{2,1,0:T(8,128)(2,1)S(1)} collective-permute-done((bf16[2,96,768]{2,1,0:T(8,128)(2,1)S(1)}, bf16[2,96,768]{2,1,0:T(8,128)(2,1)S(1)}, u32[]{:S(2)}, u32[]{:S(2)}) %collective-permute-start.50) | collective-permute-done | bytes 294944 | tf_op jit(solution)/shard_map/ppermute | solution.py:949
  499.2 7.3 %collective-permute-done.48 = bf16[48,1664]{1,0:T(8,128)(2,1)S(1)} collective-permute-done((bf16[48,1664]{1,0:T(8,128)(2,1)S(1)}, bf16[48,1664]{1,0:T(8,128)(2,1)S(1)}, u32[]{:S(2)}, u32[]{:S(2)}) %collective-permute-start.48) | collective-permute-done | bytes 159776 | tf_op jit(solution)/shard_map/ppermute | solution.py:949
  513.2 7.7 %collective-permute-done.53 = bf16[2,24,5376]{2,1,0:T(8,128)(2,1)S(1)} collective-permute-done((bf16[2,24,5376]{2,1,0:T(8,128)(2,1)S(1)}, bf16[2,24,5376]{2,1,0:T(8,128)(2,1)S(1)}, u32[]{:S(2)}, u32[]{:S(2)}) %collective-permute-start.53) | collective-permute-done | bytes 516128 | tf_op jit(solution)/shard_map/ppermute | solution.py:949
  522.6 3.5 collective-permute-done.51
  532.2 3.9 settle_half.2.refs_0_
  536.1 3.6 settle.3
  541.2 2.7 collective-permute-start.60
  544.1 4.7 collective-permute-done.60
  549.8 3.9 settle_half.3
  553.7 3.3 settle.5
  558.3 4.0 settle.4
  (639 shorter events, 197.2 us)
Async XLA Ops:
  7.2 47.5 %all-gather.8.cloned.1.call-start = ((), (), s32[]{:S(2)}) async-start(), calls=%async_computation.5 | async-start | bytes 3194880 | tf_op jit(solution)/shard_map/all_gather | solution.py:1274
  16.1 117.6 %all-gather.10.cloned.1.call-start = ((), (), s32[]{:S(2)}) async-start(), calls=%async_computation.6 | async-start | bytes 1474560 | tf_op jit(solution)/shard_map/all_gather | solution.py:1274
  16.8 120.9 %all-gather.12.cloned.1.call-start = ((), (), s32[]{:S(2)}) async-start(), calls=%async_computation.7 | async-start | bytes 5898240 | tf_op jit(solution)/shard_map/all_gather | solution.py:1274
  19.6 30.0 %collective-permute-start = (bf16[192,576]{1,0:T(8,128)(2,1)}, bf16[192,576]{1,0:T(8,128)(2,1)}, u32[]{:S(2)}, u32[]{:S(2)}) collective-permute-start(bf16[192,576]{1,0:T(8,128)(2,1)} %pad_maximum_fusion.32.own_ref), channel_id=1, source_target_pairs={{0,1},{1,0},{2,3},{3,2},{4,5},{5,4},{6,7},{7,6},{8,9},{9,8},{10,11... | collective-permute-start | bytes 663560 | tf_op jit(solution)/shard_map/ppermute | solution.py:949
  20.1 31.2 %collective-permute-start.1 = (bf16[192,576]{1,0:T(8,128)(2,1)}, bf16[192,576]{1,0:T(8,128)(2,1)}, u32[]{:S(2)}, u32[]{:S(2)}) collective-permute-start(bf16[192,576]{1,0:T(8,128)(2,1)} %pad_maximum_fusion.32.own_ref), channel_id=1, source_target_pairs={{0,2},{1,3},{2,0},{3,1},{4,6},{5,7},{6,4},{7,5},{8,10},{9,11},{10,... | collective-permute-start | bytes 663560 | tf_op jit(solution)/shard_map/ppermute | solution.py:949
  23.9 52.6 %all-to-all-start = ((bf16[8,136,768]{2,1,0:T(8,128)(2,1)}), bf16[8,136,768]{2,1,0:T(8,128)(2,1)S(1)}, u32[]{:S(2)}, u32[]{:S(2)}) async-start(bf16[8,136,768]{2,1,0:T(8,128)(2,1)} %bitcast.2), calls=%async_computation | async-start | bytes 3342336 | tf_op jit(solution)/shard_map/all_to_all | solution.py:1337
  29.7 135.9 %all-gather.14.cloned.1.call-start = ((), (), s32[]{:S(2)}) async-start(), calls=%async_computation.8 | async-start | bytes 5898240 | tf_op jit(solution)/shard_map/all_gather | solution.py:1274
  37.7 14.0 %collective-permute-start.13 = (bf16[96,1536]{1,0:T(8,128)(2,1)}, bf16[96,1536]{1,0:T(8,128)(2,1)}, u32[]{:S(2)}, u32[]{:S(2)}) collective-permute-start(bf16[96,1536]{1,0:T(8,128)(2,1)} %pad_maximum_fusion.30), channel_id=1, source_target_pairs={{0,2},{1,3},{2,0},{3,1},{4,6},{5,7},{6,4},{7,5},{8,10},{9,11},{10,... | collective-permute-start | bytes 884744 | tf_op jit(solution)/shard_map/ppermute | solution.py:949
  39.8 69.8 %collective-permute-start.3 = (bf16[768,1536]{1,0:T(8,128)(2,1)}, bf16[768,1536]{1,0:T(8,128)(2,1)}, u32[]{:S(2)}, u32[]{:S(2)}) collective-permute-start(bf16[768,1536]{1,0:T(8,128)(2,1)} %pad_maximum_fusion.own_ref), channel_id=1, source_target_pairs={{0,1},{1,0},{2,3},{3,2},{4,5},{5,4},{6,7},{7,6},{8,9},{9,8},{10,11... | collective-permute-start | bytes 7077896 | tf_op jit(solution)/shard_map/ppermute | solution.py:949
  41.4 62.5 %collective-permute-start.4 = (bf16[576,1536]{1,0:T(8,128)(2,1)S(1)}, bf16[576,1536]{1,0:T(8,128)(2,1)}, u32[]{:S(2)}, u32[]{:S(2)}) collective-permute-start(bf16[576,1536]{1,0:T(8,128)(2,1)S(1)} %pad_maximum_fusion.3.own_ref), channel_id=1, source_target_pairs={{0,1},{1,0},{2,3},{3,2},{4,5},{5,4},{6,7},{7,6},{8,9},{9,8},{10,11... | collective-permute-start | bytes 5308424 | tf_op jit(solution)/shard_map/ppermute | solution.py:949
  49.7 18.3 %collective-permute-start.2 = (bf16[192,576]{1,0:T(8,128)(2,1)}, bf16[192,576]{1,0:T(8,128)(2,1)}, u32[]{:S(2)}, u32[]{:S(2)}) collective-permute-start(bf16[192,576]{1,0:T(8,128)(2,1)} %pad_maximum_fusion.32.own_ref), channel_id=1, source_target_pairs={{0,3},{1,2},{2,1},{3,0},{4,7},{5,6},{6,5},{7,4},{8,11},{9,10},{10,... | collective-permute-start | bytes 663560 | tf_op jit(solution)/shard_map/ppermute | solution.py:949
  51.2 14.4 %collective-permute-start.5 = (bf16[72,1536]{1,0:T(8,128)(2,1)}, bf16[72,1536]{1,0:T(8,128)(2,1)}, u32[]{:S(2)}, u32[]{:S(2)}) collective-permute-start(bf16[72,1536]{1,0:T(8,128)(2,1)} %pad_maximum_fusion.33), channel_id=1, source_target_pairs={{0,2},{1,3},{2,0},{3,1},{4,6},{5,7},{6,4},{7,5},{8,10},{9,11},{10,... | collective-permute-start | bytes 663560 | tf_op jit(solution)/shard_map/ppermute | solution.py:949
  51.8 39.7 %collective-permute-start.14 = (bf16[1,96,1536]{2,1,0:T(8,128)(2,1)}, bf16[1,96,1536]{2,1,0:T(8,128)(2,1)}, u32[]{:S(2)}, u32[]{:S(2)}) collective-permute-start(bf16[1,96,1536]{2,1,0:T(8,128)(2,1)} %bitcast.22), channel_id=1, source_target_pairs={{0,16},{4,20},{8,24},{12,28},{16,0},{20,4},{24,8},{28,12},{1,17},{... | collective-permute-start | bytes 884744 | tf_op jit(solution)/shard_map/ppermute | solution.py:949
  65.6 34.1 %collective-permute-start.6 = (bf16[1,72,1536]{2,1,0:T(8,128)(2,1)}, bf16[1,72,1536]{2,1,0:T(8,128)(2,1)}, u32[]{:S(2)}, u32[]{:S(2)}) collective-permute-start(bf16[1,72,1536]{2,1,0:T(8,128)(2,1)} %bitcast.16), channel_id=1, source_target_pairs={{0,4},{4,0},{8,12},{12,8},{16,20},{20,16},{24,28},{28,24},{1,5},{5... | collective-permute-start | bytes 663560 | tf_op jit(solution)/shard_map/ppermute | solution.py:949
  91.5 27.6 %all-to-all-start.1 = ((bf16[8,128,256]{2,1,0:T(8,128)(2,1)}), bf16[8,128,256]{2,1,0:T(8,128)(2,1)}, u32[]{:S(2)}, u32[]{:S(2)}) async-start(bf16[8,128,256]{2,1,0:T(8,128)(2,1)} %bitcast.189), calls=%async_computation.1 | async-start | bytes 1048576 | tf_op jit(solution)/shard_map/all_to_all | solution.py:1343
  95.6 158.4 %all-gather.16.cloned.1.call-start = ((), (), s32[]{:S(2)}) async-start(), calls=%async_computation.9 | async-start | bytes 4177920 | tf_op jit(solution)/shard_map/all_gather | solution.py:1274
  97.8 30.3 %collective-permute-start.15 = (bf16[2,96,1536]{2,1,0:T(8,128)(2,1)}, bf16[2,96,1536]{2,1,0:T(8,128)(2,1)}, u32[]{:S(2)}, u32[]{:S(2)}) collective-permute-start(bf16[2,96,1536]{2,1,0:T(8,128)(2,1)} %pad_maximum_fusion.22), channel_id=1, source_target_pairs={{0,8},{4,12},{8,0},{12,4},{16,24},{20,28},{24,16},{28,20},{1,9},{5... | collective-permute-start | bytes 1769480 | tf_op jit(solution)/shard_map/ppermute | solution.py:949
  101.5 29.9 %collective-permute-start.7 = (bf16[2,72,1536]{2,1,0:T(8,128)(2,1)}, bf16[2,72,1536]{2,1,0:T(8,128)(2,1)}, u32[]{:S(2)}, u32[]{:S(2)}) collective-permute-start(bf16[2,72,1536]{2,1,0:T(8,128)(2,1)} %pad_maximum_fusion.26), channel_id=1, source_target_pairs={{0,16},{4,20},{8,24},{12,28},{16,0},{20,4},{24,8},{28,12},{1,17},{... | collective-permute-start | bytes 1327112 | tf_op jit(solution)/shard_map/ppermute | solution.py:949
  130.5 26.7 %collective-permute-start.16 = (bf16[4,96,1536]{2,1,0:T(8,128)(2,1)}, bf16[4,96,1536]{2,1,0:T(8,128)(2,1)}, u32[]{:S(2)}, u32[]{:S(2)}) collective-permute-start(bf16[4,96,1536]{2,1,0:T(8,128)(2,1)} %pad_maximum_fusion.7), channel_id=1, source_target_pairs={{0,4},{4,0},{8,12},{12,8},{16,20},{20,16},{24,28},{28,24},{1,5},{5... | collective-permute-start | bytes 3538952 | tf_op jit(solution)/shard_map/ppermute | solution.py:949
  133.7 23.5 %collective-permute-start.8 = (bf16[4,72,1536]{2,1,0:T(8,128)(2,1)}, bf16[4,72,1536]{2,1,0:T(8,128)(2,1)}, u32[]{:S(2)}, u32[]{:S(2)}) collective-permute-start(bf16[4,72,1536]{2,1,0:T(8,128)(2,1)} %pad_maximum_fusion.11), channel_id=1, source_target_pairs={{0,8},{4,12},{8,0},{12,4},{16,24},{20,28},{24,16},{28,20},{1,9},{5... | collective-permute-start | bytes 2654216 | tf_op jit(solution)/shard_map/ppermute | solution.py:949
  158.8 12.0 %collective-permute-start.9 = (bf16[8,72,1536]{2,1,0:T(8,128)(2,1)S(1)}, bf16[8,72,1536]{2,1,0:T(8,128)(2,1)}, u32[]{:S(2)}, u32[]{:S(2)}) collective-permute-start(bf16[8,72,1536]{2,1,0:T(8,128)(2,1)S(1)} %pad_maximum_fusion.4.piece_ref), channel_id=1, source_target_pairs={{0,1},{1,0},{2,3},{3,2},{4,5},{5,4},{6,7},{7,6},{8,9},{9,8},{10,11... | collective-permute-start | bytes 5308424 | tf_op jit(solution)/shard_map/ppermute | solution.py:949
  162.1 33.5 %collective-permute-start.17 = (bf16[8,96,1536]{2,1,0:T(8,128)(2,1)}, bf16[8,96,1536]{2,1,0:T(8,128)(2,1)}, u32[]{:S(2)}, u32[]{:S(2)}) collective-permute-start(bf16[8,96,1536]{2,1,0:T(8,128)(2,1)} %pad_maximum_fusion.1.piece_ref), channel_id=1, source_target_pairs={{0,1},{1,0},{2,3},{3,2},{4,5},{5,4},{6,7},{7,6},{8,9},{9,8},{10,11... | collective-permute-start | bytes 7077896 | tf_op jit(solution)/shard_map/ppermute | solution.py:949
  163.8 21.1 %collective-permute-start.10 = (bf16[256,768]{1,0:T(8,128)(2,1)}, bf16[256,768]{1,0:T(8,128)(2,1)}, u32[]{:S(2)}, u32[]{:S(2)}) collective-permute-start(bf16[256,768]{1,0:T(8,128)(2,1)} %get-tuple-element.275), channel_id=1, source_target_pairs={{0,1},{1,0},{2,3},{3,2},{4,5},{5,4},{6,7},{7,6},{8,9},{9,8},{10,11... | collective-permute-start | bytes 1179656 | tf_op jit(solution)/shard_map/ppermute | solution.py:949
  163.8 21.1 %collective-permute-start.11 = (bf16[256,768]{1,0:T(8,128)(2,1)}, bf16[256,768]{1,0:T(8,128)(2,1)}, u32[]{:S(2)}, u32[]{:S(2)}) collective-permute-start(bf16[256,768]{1,0:T(8,128)(2,1)} %get-tuple-element.274), channel_id=1, source_target_pairs={{0,2},{1,3},{2,0},{3,1},{4,6},{5,7},{6,4},{7,5},{8,10},{9,11},{10,... | collective-permute-start | bytes 1179656 | tf_op jit(solution)/shard_map/ppermute | solution.py:949
  164.3 20.6 %collective-permute-start.12 = (bf16[256,768]{1,0:T(8,128)(2,1)}, bf16[256,768]{1,0:T(8,128)(2,1)}, u32[]{:S(2)}, u32[]{:S(2)}) collective-permute-start(bf16[256,768]{1,0:T(8,128)(2,1)} %get-tuple-element.273), channel_id=1, source_target_pairs={{0,3},{1,2},{2,1},{3,0},{4,7},{5,6},{6,5},{7,4},{8,11},{9,10},{10,... | collective-permute-start | bytes 1179656 | tf_op jit(solution)/shard_map/ppermute | solution.py:949
  190.4 29.7 %collective-permute-start.20 = (bf16[256,384]{1,0:T(8,128)(2,1)S(1)}, bf16[256,384]{1,0:T(8,128)(2,1)S(1)}, u32[]{:S(2)}, u32[]{:S(2)}) collective-permute-start(bf16[256,384]{1,0:T(8,128)(2,1)S(1)} %get-tuple-element.286), channel_id=1, source_target_pairs={{0,1},{1,0},{2,3},{3,2},{4,5},{5,4},{6,7},{7,6},{8,9},{9,8},{10,11... | collective-permute-start | bytes 589832 | tf_op jit(solution)/shard_map/ppermute | solution.py:949
  190.4 29.7 %collective-permute-start.21 = (bf16[256,384]{1,0:T(8,128)(2,1)S(1)}, bf16[256,384]{1,0:T(8,128)(2,1)S(1)}, u32[]{:S(2)}, u32[]{:S(2)}) collective-permute-start(bf16[256,384]{1,0:T(8,128)(2,1)S(1)} %get-tuple-element.285), channel_id=1, source_target_pairs={{0,2},{1,3},{2,0},{3,1},{4,6},{5,7},{6,4},{7,5},{8,10},{9,11},{10,... | collective-permute-start | bytes 589832 | tf_op jit(solution)/shard_map/ppermute | solution.py:949
  191.0 29.8 %collective-permute-start.22 = (bf16[256,384]{1,0:T(8,128)(2,1)S(1)}, bf16[256,384]{1,0:T(8,128)(2,1)S(1)}, u32[]{:S(2)}, u32[]{:S(2)}) collective-permute-start(bf16[256,384]{1,0:T(8,128)(2,1)S(1)} %get-tuple-element.284), channel_id=1, source_target_pairs={{0,3},{1,2},{2,1},{3,0},{4,7},{5,6},{6,5},{7,4},{8,11},{9,10},{10,... | collective-permute-start | bytes 589832 | tf_op jit(solution)/shard_map/ppermute | solution.py:949
  222.6 124.6 %all-gather.18.cloned.1.call-start = ((), (), s32[]{:S(2)}) async-start(), calls=%async_computation.12 | async-start | bytes 1966080 | tf_op jit(solution)/shard_map/all_gather | solution.py:1274
  233.4 158.9 %reduce-scatter.3.cloned.1.call-start = ((), (), s32[]{:S(2)}) async-start(), calls=%async_computation.10 | async-start | bytes 10321920 | tf_op jit(solution)/shard_map/reduce_scatter | solution.py:1252
  279.7 20.5 %all-to-all-start.2 = ((bf16[8,128,256]{2,1,0:T(8,128)(2,1)}), bf16[8,128,256]{2,1,0:T(8,128)(2,1)S(1)}, u32[]{:S(2)}, u32[]{:S(2)}) async-start(bf16[8,128,256]{2,1,0:T(8,128)(2,1)} %copy-done.31), calls=%async_computation.2 | async-start | bytes 1048576 | tf_op jit(solution)/shard_map/all_to_all | solution.py:1445
  285.4 138.4 %reduce-scatter.5.cloned.1.call-start = ((), (), s32[]{:S(2)}) async-start(), calls=%async_computation.11 | async-start | bytes 4423680 | tf_op jit(solution)/shard_map/reduce_scatter | solution.py:1252
  285.4 37.4 %collective-permute-start.26 = (bf16[3,192,768]{2,1,0:T(8,128)(2,1)}, bf16[3,192,768]{2,1,0:T(8,128)(2,1)}, u32[]{:S(2)}, u32[]{:S(2)}) collective-permute-start(bf16[3,192,768]{2,1,0:T(8,128)(2,1)} %copy-done.90), channel_id=1, source_target_pairs={{0,4},{4,0},{8,12},{12,8},{16,20},{20,16},{24,28},{28,24},{1,5},{5... | collective-permute-start | bytes 2654216 | tf_op jit(solution)/shard_map/ppermute | solution.py:949
  287.4 44.4 %collective-permute-start.25 = (bf16[3,192,768]{2,1,0:T(8,128)(2,1)}, bf16[3,192,768]{2,1,0:T(8,128)(2,1)}, u32[]{:S(2)}, u32[]{:S(2)}) collective-permute-start(bf16[3,192,768]{2,1,0:T(8,128)(2,1)} %copy-done.89), channel_id=1, source_target_pairs={{0,4},{4,0},{8,12},{12,8},{16,20},{20,16},{24,28},{28,24},{1,5},{5... | collective-permute-start | bytes 2654216 | tf_op jit(solution)/shard_map/ppermute | solution.py:949
  345.8 16.8 %collective-permute-start.29 = (bf16[3,96,768]{2,1,0:T(8,128)(2,1)S(1)}, bf16[3,96,768]{2,1,0:T(8,128)(2,1)S(1)}, u32[]{:S(2)}, u32[]{:S(2)}) collective-permute-start(bf16[3,96,768]{2,1,0:T(8,128)(2,1)S(1)} %copy-done.118), channel_id=1, source_target_pairs={{0,8},{4,12},{8,0},{12,4},{16,24},{20,28},{24,16},{28,20},{1,9},{5... | collective-permute-start | bytes 1327112 | tf_op jit(solution)/shard_map/ppermute | solution.py:949
  351.5 28.4 %collective-permute-start.28 = (bf16[3,96,768]{2,1,0:T(8,128)(2,1)S(1)}, bf16[3,96,768]{2,1,0:T(8,128)(2,1)S(1)}, u32[]{:S(2)}, u32[]{:S(2)}) collective-permute-start(bf16[3,96,768]{2,1,0:T(8,128)(2,1)S(1)} %constant_dynamic-slice_fusion.13), channel_id=1, source_target_pairs={{0,16},{4,20},{8,24},{12,28},{16,0},{20,4},{24,8},{28,12},{1,17},{... | collective-permute-start | bytes 1327112 | tf_op jit(solution)/shard_map/ppermute | solution.py:949
  353.9 26.2 %collective-permute-start.27 = (bf16[2,2,1,128,768]{4,3,0,2,1:T(8,128)(2,1)S(1)}, bf16[2,2,1,128,768]{4,3,0,2,1:T(8,128)(2,1)S(1)}, u32[]{:S(2)}, u32[]{:S(2)}) collective-permute-start(bf16[2,2,1,128,768]{4,3,0,2,1:T(8,128)(2,1)S(1)} %copy-done.115), channel_id=1, source_target_pairs={{0,4},{4,0},{8,12},{12,8},{16,20},{20,16},{24,28},{28,24},{1,5},{5... | collective-permute-start | bytes 2359304 | tf_op jit(solution)/shard_map/ppermute | solution.py:949
  354.2 30.5 %collective-permute-start.33 = (bf16[384,768]{1,0:T(8,128)(2,1)S(1)}, bf16[384,768]{1,0:T(8,128)(2,1)S(1)}, u32[]{:S(2)}, u32[]{:S(2)}) collective-permute-start(bf16[384,768]{1,0:T(8,128)(2,1)S(1)} %constant_dynamic-slice_fusion.10), channel_id=1, source_target_pairs={{0,4},{4,0},{8,12},{12,8},{16,20},{20,16},{24,28},{28,24},{1,5},{5... | collective-permute-start | bytes 1769480 | tf_op jit(solution)/shard_map/ppermute | solution.py:949
  362.8 22.8 %collective-permute-start.32 = (bf16[3,48,768]{2,1,0:T(8,128)(2,1)S(1)}, bf16[3,48,768]{2,1,0:T(8,128)(2,1)S(1)}, u32[]{:S(2)}, u32[]{:S(2)}) collective-permute-start(bf16[3,48,768]{2,1,0:T(8,128)(2,1)S(1)} %constant_dynamic-slice_fusion.9), channel_id=1, source_target_pairs={{0,16},{4,20},{8,24},{12,28},{16,0},{20,4},{24,8},{28,12},{1,17},{... | collective-permute-start | bytes 663560 | tf_op jit(solution)/shard_map/ppermute | solution.py:949
  380.0 12.1 %collective-permute-start.31 = (bf16[3,48,768]{2,1,0:T(8,128)(2,1)S(1)}, bf16[3,48,768]{2,1,0:T(8,128)(2,1)S(1)}, u32[]{:S(2)}, u32[]{:S(2)}) collective-permute-start(bf16[3,48,768]{2,1,0:T(8,128)(2,1)S(1)} %constant_dynamic-slice_fusion.8), channel_id=1, source_target_pairs={{0,8},{4,12},{8,0},{12,4},{16,24},{20,28},{24,16},{28,20},{1,9},{5... | collective-permute-start | bytes 663560 | tf_op jit(solution)/shard_map/ppermute | solution.py:949
  381.1 26.7 %collective-permute-start.30 = (bf16[2,1,128,768]{3,2,1,0:T(8,128)(2,1)}, bf16[2,1,128,768]{3,2,1,0:T(8,128)(2,1)}, u32[]{:S(2)}, u32[]{:S(2)}) collective-permute-start(bf16[2,1,128,768]{3,2,1,0:T(8,128)(2,1)} %dynamic-slice_bitcast_fusion), channel_id=1, source_target_pairs={{0,8},{4,12},{8,0},{12,4},{16,24},{20,28},{24,16},{28,20},{1,9},{5... | collective-permute-start | bytes 1179656 | tf_op jit(solution)/shard_map/ppermute | solution.py:949
  385.7 13.5 %collective-permute-start.35 = (bf16[1,3,48,768]{3,2,1,0:T(8,128)(2,1)S(1)}, bf16[1,3,48,768]{3,2,1,0:T(8,128)(2,1)S(1)}, u32[]{:S(2)}, u32[]{:S(2)}) collective-permute-start(bf16[1,3,48,768]{3,2,1,0:T(8,128)(2,1)S(1)} %fusion.38), channel_id=1, source_target_pairs={{0,16},{4,20},{8,24},{12,28},{16,0},{20,4},{24,8},{28,12},{1,17},{... | collective-permute-start | bytes 663560 | tf_op jit(solution)/shard_map/ppermute | solution.py:949
  392.1 14.2 %collective-permute-start.34 = (bf16[1,3,48,768]{3,2,1,0:T(8,128)(2,1)S(1)}, bf16[1,3,48,768]{3,2,1,0:T(8,128)(2,1)S(1)}, u32[]{:S(2)}, u32[]{:S(2)}) collective-permute-start(bf16[1,3,48,768]{3,2,1,0:T(8,128)(2,1)S(1)} %fusion.39), channel_id=1, source_target_pairs={{0,8},{4,12},{8,0},{12,4},{16,24},{20,28},{24,16},{28,20},{1,9},{5... | collective-permute-start | bytes 663560 | tf_op jit(solution)/shard_map/ppermute | solution.py:949
  393.5 28.7 %collective-permute-start.41 = (bf16[96,5376]{1,0:T(8,128)(2,1)S(1)}, bf16[96,5376]{1,0:T(8,128)(2,1)S(1)}, u32[]{:S(2)}, u32[]{:S(2)}) collective-permute-start(bf16[96,5376]{1,0:T(8,128)(2,1)S(1)} %constant_dynamic-slice_fusion.6), channel_id=1, source_target_pairs={{0,4},{4,0},{8,12},{12,8},{16,20},{20,16},{24,28},{28,24},{1,5},{5... | collective-permute-start | bytes 3096584 | tf_op jit(solution)/shard_map/ppermute | solution.py:949
  393.6 28.5 %collective-permute-start.37 = (bf16[192,768]{1,0:T(8,128)(2,1)}, bf16[192,768]{1,0:T(8,128)(2,1)S(1)}, u32[]{:S(2)}, u32[]{:S(2)}) collective-permute-start(bf16[192,768]{1,0:T(8,128)(2,1)} %constant_dynamic-slice_fusion.7), channel_id=1, source_target_pairs={{0,8},{4,12},{8,0},{12,4},{16,24},{20,28},{24,16},{28,20},{1,9},{5... | collective-permute-start | bytes 884744 | tf_op jit(solution)/shard_map/ppermute | solution.py:949
  399.9 39.2 %collective-permute-start.40 = (bf16[2,3,48,768]{3,2,1,0:T(8,128)(2,1)}, bf16[2,3,48,768]{3,2,1,0:T(8,128)(2,1)}, u32[]{:S(2)}, u32[]{:S(2)}) collective-permute-start(bf16[2,3,48,768]{3,2,1,0:T(8,128)(2,1)} %pad_maximum_fusion.27), channel_id=1, source_target_pairs={{0,8},{4,12},{8,0},{12,4},{16,24},{20,28},{24,16},{28,20},{1,9},{5... | collective-permute-start | bytes 1327112 | tf_op jit(solution)/shard_map/ppermute | solution.py:949
  407.2 33.6 %collective-permute-start.39 = (bf16[2,3,48,768]{3,2,1,0:T(8,128)(2,1)}, bf16[2,3,48,768]{3,2,1,0:T(8,128)(2,1)}, u32[]{:S(2)}, u32[]{:S(2)}) collective-permute-start(bf16[2,3,48,768]{3,2,1,0:T(8,128)(2,1)} %pad_maximum_fusion.28), channel_id=1, source_target_pairs={{0,16},{4,20},{8,24},{12,28},{16,0},{20,4},{24,8},{28,12},{1,17},{... | collective-permute-start | bytes 1327112 | tf_op jit(solution)/shard_map/ppermute | solution.py:949
  423.8 25.1 %collective-permute-start.42 = (bf16[48,5376]{1,0:T(8,128)(2,1)}, bf16[48,5376]{1,0:T(8,128)(2,1)}, u32[]{:S(2)}, u32[]{:S(2)}) collective-permute-start(bf16[48,5376]{1,0:T(8,128)(2,1)} %constant_dynamic-slice_fusion.4), channel_id=1, source_target_pairs={{0,8},{4,12},{8,0},{12,4},{16,24},{20,28},{24,16},{28,20},{1,9},{5... | collective-permute-start | bytes 1548296 | tf_op jit(solution)/shard_map/ppermute | solution.py:949
  425.9 17.6 %collective-permute-start.38 = (bf16[96,768]{1,0:T(8,128)(2,1)S(1)}, bf16[96,768]{1,0:T(8,128)(2,1)S(1)}, u32[]{:S(2)}, u32[]{:S(2)}) collective-permute-start(bf16[96,768]{1,0:T(8,128)(2,1)S(1)} %constant_dynamic-slice_fusion.5), channel_id=1, source_target_pairs={{0,16},{4,20},{8,24},{12,28},{16,0},{20,4},{24,8},{28,12},{1,17},{... | collective-permute-start | bytes 442376 | tf_op jit(solution)/shard_map/ppermute | solution.py:949
  426.0 106.2 %collective-permute-start.36 = (bf16[1,128,768]{2,1,0:T(8,128)(2,1)}, bf16[1,128,768]{2,1,0:T(8,128)(2,1)S(1)}, u32[]{:S(2)}, u32[]{:S(2)}) collective-permute-start(bf16[1,128,768]{2,1,0:T(8,128)(2,1)} %get-tuple-element.296), channel_id=1, source_target_pairs={{0,16},{4,20},{8,24},{12,28},{16,0},{20,4},{24,8},{28,12},{1,17},{... | collective-permute-start | bytes 589832 | tf_op jit(solution)/shard_map/ppermute | solution.py:949
  440.2 67.6 %collective-permute-start.55 = (bf16[4,3,48,768]{3,2,1,0:T(8,128)(2,1)S(1)}, bf16[4,3,48,768]{3,2,1,0:T(8,128)(2,1)S(1)}, u32[]{:S(2)}, u32[]{:S(2)}) collective-permute-start(bf16[4,3,48,768]{3,2,1,0:T(8,128)(2,1)S(1)} %pad_maximum_fusion.12), channel_id=1, source_target_pairs={{0,4},{4,0},{8,12},{12,8},{16,20},{20,16},{24,28},{28,24},{1,5},{5... | collective-permute-start | bytes 2654216 | tf_op jit(solution)/shard_map/ppermute | solution.py:949
  441.9 68.3 %collective-permute-start.54 = (bf16[4,3,48,768]{3,2,1,0:T(8,128)(2,1)S(1)}, bf16[4,3,48,768]{3,2,1,0:T(8,128)(2,1)S(1)}, u32[]{:S(2)}, u32[]{:S(2)}) collective-permute-start(bf16[4,3,48,768]{3,2,1,0:T(8,128)(2,1)S(1)} %pad_maximum_fusion.13), channel_id=1, source_target_pairs={{0,4},{4,0},{8,12},{12,8},{16,20},{20,16},{24,28},{28,24},{1,5},{5... | collective-permute-start | bytes 2654216 | tf_op jit(solution)/shard_map/ppermute | solution.py:949
  443.5 10.9 %collective-permute-start.46 = (bf16[1,96,768]{2,1,0:T(8,128)(2,1)S(1)}, bf16[1,96,768]{2,1,0:T(8,128)(2,1)S(1)}, u32[]{:S(2)}, u32[]{:S(2)}) collective-permute-start(bf16[1,96,768]{2,1,0:T(8,128)(2,1)S(1)} %fusion.40), channel_id=1, source_target_pairs={{0,16},{4,20},{8,24},{12,28},{16,0},{20,4},{24,8},{28,12},{1,17},{... | collective-permute-start | bytes 442376 | tf_op jit(solution)/shard_map/ppermute | solution.py:949
  450.1 15.7 %collective-permute-start.45 = (bf16[24,5376]{1,0:T(8,128)(2,1)S(1)}, bf16[24,5376]{1,0:T(8,128)(2,1)S(1)}, u32[]{:S(2)}, u32[]{:S(2)}) collective-permute-start(bf16[24,5376]{1,0:T(8,128)(2,1)S(1)} %constant_dynamic-slice_fusion.3), channel_id=1, source_target_pairs={{0,16},{4,20},{8,24},{12,28},{16,0},{20,4},{24,8},{28,12},{1,17},{... | collective-permute-start | bytes 774152 | tf_op jit(solution)/shard_map/ppermute | solution.py:949
  454.4 30.2 %collective-permute-start.44 = (bf16[96,1664]{1,0:T(8,128)(2,1)S(1)}, bf16[96,1664]{1,0:T(8,128)(2,1)S(1)}, u32[]{:S(2)}, u32[]{:S(2)}) collective-permute-start(bf16[96,1664]{1,0:T(8,128)(2,1)S(1)} %constant_dynamic-slice_fusion.2), channel_id=1, source_target_pairs={{0,4},{4,0},{8,12},{12,8},{16,20},{20,16},{24,28},{28,24},{1,5},{5... | collective-permute-start | bytes 958472 | tf_op jit(solution)/shard_map/ppermute | solution.py:949
  465.7 19.0 %collective-permute-start.43 = (bf16[192,576]{1,0:T(8,128)(2,1)S(1)}, bf16[192,576]{1,0:T(8,128)(2,1)S(1)}, u32[]{:S(2)}, u32[]{:S(2)}) collective-permute-start(bf16[192,576]{1,0:T(8,128)(2,1)S(1)} %slice.207), channel_id=1, source_target_pairs={{0,16},{4,20},{8,24},{12,28},{16,0},{20,4},{24,8},{28,12},{1,17},{... | collective-permute-start | bytes 663560 | tf_op jit(solution)/shard_map/ppermute | solution.py:949
  484.6 14.0 %collective-permute-start.50 = (bf16[2,96,768]{2,1,0:T(8,128)(2,1)S(1)}, bf16[2,96,768]{2,1,0:T(8,128)(2,1)S(1)}, u32[]{:S(2)}, u32[]{:S(2)}) collective-permute-start(bf16[2,96,768]{2,1,0:T(8,128)(2,1)S(1)} %pad_maximum_fusion.31), channel_id=1, source_target_pairs={{0,8},{4,12},{8,0},{12,4},{16,24},{20,28},{24,16},{28,20},{1,9},{5... | collective-permute-start | bytes 884744 | tf_op jit(solution)/shard_map/ppermute | solution.py:949
  484.7 13.9 %collective-permute-start.49 = (bf16[1,24,5376]{2,1,0:T(8,128)(2,1)S(1)}, bf16[1,24,5376]{2,1,0:T(8,128)(2,1)S(1)}, u32[]{:S(2)}, u32[]{:S(2)}) collective-permute-start(bf16[1,24,5376]{2,1,0:T(8,128)(2,1)S(1)} %fusion.36), channel_id=1, source_target_pairs={{0,16},{4,20},{8,24},{12,28},{16,0},{20,4},{24,8},{28,12},{1,17},{... | collective-permute-start | bytes 774152 | tf_op jit(solution)/shard_map/ppermute | solution.py:949
  506.5 14.4 %collective-permute-start.53 = (bf16[2,24,5376]{2,1,0:T(8,128)(2,1)S(1)}, bf16[2,24,5376]{2,1,0:T(8,128)(2,1)S(1)}, u32[]{:S(2)}, u32[]{:S(2)}) collective-permute-start(bf16[2,24,5376]{2,1,0:T(8,128)(2,1)S(1)} %pad_maximum_fusion.24), channel_id=1, source_target_pairs={{0,8},{4,12},{8,0},{12,4},{16,24},{20,28},{24,16},{28,20},{1,9},{5... | collective-permute-start | bytes 1548296 | tf_op jit(solution)/shard_map/ppermute | solution.py:949
  507.5 18.8 %collective-permute-start.58 = (bf16[4,96,768]{2,1,0:T(8,128)(2,1)S(1)}, bf16[4,96,768]{2,1,0:T(8,128)(2,1)S(1)}, u32[]{:S(2)}, u32[]{:S(2)}) collective-permute-start(bf16[4,96,768]{2,1,0:T(8,128)(2,1)S(1)} %pad_maximum_fusion.23), channel_id=1, source_target_pairs={{0,4},{4,0},{8,12},{12,8},{16,20},{20,16},{24,28},{28,24},{1,5},{5... | collective-permute-start | bytes 1769480 | tf_op jit(solution)/shard_map/ppermute | solution.py:949
  507.8 14.6 %collective-permute-start.52 = (bf16[24,1664]{1,0:T(8,128)(2,1)S(1)}, bf16[24,1664]{1,0:T(8,128)(2,1)S(1)}, u32[]{:S(2)}, u32[]{:S(2)}) collective-permute-start(bf16[24,1664]{1,0:T(8,128)(2,1)S(1)} %constant_dynamic-slice_fusion), channel_id=1, source_target_pairs={{0,16},{4,20},{8,24},{12,28},{16,0},{20,4},{24,8},{28,12},{1,17},{... | collective-permute-start | bytes 239624 | tf_op jit(solution)/shard_map/ppermute | solution.py:949
  510.2 15.9 %collective-permute-start.51 = (bf16[2,192,576]{2,1,0:T(8,128)(2,1)S(1)}, bf16[2,192,576]{2,1,0:T(8,128)(2,1)S(1)}, u32[]{:S(2)}, u32[]{:S(2)}) collective-permute-start(bf16[2,192,576]{2,1,0:T(8,128)(2,1)S(1)} %pad_maximum_fusion.25), channel_id=1, source_target_pairs={{0,8},{4,12},{8,0},{12,4},{16,24},{20,28},{24,16},{28,20},{1,9},{5... | collective-permute-start | bytes 1327112 | tf_op jit(solution)/shard_map/ppermute | solution.py:949
  521.0 23.0 %collective-permute-start.56 = (bf16[4,24,5376]{2,1,0:T(8,128)(2,1)S(1)}, bf16[4,24,5376]{2,1,0:T(8,128)(2,1)S(1)}, u32[]{:S(2)}, u32[]{:S(2)}) collective-permute-start(bf16[4,24,5376]{2,1,0:T(8,128)(2,1)S(1)} %pad_maximum_fusion.9), channel_id=1, source_target_pairs={{0,4},{4,0},{8,12},{12,8},{16,20},{20,16},{24,28},{28,24},{1,5},{5... | collective-permute-start | bytes 3096584 | tf_op jit(solution)/shard_map/ppermute | solution.py:949
  528.0 13.2 %collective-permute-start.59 = (bf16[2,24,1664]{2,1,0:T(8,128)(2,1)S(1)}, bf16[2,24,1664]{2,1,0:T(8,128)(2,1)S(1)}, u32[]{:S(2)}, u32[]{:S(2)}) collective-permute-start(bf16[2,24,1664]{2,1,0:T(8,128)(2,1)S(1)} %pad_maximum_fusion.34), channel_id=1, source_target_pairs={{0,8},{4,12},{8,0},{12,4},{16,24},{20,28},{24,16},{28,20},{1,9},{5... | collective-permute-start | bytes 479240 | tf_op jit(solution)/shard_map/ppermute | solution.py:949
  (171 other events, 1394.4 us)
Sparse Core Ops, SparseCore 0:
  16.2 30.9 all-gather.7
  48.8 21.8 all-gather.9
  72.3 38.8 all-gather.11
  112.6 37.4 all-gather.13
  222.7 31.2 all-gather.15
  256.0 19.6 all-gather.17
  279.8 70.9 reduce-scatter.2
  353.9 40.4 reduce-scatter.4

commit v2 on v1

--- a/solution.py
+++ b/solution.py
@@ -702,18 +702,30 @@
     )(hidden1, context, hidden2, chars, d_pre, d_attn, d_joined)
 
 
-def down_grad_kernel(own_ref, core_ref, far_ref, far_core_ref, grad_ref, out_ref):
-    total = jnp.zeros(out_ref.shape, F32)
+def store_halves(total, keep_ref, send_ref, lead):
+    half = total.shape[0] // 2
+    halves = (total[:half].astype(BF16), total[half:].astype(BF16))
+    for mine in (0, 1):
+
+        @pl.when(lax.rem(lax.axis_index("ctx"), 2) == mine)
+        def store():
+            keep_ref[lead] = halves[mine]
+            send_ref[lead] = halves[1 - mine]
+
+
+def down_grad_kernel(own_ref, core_ref, far_ref, far_core_ref, grad_ref, keep_ref, send_ref):
+    total = jnp.zeros((own_ref.shape[1], grad_ref.shape[2]), F32)
     for other, inner_ref in enumerate((own_ref, core_ref, far_ref, far_core_ref)):
         source = jnp.bitwise_xor(lax.axis_index("fsdp"), other)
         total = total + matmul_tn(inner_ref[...], grad_ref[source])
-    out_ref[...] = total.astype(BF16)
+    store_halves(total, keep_ref, send_ref, ...)
 
 
 def down_gradient(inner, grads):
+    half = jax.ShapeDtypeStruct((inner[0].shape[1] // 2, grads.shape[2]), BF16)
     return pl.pallas_call(
         down_grad_kernel,
-        out_shape=jax.ShapeDtypeStruct((inner[0].shape[1], grads.shape[2]), BF16),
+        out_shape=[half, half],
         compiler_params=params(),
         cost_estimate=cost(1, 1),
         name="down_gradient",
@@ -754,14 +766,7 @@
                 side_scr[here] = jnp.where(row == 0, before, moved).astype(BF16)
 
         total = total + matmul_tn(joined_ref[...], side_scr[...])
-    half = keep_ref.shape[1]
-    halves = (total[:half].astype(BF16), total[half:].astype(BF16))
-    for mine in (0, 1):
-
-        @pl.when(lax.rem(lax.axis_index("ctx"), 2) == mine)
-        def store():
-            keep_ref[0] = halves[mine]
-            send_ref[0] = halves[1 - mine]
+    store_halves(total, keep_ref, send_ref, 0)
 
 
 def conv_gradient(joined, grads, rows, part):
@@ -785,15 +790,22 @@
 
 def last_grads_kernel(chars_ref, gates_ref, small_ref, heads_ref, out_ref):
     wide = gates_ref.shape[1]
-    narrow = small_ref.shape[1]
+    narrow = 128
     out_ref[:, :wide] = matmul_tn(chars_ref[...], gates_ref[...]).astype(BF16)
-    out_ref[:, wide : wide + narrow] = small_ref[...].astype(BF16)
+    count = small_ref.shape[0]
+    eye = jnp.where(
+        lax.broadcasted_iota(jnp.int32, (count, narrow), 0)
+        == lax.broadcasted_iota(jnp.int32, (count, narrow), 1),
+        1.0,
+        0.0,
+    ).astype(BF16)
+    out_ref[:, wide : wide + narrow] = matmul_tn(small_ref[...].astype(BF16), eye).astype(BF16)
     out_ref[:, wide + narrow :] = heads_ref[...].astype(BF16)
 
 
 def last_gradients(chars, d_gates, small, heads_grad):
     width = chars.shape[1]
-    wide = d_gates.shape[1] + small.shape[1] + heads_grad.shape[1]
+    wide = d_gates.shape[1] + 128 + heads_grad.shape[1]
     return pl.pallas_call(
         last_grads_kernel,
         out_shape=jax.ShapeDtypeStruct((width, wide), BF16),
@@ -942,7 +954,7 @@
 
 STEPS = (1, 2, 4)
 OTHER_STEPS = (1, 4, 2)
-ORDER = "DABXDABTABXDTABDXTGKDTGKDTGKABTGKDGGTG"
+ORDER = "XABTXABDXTABDXGKTABDGKTDGKTDGKABTGDGTDG"
 
 
 def flip(value, axis, bit):
@@ -1054,18 +1066,21 @@
         return self.sent
 
 
-def run_in_order(chains, finish, ready):
+def run_in_order(chains, finish, begin):
     last, done = (), {}
+    final = max(i for i, name in enumerate(ORDER[:-2]) if name == "G")
     for event, name in enumerate(ORDER):
+        others = last
+        if event == final or event == len(ORDER) - 1:
+            ready = [done[other] for other in "ABKDT" if other in done]
+            others = others + tuple(jax.tree.leaves(ready))
+        step = chains[name].advance if name in chains else begin[name]
+        last = (step(*others),)
         chain = chains[name]
-        others = last
         if event == ORDER.index("T"):
-            others = others + (ready,)
-        if event == len(ORDER) - 3:
-            others = others + tuple(done["D"]) + (done["K"],)
-        last = (chain.advance(*others),)
+            begin["last"](*last)
         if hasattr(chain, "result"):
-            done[name] = finish[name](chain.result)
+            done[name] = finish[name](chain.result, done)
     return done
 
 
@@ -1433,25 +1448,23 @@
     d_attn = d_in1.astype(BF16)
     if heads:
         sent = send_grad(d_attn, w_out, back_edges, heads, batch)
-        conv_pieces = [after(joined_own[0], sent)] + joined_own[1:]
+        hidden1_b = after(hidden1_b, sent)
+    third = gradients(hidden1_b, context_b, hidden2_b, char_tok_b, d_pre_low, d_attn, d_joined)
+    third_sum = reduced(third)
+
+    if heads:
+        conv_pieces = [after(joined_own[0], sent, third)] + joined_own[1:]
         first_chain = CtxSum.begun(*conv_gradient(conv_pieces, d_all, rows, 0))
         other_chain = CtxSum.begun(*conv_gradient(conv_pieces, d_all, rows, 1), OTHER_STEPS)
-        hidden1_b = after(hidden1_b, first_chain.sent, other_chain.sent)
-    third_sum = reduced(
-        gradients(hidden1_b, context_b, hidden2_b, char_tok_b, d_pre_low, d_attn, d_joined)
-    )
-
-    if heads:
         received = lax.all_to_all(sent, "ctx", 0, 0, tiled=True)
+        received = after(received, first_chain.sent, other_chain.sent)
         d_tok_part, heads_grad, back_enter = attend_back(
             tokens_all, w_heads, saved, kept, received.reshape(count * rows, -1), edges_all,
             heads, rows,
         )
         token_chain = TokenSum(d_tok_part.reshape(2, 2, 2, rows, width))
         last = other_chain.advance(first_chain.advance(heads_grad))
-        last = token_chain.advance(last)
         gate = after(gate, last)
-        second_chain = CtxSum(down_gradient(inner_own, d_ffn_all))
     else:
         back_enter = back_entering(edges_all, all_edges(back_edges))
         d_context = matmul_nt(d_attn, w_out).reshape(batch, rows, width)
@@ -1474,21 +1487,19 @@
         heads_grad = matmul_tn(flat_tokens, d_qkv)
         d_tokens = matmul_nt(d_qkv, w_qkv)
 
-    small = jnp.stack(
-        [
-            gain1_grad, bias1_grad, gain2_grad, bias2_grad, jnp.sum(bgate_grad, axis=(0, 1)),
-            gain3_grad, bias3_grad, gain4_grad, bias4_grad,
-        ],
-        axis=1,
-    )
-    up_small = bup_grad.reshape(shards, -1, width // shards)
-    up_small = jnp.swapaxes(up_small, 1, 2).reshape(width, -1)
-    small = jnp.concatenate([small, up_small], axis=1)
-    small = jnp.pad(small, ((0, 0), (0, 128 - small_count)))
-    fourth = last_gradients(
-        chars_pad.reshape(batch * padded_rows, width), d_gate_in, small, heads_grad
-    )
-    fourth_sum = reduced(fourth)
+    small = [
+        gain1_grad, bias1_grad, gain2_grad, bias2_grad, jnp.sum(bgate_grad, axis=(0, 1)),
+        gain3_grad, bias3_grad, gain4_grad, bias4_grad,
+    ]
+    up_small = jnp.swapaxes(bup_grad.reshape(shards, -1, width // shards), 0, 1)
+    small = jnp.concatenate([value[None] for value in small] + [up_small.reshape(-1, width)])
+    small = jnp.pad(small, ((0, 16 - small_count), (0, 0)))
+
+    def last_sum(*others):
+        gates = after(d_gate_in, *others) if others else d_gate_in
+        return last_gradients(
+            chars_pad.reshape(batch * padded_rows, width), gates, small, heads_grad
+        )
 
     widths = ((width,), (w_up.shape[1],) + (width,) * 3, (wide_gru, 128, width_qkv))
     if routed():
@@ -1496,30 +1507,41 @@
         chains = dict(
             A=first_chain,
             B=other_chain,
-            D=second_chain,
             X=token_chain,
             T=CtxSum(third_sum),
-            G=CtxSum(fourth_sum[:, :own_wide]),
-            K=HeadSum(fourth_sum[:, own_wide:]),
-        )
+        )
+
+        def begin_down(*others):
+            chains["D"] = CtxSum.begun(*down_gradient(after(inner_own, *others), d_ffn_all))
+            return chains["D"].sent
+
+        def begin_last(*others):
+            chains["last"] = reduced(last_sum(*others))
+
+        def begin_G(*others):
+            value = after(chains["last"], *others)
+            chains["G"] = CtxSum(value[:, :own_wide])
+            chains["K"] = HeadSum(value[:, own_wide:])
+            return chains["G"].advance()
+
         finish = dict(
-            A=lambda value: settle_half(value, STEPS, 0),
-            B=lambda value: value,
-            D=lambda value: settle(value, widths[0]),
-            T=lambda value: settle(value, widths[1]),
-            G=lambda value: settle(value, widths[2][:2]),
-            K=lambda value: spread_columns(value, heads),
-            X=lambda value: value.reshape(total_rows, width),
-        )
-        done = run_in_order(chains, finish, fourth)
+            A=lambda value, done: settle_half(value, STEPS, 0),
+            B=lambda value, done: settle_half(value, OTHER_STEPS, 1, done.pop("A")),
+            D=lambda value, done: settle(value, widths[0]),
+            T=lambda value, done: settle(value, widths[1]),
+            G=lambda value, done: settle(value, widths[2][:2]),
+            K=lambda value, done: spread_columns(value, heads),
+            X=lambda value, done: value.reshape(total_rows, width),
+        )
+        done = run_in_order(chains, finish, dict(D=begin_down, G=begin_G, last=begin_last))
         (down_sum,), third = done["D"], done["T"]
-        conv_sum = settle_half(done["B"], OTHER_STEPS, 1, done["A"])
+        conv_sum = done["B"]
         fourth = [*done["G"], done["K"]]
         d_tokens = done["X"]
     else:
         (down_sum,), third, fourth = (
             jnp.split(value, [sum(split[:i]) for i in range(1, len(split))], axis=1)
-            for value, split in zip((second_sum, third_sum, fourth_sum), widths)
+            for value, split in zip((second_sum, third_sum, reduced(last_sum())), widths)
         )
     d_tokens = (d_in1 + d_tokens).astype(BF16)
     vector = fourth[1]

time: 578 us -> 570 us (0.986)
  waiting for transfers between devices: 182 us -> 148 us
  starting transfers between devices: 90.2 us -> 107 us
  other arithmetic: 48.9 us -> 58.1 us
    ppermute x57, waiting for transfers between devices: 154 us -> 136 us  [flip(): lax.ppermute(value, axis, [(i, i ^ bit) for i in range(lax.axis_size(axis...]
    all_gather x6, starting transfers between devices: 0.45 us -> 11.6 us  [gather(): return lax.all_gather(weight, 'fsdp', axis=axis, tiled=True)]
    all_to_all x1, waiting for transfers between devices: 11.1 us -> 0.01 us  [local(): received = lax.all_to_all(sent, 'ctx', 0, 0, tiled=True)]
    unnamed x333 -> x292, local copies, waits for them, and re-layouts: 62.9 us -> 62.1 us
  transfers between devices with their start and end apart: 72 -> 72, of which waited for: 26 -> 26; matrix products, arithmetic and copies ran while one was open for 19% -> 21% of each run, Pallas kernels for 16% -> 18%
where the time goes in v2:
time: 570 us; the launch traced here: 561 us
  waiting for transfers between devices  148 us (26%)
  starting transfers between devices  107 us (19%)
  Pallas kernels  102 us (18%)
  local copies, waits for them, and re-layouts  101 us (18%)
  other arithmetic  58.1 us (10%)
  matrix products  28.2 us (5%)
  between operations  16.6 us (3%)
    ppermute x57, waiting for transfers between devices, flip(): lax.ppermute(value, axis, [(i, i ^ bit) for i in range(lax.axis_size(axis...  136 us
    ppermute x57, starting transfers between devices, flip(): lax.ppermute(value, axis, [(i, i ^ bit) for i in range(lax.axis_size(axis...  68.7 us
    unnamed x292, local copies, waits for them, and re-layouts  62.1 us
    dot_general x8, matrix products, matmul_nt(): lax.dot_general(left, right, (((1,), (1,)), ((), ())), preferred_element_...  16.4 us
    pallas_call x1, Pallas kernels, attend_back(): pl.pallas_call(functools.partial(attend_back_kernel, heads, tokens), grid...  16.3 us
    pallas_call x2, Pallas kernels, finish(): pl.pallas_call(functools.partial(place_kernel, spans, self.order), in_spe...  15.2 us
    concatenate x6, other arithmetic, take(): jnp.concatenate([self.base, got], axis=0)  13.1 us
    convert_element_type x12, other arithmetic, advance(): piece = (self.keep.astype(F32) + got).astype(BF16)  12.3 us
  transfers between devices with their start and end apart: 72, of which 26 were waited for; matrix products, arithmetic and copies ran while one was open for 21% of the time, Pallas kernels for 18%

profile of v2, /device:TPU:0, one launch (start us, length us, event | category | flops | bytes accessed | tf_op | source)
XLA Modules:
  0.0 561.4 jit_solution(16850436058244678212)
XLA Ops:
  20.1 2.5 collective-permute-start.1
  23.9 5.8 %all-to-all-start = ((bf16[8,136,768]{2,1,0:T(8,128)(2,1)}), bf16[8,136,768]{2,1,0:T(8,128)(2,1)S(1)}, u32[]{:S(2)}, u32[]{:S(2)}) async-start(bf16[8,136,768]{2,1,0:T(8,128)(2,1)} %bitcast.2), calls=%async_computation | async-start | bytes 3342336 | tf_op jit(solution)/shard_map/all_to_all | solution.py:1352
  30.3 4.7 fusion.50
  51.7 2.9 collective-permute-start.14
  57.7 2.7 gru_forward.1
  65.6 2.4 collective-permute-start.6
  68.0 8.6 %all-to-all-done.tok_ref = bf16[8,136,768]{2,1,0:T(8,128)(2,1)S(1)} async-done(((bf16[8,136,768]{2,1,0:T(8,128)(2,1)}), bf16[8,136,768]{2,1,0:T(8,128)(2,1)S(1)}, u32[]{:S(2)}, u32[]{:S(2)}) %all-to-all-start) | async-done | bytes 1671200 | tf_op jit(solution)/shard_map/all_to_all | solution.py:1352
  76.6 9.3 %attend.1 = (bf16[1024,256]{1,0:T(8,128)(2,1)S(1)}, f32[1024,384]{1,0:T(8,128)S(1)}, bf16[3,1024,128]{2,1,0:T(8,128)(2,1)S(1)}, bf16[3,1024,128]{2,1,0:T(8,128)(...) custom-call(bf16[8,136,768]{2,1,0:T(8,128)(2,1)S(1)} %all-to-all-done.tok_ref, ...), custom_call_target="tpu_custom_call" | custom-call | flops 1 | bytes 1 | tf_op jit(solution)/shard_map/attend/pallas_call | solution.py:501
  91.5 4.1 all-to-all-start.1
  101.5 2.4 collective-permute-start.7
  109.6 2.8 place_own.2
  119.8 8.3 %collective-permute-done.15 = bf16[2,96,1536]{2,1,0:T(8,128)(2,1)} collective-permute-done((bf16[2,96,1536]{2,1,0:T(8,128)(2,1)}, bf16[2,96,1536]{2,1,0:T(8,128)(2,1)}, u32[]{:S(2)}, u32[]{:S(2)}) %collective-permute-start.15) | collective-permute-done | bytes 589856 | tf_op jit(solution)/shard_map/ppermute | solution.py:961
  128.1 2.4 pad_maximum_fusion.7
  131.4 2.2 pad_maximum_fusion.11
  137.7 2.5 copy-done.13
  140.2 5.4 feed_forward.1
  145.6 11.6 %collective-permute-done.16 = bf16[4,96,1536]{2,1,0:T(8,128)(2,1)} collective-permute-done((bf16[4,96,1536]{2,1,0:T(8,128)(2,1)}, bf16[4,96,1536]{2,1,0:T(8,128)(2,1)}, u32[]{:S(2)}, u32[]{:S(2)}) %collective-permute-start.16) | collective-permute-done | bytes 1179680 | tf_op jit(solution)/shard_map/ppermute | solution.py:961
  158.8 3.2 pad_maximum_fusion.1.piece_ref
  165.6 4.6 fusion.57
  170.7 2.5 copy-done.15
  173.2 7.6 %place.2 = (bf16[4,384,1536]{2,1,0:T(8,128)(2,1)S(1)}, bf16[4,192,1536]{2,1,0:T(8,128)(2,1)S(1)}) custom-call(bf16[8,72,1536]{2,1,0:T(8,128)(2,1)S(1)} %pad_maximum_fusion.4.piece_ref, bf16[8,72,1536]{2,1,0:T(8,128)(2,1)} %collective-permute-done.9.core_ref, bf16[4,384,1536]{2,1,0:T(8,128)(2,1)S(1)} %copy-done.15, ...), custom_call_target="tpu_custom_call", output_to_operand_aliasing={{0}: (2, {}), {1}: (3, {})} | custom-call | flops 1 | bytes 1 | tf_op jit(solution)/shard_map/place/pallas_call | solution.py:1252
  184.9 3.1 collective-permute-start.18
  196.2 7.6 %place.3 = (bf16[4,384,1536]{2,1,0:T(8,128)(2,1)S(1)}, bf16[4,384,1536]{2,1,0:T(8,128)(2,1)S(1)}) custom-call(bf16[8,96,1536]{2,1,0:T(8,128)(2,1)} %pad_maximum_fusion.1.piece_ref, bf16[8,96,1536]{2,1,0:T(8,128)(2,1)} %collective-permute-done.17.core_ref, bf16[4,384,1536]{2,1,0:T(8,128)(2,1)S(1)} %bitcast.165, ...), custom_call_target="tpu_custom_call", output_to_operand_aliasing={{0}: (2, {}), {1}: (3, {})} | custom-call | flops 1 | bytes 1 | tf_op jit(solution)/shard_map/place/pallas_call | solution.py:1252
  214.0 4.5 collective-permute-start.24
  224.9 3.9 fusion.60
  233.5 2.2 gru_back.1
  238.7 5.2 fusion.51
  249.4 4.5 gradients.1
  254.0 3.3 copy-done
  257.3 5.8 %all-to-all-start.2 = ((bf16[8,128,256]{2,1,0:T(8,128)(2,1)}), bf16[8,128,256]{2,1,0:T(8,128)(2,1)S(1)}, u32[]{:S(2)}, u32[]{:S(2)}) async-start(bf16[8,128,256]{2,1,0:T(8,128)(2,1)} %copy-done.31), calls=%async_computation.2 | async-start | bytes 1048576 | tf_op jit(solution)/shard_map/all_to_all | solution.py:1459
  263.1 11.2 %all-gather.18.cloned.1.call-start = ((), (), s32[]{:S(2)}) async-start(), calls=%async_computation.12 | async-start | bytes 1966080 | tf_op jit(solution)/shard_map/all_gather | solution.py:1289
  279.1 5.8 %conv_gradient.2 = (bf16[3,192,768]{2,1,0:T(8,128)(2,1)S(1)}, bf16[3,192,768]{2,1,0:T(8,128)(2,1)}) custom-call(bf16[256,384]{1,0:T(8,128)(2,1)S(1)} %get-tuple-element.163.own_ref, bf16[256,384]{1,0:T(8,128)(2,1)S(1)} %copy-done.68, bf16[256,384]{1,0:T(8,128)(2,1)S(1)} %copy-done.70, bf16[256,384]{1,0:T(8,128)(2,1)S(1)} %copy-done.72, ...), custom_call_target="tpu_custom_call" | custom-call | flops 1 | bytes 1 | tf_op jit(solution)/shard_map/conv_gradient/pallas_call | solution.py:777
  287.5 5.8 %conv_gradient.3 = (bf16[3,192,768]{2,1,0:T(8,128)(2,1)S(1)}, bf16[3,192,768]{2,1,0:T(8,128)(2,1)}) custom-call(bf16[256,384]{1,0:T(8,128)(2,1)S(1)} %get-tuple-element.163.own_ref, bf16[256,384]{1,0:T(8,128)(2,1)S(1)} %copy-done.68, bf16[256,384]{1,0:T(8,128)(2,1)S(1)} %copy-done.70, bf16[256,384]{1,0:T(8,128)(2,1)S(1)} %copy-done.72, ...), custom_call_target="tpu_custom_call" | custom-call | flops 1 | bytes 1 | tf_op jit(solution)/shard_map/conv_gradient/pallas_call | solution.py:777
  302.0 16.3 %attend_back.1 = (bf16[1024,768]{1,0:T(8,128)(2,1)S(1)}, f32[768,576]{1,0:T(8,128)S(1)}, f32[2,1,768]{2,1,0:T(1,128)S(1)}) custom-call(bf16[8,136,768]{2,1,0:T(8,128)(2,1)S(1)} %all-to-all-done.tok_ref, bf16[768,576]{1,0:T(8,128)(2,1)S(1)} %copy-done.62, bf16[3,1024,128]{2,1,0:T(8,128)(2,1)S(1)} %copy-done.74, bf16[3,1024,128]{2,1,0:T(8,128)(2,1)S(1)} %copy-done.76, ...), custom_call_target="tpu_custom_call" | custom-call | flops 1 | bytes 1 | tf_op jit(solution)/shard_map/attend_back/pallas_call | solution.py:540
  318.5 2.2 add_convert_fusion.2
  327.3 2.3 collective-permute-start.28
  332.7 2.6 collective-permute-done.29
  337.1 10.3 %collective-permute-done.28 = bf16[3,96,768]{2,1,0:T(8,128)(2,1)} collective-permute-done((bf16[3,96,768]{2,1,0:T(8,128)(2,1)}, bf16[3,96,768]{2,1,0:T(8,128)(2,1)}, u32[]{:S(2)}, u32[]{:S(2)}) %collective-permute-start.28) | collective-permute-done | bytes 442400 | tf_op jit(solution)/shard_map/ppermute | solution.py:961
  350.1 2.2 constant_dynamic-slice_fusion.8
  353.9 3.3 last_gradients.1
  358.5 3.7 collective-permute-start.31
  362.8 15.3 %collective-permute-done.25 = bf16[2,2,1,128,768]{4,3,2,1,0:T(8,128)(2,1)} collective-permute-done((bf16[2,2,1,128,768]{4,3,2,1,0:T(8,128)(2,1)}, bf16[2,2,1,128,768]{4,3,2,1,0:T(8,128)(2,1)}, u32[]{:S(2)}, u32[]{:S(2)}) %collective-permute-start.25) | collective-permute-done | bytes 786464 | tf_op jit(solution)/shard_map/ppermute | solution.py:961
  381.4 3.4 collective-permute-start.36
  387.1 3.1 down_gradient.1
  394.2 6.1 %collective-permute-done.37 = bf16[96,5376]{1,0:T(8,128)(2,1)} collective-permute-done((bf16[96,5376]{1,0:T(8,128)(2,1)}, bf16[96,5376]{1,0:T(8,128)(2,1)}, u32[]{:S(2)}, u32[]{:S(2)}) %collective-permute-start.37) | collective-permute-done | bytes 1032224 | tf_op jit(solution)/shard_map/ppermute | solution.py:961
  416.9 11.4 %collective-permute-done.43 = bf16[48,5376]{1,0:T(8,128)(2,1)} collective-permute-done((bf16[48,5376]{1,0:T(8,128)(2,1)}, bf16[48,5376]{1,0:T(8,128)(2,1)}, u32[]{:S(2)}, u32[]{:S(2)}) %collective-permute-start.43) | collective-permute-done | bytes 516128 | tf_op jit(solution)/shard_map/ppermute | solution.py:961
  431.1 4.5 collective-permute-done.42
  443.0 5.3 collective-permute-start.46
  448.4 3.2 collective-permute-done.38
  451.7 5.3 collective-permute-done.47
  457.9 9.6 %collective-permute-done.46 = bf16[96,768]{1,0:T(8,128)(2,1)S(1)} collective-permute-done((bf16[96,768]{1,0:T(8,128)(2,1)S(1)}, bf16[96,768]{1,0:T(8,128)(2,1)S(1)}, u32[]{:S(2)}, u32[]{:S(2)}) %collective-permute-start.46) | collective-permute-done | bytes 147488 | tf_op jit(solution)/shard_map/ppermute | solution.py:961
  467.5 3.0 collective-permute-start.50
  470.6 3.4 collective-permute-done.44
  481.7 9.9 %collective-permute-done.48 = bf16[2,192,576]{2,1,0:T(8,128)(2,1)S(1)} collective-permute-done((bf16[2,192,576]{2,1,0:T(8,128)(2,1)S(1)}, bf16[2,192,576]{2,1,0:T(8,128)(2,1)S(1)}, u32[]{:S(2)}, u32[]{:S(2)}) %collective-permute-start.48) | collective-permute-done | bytes 442400 | tf_op jit(solution)/shard_map/ppermute | solution.py:961
  494.4 7.3 %collective-permute-done.52 = bf16[2,24,5376]{2,1,0:T(8,128)(2,1)S(1)} collective-permute-done((bf16[2,24,5376]{2,1,0:T(8,128)(2,1)S(1)}, bf16[2,24,5376]{2,1,0:T(8,128)(2,1)S(1)}, u32[]{:S(2)}, u32[]{:S(2)}) %collective-permute-start.52) | collective-permute-done | bytes 516128 | tf_op jit(solution)/shard_map/ppermute | solution.py:961
  502.9 2.5 collective-permute-start.58
  507.7 4.6 collective-permute-done.33
  512.3 3.9 settle_half.2.refs_0_
  517.7 3.9 settle_half.3
  523.8 3.9 collective-permute-done.55
  527.9 12.4 %collective-permute-done.60 = bf16[4,96,768]{2,1,0:T(8,128)(2,1)S(1)} collective-permute-done((bf16[4,96,768]{2,1,0:T(8,128)(2,1)S(1)}, bf16[4,96,768]{2,1,0:T(8,128)(2,1)S(1)}, u32[]{:S(2)}, u32[]{:S(2)}) %collective-permute-start.60) | collective-permute-done | bytes 589856 | tf_op jit(solution)/shard_map/ppermute | solution.py:961
  540.5 4.0 settle.3
  544.5 3.6 settle.4
  549.0 3.3 settle.5
  (595 shorter events, 207.9 us)
Async XLA Ops:
  7.2 47.5 %all-gather.8.cloned.1.call-start = ((), (), s32[]{:S(2)}) async-start(), calls=%async_computation.5 | async-start | bytes 3194880 | tf_op jit(solution)/shard_map/all_gather | solution.py:1289
  16.1 117.6 %all-gather.10.cloned.1.call-start = ((), (), s32[]{:S(2)}) async-start(), calls=%async_computation.6 | async-start | bytes 1474560 | tf_op jit(solution)/shard_map/all_gather | solution.py:1289
  16.8 120.9 %all-gather.12.cloned.1.call-start = ((), (), s32[]{:S(2)}) async-start(), calls=%async_computation.7 | async-start | bytes 5898240 | tf_op jit(solution)/shard_map/all_gather | solution.py:1289
  19.6 30.0 %collective-permute-start = (bf16[192,576]{1,0:T(8,128)(2,1)}, bf16[192,576]{1,0:T(8,128)(2,1)}, u32[]{:S(2)}, u32[]{:S(2)}) collective-permute-start(bf16[192,576]{1,0:T(8,128)(2,1)} %pad_maximum_fusion.32.own_ref), channel_id=1, source_target_pairs={{0,1},{1,0},{2,3},{3,2},{4,5},{5,4},{6,7},{7,6},{8,9},{9,8},{10,11... | collective-permute-start | bytes 663560 | tf_op jit(solution)/shard_map/ppermute | solution.py:961
  20.1 31.1 %collective-permute-start.1 = (bf16[192,576]{1,0:T(8,128)(2,1)}, bf16[192,576]{1,0:T(8,128)(2,1)}, u32[]{:S(2)}, u32[]{:S(2)}) collective-permute-start(bf16[192,576]{1,0:T(8,128)(2,1)} %pad_maximum_fusion.32.own_ref), channel_id=1, source_target_pairs={{0,2},{1,3},{2,0},{3,1},{4,6},{5,7},{6,4},{7,5},{8,10},{9,11},{10,... | collective-permute-start | bytes 663560 | tf_op jit(solution)/shard_map/ppermute | solution.py:961
  23.9 52.6 %all-to-all-start = ((bf16[8,136,768]{2,1,0:T(8,128)(2,1)}), bf16[8,136,768]{2,1,0:T(8,128)(2,1)S(1)}, u32[]{:S(2)}, u32[]{:S(2)}) async-start(bf16[8,136,768]{2,1,0:T(8,128)(2,1)} %bitcast.2), calls=%async_computation | async-start | bytes 3342336 | tf_op jit(solution)/shard_map/all_to_all | solution.py:1352
  29.7 135.9 %all-gather.14.cloned.1.call-start = ((), (), s32[]{:S(2)}) async-start(), calls=%async_computation.8 | async-start | bytes 5898240 | tf_op jit(solution)/shard_map/all_gather | solution.py:1289
  37.7 14.0 %collective-permute-start.13 = (bf16[96,1536]{1,0:T(8,128)(2,1)}, bf16[96,1536]{1,0:T(8,128)(2,1)}, u32[]{:S(2)}, u32[]{:S(2)}) collective-permute-start(bf16[96,1536]{1,0:T(8,128)(2,1)} %pad_maximum_fusion.30), channel_id=1, source_target_pairs={{0,2},{1,3},{2,0},{3,1},{4,6},{5,7},{6,4},{7,5},{8,10},{9,11},{10,... | collective-permute-start | bytes 884744 | tf_op jit(solution)/shard_map/ppermute | solution.py:961
  39.8 69.8 %collective-permute-start.3 = (bf16[768,1536]{1,0:T(8,128)(2,1)}, bf16[768,1536]{1,0:T(8,128)(2,1)}, u32[]{:S(2)}, u32[]{:S(2)}) collective-permute-start(bf16[768,1536]{1,0:T(8,128)(2,1)} %pad_maximum_fusion.own_ref), channel_id=1, source_target_pairs={{0,1},{1,0},{2,3},{3,2},{4,5},{5,4},{6,7},{7,6},{8,9},{9,8},{10,11... | collective-permute-start | bytes 7077896 | tf_op jit(solution)/shard_map/ppermute | solution.py:961
  41.4 62.5 %collective-permute-start.4 = (bf16[576,1536]{1,0:T(8,128)(2,1)S(1)}, bf16[576,1536]{1,0:T(8,128)(2,1)}, u32[]{:S(2)}, u32[]{:S(2)}) collective-permute-start(bf16[576,1536]{1,0:T(8,128)(2,1)S(1)} %pad_maximum_fusion.3.own_ref), channel_id=1, source_target_pairs={{0,1},{1,0},{2,3},{3,2},{4,5},{5,4},{6,7},{7,6},{8,9},{9,8},{10,11... | collective-permute-start | bytes 5308424 | tf_op jit(solution)/shard_map/ppermute | solution.py:961
  49.7 18.3 %collective-permute-start.2 = (bf16[192,576]{1,0:T(8,128)(2,1)}, bf16[192,576]{1,0:T(8,128)(2,1)}, u32[]{:S(2)}, u32[]{:S(2)}) collective-permute-start(bf16[192,576]{1,0:T(8,128)(2,1)} %pad_maximum_fusion.32.own_ref), channel_id=1, source_target_pairs={{0,3},{1,2},{2,1},{3,0},{4,7},{5,6},{6,5},{7,4},{8,11},{9,10},{10,... | collective-permute-start | bytes 663560 | tf_op jit(solution)/shard_map/ppermute | solution.py:961
  51.2 14.4 %collective-permute-start.5 = (bf16[72,1536]{1,0:T(8,128)(2,1)}, bf16[72,1536]{1,0:T(8,128)(2,1)}, u32[]{:S(2)}, u32[]{:S(2)}) collective-permute-start(bf16[72,1536]{1,0:T(8,128)(2,1)} %pad_maximum_fusion.33), channel_id=1, source_target_pairs={{0,2},{1,3},{2,0},{3,1},{4,6},{5,7},{6,4},{7,5},{8,10},{9,11},{10,... | collective-permute-start | bytes 663560 | tf_op jit(solution)/shard_map/ppermute | solution.py:961
  51.7 39.7 %collective-permute-start.14 = (bf16[1,96,1536]{2,1,0:T(8,128)(2,1)}, bf16[1,96,1536]{2,1,0:T(8,128)(2,1)}, u32[]{:S(2)}, u32[]{:S(2)}) collective-permute-start(bf16[1,96,1536]{2,1,0:T(8,128)(2,1)} %bitcast.22), channel_id=1, source_target_pairs={{0,16},{4,20},{8,24},{12,28},{16,0},{20,4},{24,8},{28,12},{1,17},{... | collective-permute-start | bytes 884744 | tf_op jit(solution)/shard_map/ppermute | solution.py:961
  65.6 34.1 %collective-permute-start.6 = (bf16[1,72,1536]{2,1,0:T(8,128)(2,1)}, bf16[1,72,1536]{2,1,0:T(8,128)(2,1)}, u32[]{:S(2)}, u32[]{:S(2)}) collective-permute-start(bf16[1,72,1536]{2,1,0:T(8,128)(2,1)} %bitcast.16), channel_id=1, source_target_pairs={{0,4},{4,0},{8,12},{12,8},{16,20},{20,16},{24,28},{28,24},{1,5},{5... | collective-permute-start | bytes 663560 | tf_op jit(solution)/shard_map/ppermute | solution.py:961
  91.5 27.0 %all-to-all-start.1 = ((bf16[8,128,256]{2,1,0:T(8,128)(2,1)}), bf16[8,128,256]{2,1,0:T(8,128)(2,1)}, u32[]{:S(2)}, u32[]{:S(2)}) async-start(bf16[8,128,256]{2,1,0:T(8,128)(2,1)} %bitcast.189), calls=%async_computation.1 | async-start | bytes 1048576 | tf_op jit(solution)/shard_map/all_to_all | solution.py:1358
  95.6 178.7 %all-gather.16.cloned.1.call-start = ((), (), s32[]{:S(2)}) async-start(), calls=%async_computation.9 | async-start | bytes 4177920 | tf_op jit(solution)/shard_map/all_gather | solution.py:1289
  97.8 30.3 %collective-permute-start.15 = (bf16[2,96,1536]{2,1,0:T(8,128)(2,1)}, bf16[2,96,1536]{2,1,0:T(8,128)(2,1)}, u32[]{:S(2)}, u32[]{:S(2)}) collective-permute-start(bf16[2,96,1536]{2,1,0:T(8,128)(2,1)} %pad_maximum_fusion.22), channel_id=1, source_target_pairs={{0,8},{4,12},{8,0},{12,4},{16,24},{20,28},{24,16},{28,20},{1,9},{5... | collective-permute-start | bytes 1769480 | tf_op jit(solution)/shard_map/ppermute | solution.py:961
  101.5 29.9 %collective-permute-start.7 = (bf16[2,72,1536]{2,1,0:T(8,128)(2,1)}, bf16[2,72,1536]{2,1,0:T(8,128)(2,1)}, u32[]{:S(2)}, u32[]{:S(2)}) collective-permute-start(bf16[2,72,1536]{2,1,0:T(8,128)(2,1)} %pad_maximum_fusion.26), channel_id=1, source_target_pairs={{0,16},{4,20},{8,24},{12,28},{16,0},{20,4},{24,8},{28,12},{1,17},{... | collective-permute-start | bytes 1327112 | tf_op jit(solution)/shard_map/ppermute | solution.py:961
  130.4 26.7 %collective-permute-start.16 = (bf16[4,96,1536]{2,1,0:T(8,128)(2,1)}, bf16[4,96,1536]{2,1,0:T(8,128)(2,1)}, u32[]{:S(2)}, u32[]{:S(2)}) collective-permute-start(bf16[4,96,1536]{2,1,0:T(8,128)(2,1)} %pad_maximum_fusion.7), channel_id=1, source_target_pairs={{0,4},{4,0},{8,12},{12,8},{16,20},{20,16},{24,28},{28,24},{1,5},{5... | collective-permute-start | bytes 3538952 | tf_op jit(solution)/shard_map/ppermute | solution.py:961
  133.6 23.5 %collective-permute-start.8 = (bf16[4,72,1536]{2,1,0:T(8,128)(2,1)}, bf16[4,72,1536]{2,1,0:T(8,128)(2,1)}, u32[]{:S(2)}, u32[]{:S(2)}) collective-permute-start(bf16[4,72,1536]{2,1,0:T(8,128)(2,1)} %pad_maximum_fusion.11), channel_id=1, source_target_pairs={{0,8},{4,12},{8,0},{12,4},{16,24},{20,28},{24,16},{28,20},{1,9},{5... | collective-permute-start | bytes 2654216 | tf_op jit(solution)/shard_map/ppermute | solution.py:961
  158.7 12.0 %collective-permute-start.9 = (bf16[8,72,1536]{2,1,0:T(8,128)(2,1)S(1)}, bf16[8,72,1536]{2,1,0:T(8,128)(2,1)}, u32[]{:S(2)}, u32[]{:S(2)}) collective-permute-start(bf16[8,72,1536]{2,1,0:T(8,128)(2,1)S(1)} %pad_maximum_fusion.4.piece_ref), channel_id=1, source_target_pairs={{0,1},{1,0},{2,3},{3,2},{4,5},{5,4},{6,7},{7,6},{8,9},{9,8},{10,11... | collective-permute-start | bytes 5308424 | tf_op jit(solution)/shard_map/ppermute | solution.py:961
  162.0 33.3 %collective-permute-start.17 = (bf16[8,96,1536]{2,1,0:T(8,128)(2,1)}, bf16[8,96,1536]{2,1,0:T(8,128)(2,1)}, u32[]{:S(2)}, u32[]{:S(2)}) collective-permute-start(bf16[8,96,1536]{2,1,0:T(8,128)(2,1)} %pad_maximum_fusion.1.piece_ref), channel_id=1, source_target_pairs={{0,1},{1,0},{2,3},{3,2},{4,5},{5,4},{6,7},{7,6},{8,9},{9,8},{10,11... | collective-permute-start | bytes 7077896 | tf_op jit(solution)/shard_map/ppermute | solution.py:961
  163.7 21.1 %collective-permute-start.10 = (bf16[256,768]{1,0:T(8,128)(2,1)}, bf16[256,768]{1,0:T(8,128)(2,1)}, u32[]{:S(2)}, u32[]{:S(2)}) collective-permute-start(bf16[256,768]{1,0:T(8,128)(2,1)} %get-tuple-element.289), channel_id=1, source_target_pairs={{0,1},{1,0},{2,3},{3,2},{4,5},{5,4},{6,7},{7,6},{8,9},{9,8},{10,11... | collective-permute-start | bytes 1179656 | tf_op jit(solution)/shard_map/ppermute | solution.py:961
  163.7 21.1 %collective-permute-start.11 = (bf16[256,768]{1,0:T(8,128)(2,1)}, bf16[256,768]{1,0:T(8,128)(2,1)}, u32[]{:S(2)}, u32[]{:S(2)}) collective-permute-start(bf16[256,768]{1,0:T(8,128)(2,1)} %get-tuple-element.288), channel_id=1, source_target_pairs={{0,2},{1,3},{2,0},{3,1},{4,6},{5,7},{6,4},{7,5},{8,10},{9,11},{10,... | collective-permute-start | bytes 1179656 | tf_op jit(solution)/shard_map/ppermute | solution.py:961
  164.2 20.6 %collective-permute-start.12 = (bf16[256,768]{1,0:T(8,128)(2,1)}, bf16[256,768]{1,0:T(8,128)(2,1)}, u32[]{:S(2)}, u32[]{:S(2)}) collective-permute-start(bf16[256,768]{1,0:T(8,128)(2,1)} %get-tuple-element.287), channel_id=1, source_target_pairs={{0,3},{1,2},{2,1},{3,0},{4,7},{5,6},{6,5},{7,4},{8,11},{9,10},{10,... | collective-permute-start | bytes 1179656 | tf_op jit(solution)/shard_map/ppermute | solution.py:961
  189.9 28.7 %collective-permute-start.20 = (bf16[256,384]{1,0:T(8,128)(2,1)S(1)}, bf16[256,384]{1,0:T(8,128)(2,1)S(1)}, u32[]{:S(2)}, u32[]{:S(2)}) collective-permute-start(bf16[256,384]{1,0:T(8,128)(2,1)S(1)} %get-tuple-element.300), channel_id=1, source_target_pairs={{0,1},{1,0},{2,3},{3,2},{4,5},{5,4},{6,7},{7,6},{8,9},{9,8},{10,11... | collective-permute-start | bytes 589832 | tf_op jit(solution)/shard_map/ppermute | solution.py:961
  190.0 29.3 %collective-permute-start.21 = (bf16[256,384]{1,0:T(8,128)(2,1)S(1)}, bf16[256,384]{1,0:T(8,128)(2,1)S(1)}, u32[]{:S(2)}, u32[]{:S(2)}) collective-permute-start(bf16[256,384]{1,0:T(8,128)(2,1)S(1)} %get-tuple-element.299), channel_id=1, source_target_pairs={{0,2},{1,3},{2,0},{3,1},{4,6},{5,7},{6,4},{7,5},{8,10},{9,11},{10,... | collective-permute-start | bytes 589832 | tf_op jit(solution)/shard_map/ppermute | solution.py:961
  190.6 29.4 %collective-permute-start.22 = (bf16[256,384]{1,0:T(8,128)(2,1)S(1)}, bf16[256,384]{1,0:T(8,128)(2,1)S(1)}, u32[]{:S(2)}, u32[]{:S(2)}) collective-permute-start(bf16[256,384]{1,0:T(8,128)(2,1)S(1)} %get-tuple-element.298), channel_id=1, source_target_pairs={{0,3},{1,2},{2,1},{3,0},{4,7},{5,6},{6,5},{7,4},{8,11},{9,10},{10,... | collective-permute-start | bytes 589832 | tf_op jit(solution)/shard_map/ppermute | solution.py:961
  223.0 127.1 %reduce-scatter.3.cloned.1.call-start = ((), (), s32[]{:S(2)}) async-start(), calls=%async_computation.10 | async-start | bytes 10321920 | tf_op jit(solution)/shard_map/reduce_scatter | solution.py:1267
  257.3 37.6 %all-to-all-start.2 = ((bf16[8,128,256]{2,1,0:T(8,128)(2,1)}), bf16[8,128,256]{2,1,0:T(8,128)(2,1)S(1)}, u32[]{:S(2)}, u32[]{:S(2)}) async-start(bf16[8,128,256]{2,1,0:T(8,128)(2,1)} %copy-done.31), calls=%async_computation.2 | async-start | bytes 1048576 | tf_op jit(solution)/shard_map/all_to_all | solution.py:1459
  263.1 122.6 %all-gather.18.cloned.1.call-start = ((), (), s32[]{:S(2)}) async-start(), calls=%async_computation.12 | async-start | bytes 1966080 | tf_op jit(solution)/shard_map/all_gather | solution.py:1289
  285.8 32.6 %collective-permute-start.27 = (bf16[3,192,768]{2,1,0:T(8,128)(2,1)}, bf16[3,192,768]{2,1,0:T(8,128)(2,1)}, u32[]{:S(2)}, u32[]{:S(2)}) collective-permute-start(bf16[3,192,768]{2,1,0:T(8,128)(2,1)} %get-tuple-element.164), channel_id=1, source_target_pairs={{0,4},{4,0},{8,12},{12,8},{16,20},{20,16},{24,28},{28,24},{1,5},{5... | collective-permute-start | bytes 2654216 | tf_op jit(solution)/shard_map/ppermute | solution.py:961
  294.2 30.7 %collective-permute-start.26 = (bf16[3,192,768]{2,1,0:T(8,128)(2,1)}, bf16[3,192,768]{2,1,0:T(8,128)(2,1)}, u32[]{:S(2)}, u32[]{:S(2)}) collective-permute-start(bf16[3,192,768]{2,1,0:T(8,128)(2,1)} %get-tuple-element.165), channel_id=1, source_target_pairs={{0,4},{4,0},{8,12},{12,8},{16,20},{20,16},{24,28},{28,24},{1,5},{5... | collective-permute-start | bytes 2654216 | tf_op jit(solution)/shard_map/ppermute | solution.py:961
  294.8 118.5 %reduce-scatter.5.cloned.1.call-start = ((), (), s32[]{:S(2)}) async-start(), calls=%async_computation.11 | async-start | bytes 4423680 | tf_op jit(solution)/shard_map/reduce_scatter | solution.py:1267
  321.5 13.7 %collective-permute-start.29 = (bf16[3,96,768]{2,1,0:T(8,128)(2,1)}, bf16[3,96,768]{2,1,0:T(8,128)(2,1)S(1)}, u32[]{:S(2)}, u32[]{:S(2)}) collective-permute-start(bf16[3,96,768]{2,1,0:T(8,128)(2,1)} %constant_dynamic-slice_fusion.12), channel_id=1, source_target_pairs={{0,8},{4,12},{8,0},{12,4},{16,24},{20,28},{24,16},{28,20},{1,9},{5... | collective-permute-start | bytes 1327112 | tf_op jit(solution)/shard_map/ppermute | solution.py:961
  327.3 20.2 %collective-permute-start.28 = (bf16[3,96,768]{2,1,0:T(8,128)(2,1)}, bf16[3,96,768]{2,1,0:T(8,128)(2,1)}, u32[]{:S(2)}, u32[]{:S(2)}) collective-permute-start(bf16[3,96,768]{2,1,0:T(8,128)(2,1)} %constant_dynamic-slice_fusion.11), channel_id=1, source_target_pairs={{0,16},{4,20},{8,24},{12,28},{16,0},{20,4},{24,8},{28,12},{1,17},{... | collective-permute-start | bytes 1327112 | tf_op jit(solution)/shard_map/ppermute | solution.py:961
  357.2 20.9 %collective-permute-start.25 = (bf16[2,2,1,128,768]{4,3,2,1,0:T(8,128)(2,1)}, bf16[2,2,1,128,768]{4,3,2,1,0:T(8,128)(2,1)}, u32[]{:S(2)}, u32[]{:S(2)}) collective-permute-start(bf16[2,2,1,128,768]{4,3,2,1,0:T(8,128)(2,1)} %constant_dynamic-slice_fusion.13), channel_id=1, source_target_pairs={{0,4},{4,0},{8,12},{12,8},{16,20},{20,16},{24,28},{28,24},{1,5},{5... | collective-permute-start | bytes 2359304 | tf_op jit(solution)/shard_map/ppermute | solution.py:961
  358.5 21.9 %collective-permute-start.32 = (bf16[3,48,768]{2,1,0:T(8,128)(2,1)S(1)}, bf16[3,48,768]{2,1,0:T(8,128)(2,1)S(1)}, u32[]{:S(2)}, u32[]{:S(2)}) collective-permute-start(bf16[3,48,768]{2,1,0:T(8,128)(2,1)S(1)} %constant_dynamic-slice_fusion.10), channel_id=1, source_target_pairs={{0,16},{4,20},{8,24},{12,28},{16,0},{20,4},{24,8},{28,12},{1,17},{... | collective-permute-start | bytes 663560 | tf_op jit(solution)/shard_map/ppermute | solution.py:961
  358.5 26.3 %collective-permute-start.31 = (bf16[3,48,768]{2,1,0:T(8,128)(2,1)}, bf16[3,48,768]{2,1,0:T(8,128)(2,1)S(1)}, u32[]{:S(2)}, u32[]{:S(2)}) collective-permute-start(bf16[3,48,768]{2,1,0:T(8,128)(2,1)} %constant_dynamic-slice_fusion.9), channel_id=1, source_target_pairs={{0,8},{4,12},{8,0},{12,4},{16,24},{20,28},{24,16},{28,20},{1,9},{5... | collective-permute-start | bytes 663560 | tf_op jit(solution)/shard_map/ppermute | solution.py:961
  362.2 38.0 %collective-permute-start.37 = (bf16[96,5376]{1,0:T(8,128)(2,1)}, bf16[96,5376]{1,0:T(8,128)(2,1)}, u32[]{:S(2)}, u32[]{:S(2)}) collective-permute-start(bf16[96,5376]{1,0:T(8,128)(2,1)} %constant_dynamic-slice_fusion.8), channel_id=1, source_target_pairs={{0,4},{4,0},{8,12},{12,8},{16,20},{20,16},{24,28},{28,24},{1,5},{5... | collective-permute-start | bytes 3096584 | tf_op jit(solution)/shard_map/ppermute | solution.py:961
  380.3 12.0 %collective-permute-start.30 = (bf16[2,1,128,768]{3,2,0,1:T(8,128)(2,1)}, bf16[2,1,128,768]{3,2,0,1:T(8,128)(2,1)}, u32[]{:S(2)}, u32[]{:S(2)}) collective-permute-start(bf16[2,1,128,768]{3,2,0,1:T(8,128)(2,1)} %dynamic-slice_bitcast_fusion), channel_id=1, source_target_pairs={{0,8},{4,12},{8,0},{12,4},{16,24},{20,28},{24,16},{28,20},{1,9},{5... | collective-permute-start | bytes 1179656 | tf_op jit(solution)/shard_map/ppermute | solution.py:961
  381.4 21.2 %collective-permute-start.36 = (bf16[1,3,48,768]{3,2,1,0:T(8,128)(2,1)S(1)}, bf16[1,3,48,768]{3,2,1,0:T(8,128)(2,1)}, u32[]{:S(2)}, u32[]{:S(2)}) collective-permute-start(bf16[1,3,48,768]{3,2,1,0:T(8,128)(2,1)S(1)} %fusion.38), channel_id=1, source_target_pairs={{0,16},{4,20},{8,24},{12,28},{16,0},{20,4},{24,8},{28,12},{1,17},{... | collective-permute-start | bytes 663560 | tf_op jit(solution)/shard_map/ppermute | solution.py:961
  385.5 20.7 %collective-permute-start.35 = (bf16[1,3,48,768]{3,2,1,0:T(8,128)(2,1)}, bf16[1,3,48,768]{3,2,1,0:T(8,128)(2,1)}, u32[]{:S(2)}, u32[]{:S(2)}) collective-permute-start(bf16[1,3,48,768]{3,2,1,0:T(8,128)(2,1)} %fusion.39), channel_id=1, source_target_pairs={{0,8},{4,12},{8,0},{12,4},{16,24},{20,28},{24,16},{28,20},{1,9},{5... | collective-permute-start | bytes 663560 | tf_op jit(solution)/shard_map/ppermute | solution.py:961
  390.2 19.4 %collective-permute-start.34 = (bf16[384,768]{1,0:T(8,128)(2,1)S(1)}, bf16[384,768]{1,0:T(8,128)(2,1)S(1)}, u32[]{:S(2)}, u32[]{:S(2)}) collective-permute-start(bf16[384,768]{1,0:T(8,128)(2,1)S(1)} %get-tuple-element.183), channel_id=1, source_target_pairs={{0,4},{4,0},{8,12},{12,8},{16,20},{20,16},{24,28},{28,24},{1,5},{5... | collective-permute-start | bytes 1769480 | tf_op jit(solution)/shard_map/ppermute | solution.py:961
  402.5 25.8 %collective-permute-start.43 = (bf16[48,5376]{1,0:T(8,128)(2,1)}, bf16[48,5376]{1,0:T(8,128)(2,1)}, u32[]{:S(2)}, u32[]{:S(2)}) collective-permute-start(bf16[48,5376]{1,0:T(8,128)(2,1)} %constant_dynamic-slice_fusion.6), channel_id=1, source_target_pairs={{0,8},{4,12},{8,0},{12,4},{16,24},{20,28},{24,16},{28,20},{1,9},{5... | collective-permute-start | bytes 1548296 | tf_op jit(solution)/shard_map/ppermute | solution.py:961
  404.3 31.2 %collective-permute-start.42 = (bf16[2,3,48,768]{3,2,1,0:T(8,128)(2,1)}, bf16[2,3,48,768]{3,2,1,0:T(8,128)(2,1)}, u32[]{:S(2)}, u32[]{:S(2)}) collective-permute-start(bf16[2,3,48,768]{3,2,1,0:T(8,128)(2,1)} %pad_maximum_fusion.27), channel_id=1, source_target_pairs={{0,8},{4,12},{8,0},{12,4},{16,24},{20,28},{24,16},{28,20},{1,9},{5... | collective-permute-start | bytes 1327112 | tf_op jit(solution)/shard_map/ppermute | solution.py:961
  408.1 29.5 %collective-permute-start.41 = (bf16[2,3,48,768]{3,2,1,0:T(8,128)(2,1)}, bf16[2,3,48,768]{3,2,1,0:T(8,128)(2,1)S(1)}, u32[]{:S(2)}, u32[]{:S(2)}) collective-permute-start(bf16[2,3,48,768]{3,2,1,0:T(8,128)(2,1)} %pad_maximum_fusion.28), channel_id=1, source_target_pairs={{0,16},{4,20},{8,24},{12,28},{16,0},{20,4},{24,8},{28,12},{1,17},{... | collective-permute-start | bytes 1327112 | tf_op jit(solution)/shard_map/ppermute | solution.py:961
  411.3 29.2 %collective-permute-start.40 = (bf16[192,768]{1,0:T(8,128)(2,1)}, bf16[192,768]{1,0:T(8,128)(2,1)}, u32[]{:S(2)}, u32[]{:S(2)}) collective-permute-start(bf16[192,768]{1,0:T(8,128)(2,1)} %constant_dynamic-slice_fusion.5), channel_id=1, source_target_pairs={{0,8},{4,12},{8,0},{12,4},{16,24},{20,28},{24,16},{28,20},{1,9},{5... | collective-permute-start | bytes 884744 | tf_op jit(solution)/shard_map/ppermute | solution.py:961
  415.4 27.5 %collective-permute-start.39 = (bf16[96,1664]{1,0:T(8,128)(2,1)S(1)}, bf16[96,1664]{1,0:T(8,128)(2,1)S(1)}, u32[]{:S(2)}, u32[]{:S(2)}) collective-permute-start(bf16[96,1664]{1,0:T(8,128)(2,1)S(1)} %constant_dynamic-slice_fusion.4), channel_id=1, source_target_pairs={{0,4},{4,0},{8,12},{12,8},{16,20},{20,16},{24,28},{28,24},{1,5},{5... | collective-permute-start | bytes 958472 | tf_op jit(solution)/shard_map/ppermute | solution.py:961
  428.3 23.3 %collective-permute-start.38 = (bf16[192,576]{1,0:T(8,128)(2,1)S(1)}, bf16[192,576]{1,0:T(8,128)(2,1)S(1)}, u32[]{:S(2)}, u32[]{:S(2)}) collective-permute-start(bf16[192,576]{1,0:T(8,128)(2,1)S(1)} %slice.205), channel_id=1, source_target_pairs={{0,16},{4,20},{8,24},{12,28},{16,0},{20,4},{24,8},{28,12},{1,17},{... | collective-permute-start | bytes 663560 | tf_op jit(solution)/shard_map/ppermute | solution.py:961
  435.6 21.4 %collective-permute-start.47 = (bf16[24,5376]{1,0:T(8,128)(2,1)S(1)}, bf16[24,5376]{1,0:T(8,128)(2,1)S(1)}, u32[]{:S(2)}, u32[]{:S(2)}) collective-permute-start(bf16[24,5376]{1,0:T(8,128)(2,1)S(1)} %constant_dynamic-slice_fusion.3), channel_id=1, source_target_pairs={{0,16},{4,20},{8,24},{12,28},{16,0},{20,4},{24,8},{28,12},{1,17},{... | collective-permute-start | bytes 774152 | tf_op jit(solution)/shard_map/ppermute | solution.py:961
  437.7 54.0 %collective-permute-start.54 = (bf16[4,3,48,768]{3,2,1,0:T(8,128)(2,1)S(1)}, bf16[4,3,48,768]{3,2,1,0:T(8,128)(2,1)S(1)}, u32[]{:S(2)}, u32[]{:S(2)}) collective-permute-start(bf16[4,3,48,768]{3,2,1,0:T(8,128)(2,1)S(1)} %pad_maximum_fusion.12), channel_id=1, source_target_pairs={{0,4},{4,0},{8,12},{12,8},{16,20},{20,16},{24,28},{28,24},{1,5},{5... | collective-permute-start | bytes 2654216 | tf_op jit(solution)/shard_map/ppermute | solution.py:961
  440.4 52.6 %collective-permute-start.53 = (bf16[4,3,48,768]{3,2,1,0:T(8,128)(2,1)S(1)}, bf16[4,3,48,768]{3,2,1,0:T(8,128)(2,1)S(1)}, u32[]{:S(2)}, u32[]{:S(2)}) collective-permute-start(bf16[4,3,48,768]{3,2,1,0:T(8,128)(2,1)S(1)} %pad_maximum_fusion.13), channel_id=1, source_target_pairs={{0,4},{4,0},{8,12},{12,8},{16,20},{20,16},{24,28},{28,24},{1,5},{5... | collective-permute-start | bytes 2654216 | tf_op jit(solution)/shard_map/ppermute | solution.py:961
  443.0 24.5 %collective-permute-start.46 = (bf16[96,768]{1,0:T(8,128)(2,1)S(1)}, bf16[96,768]{1,0:T(8,128)(2,1)S(1)}, u32[]{:S(2)}, u32[]{:S(2)}) collective-permute-start(bf16[96,768]{1,0:T(8,128)(2,1)S(1)} %constant_dynamic-slice_fusion.2), channel_id=1, source_target_pairs={{0,16},{4,20},{8,24},{12,28},{16,0},{20,4},{24,8},{28,12},{1,17},{... | collective-permute-start | bytes 442376 | tf_op jit(solution)/shard_map/ppermute | solution.py:961
  451.6 15.9 %collective-permute-start.45 = (bf16[48,1664]{1,0:T(8,128)(2,1)S(1)}, bf16[48,1664]{1,0:T(8,128)(2,1)S(1)}, u32[]{:S(2)}, u32[]{:S(2)}) collective-permute-start(bf16[48,1664]{1,0:T(8,128)(2,1)S(1)} %constant_dynamic-slice_fusion.1), channel_id=1, source_target_pairs={{0,8},{4,12},{8,0},{12,4},{16,24},{20,28},{24,16},{28,20},{1,9},{5... | collective-permute-start | bytes 479240 | tf_op jit(solution)/shard_map/ppermute | solution.py:961
  457.0 17.0 %collective-permute-start.44 = (bf16[1,192,576]{2,1,0:T(8,128)(2,1)S(1)}, bf16[1,192,576]{2,1,0:T(8,128)(2,1)S(1)}, u32[]{:S(2)}, u32[]{:S(2)}) collective-permute-start(bf16[1,192,576]{2,1,0:T(8,128)(2,1)S(1)} %fusion.37), channel_id=1, source_target_pairs={{0,4},{4,0},{8,12},{12,8},{16,20},{20,16},{24,28},{28,24},{1,5},{5... | collective-permute-start | bytes 663560 | tf_op jit(solution)/shard_map/ppermute | solution.py:961
  476.1 15.4 %collective-permute-start.48 = (bf16[2,192,576]{2,1,0:T(8,128)(2,1)S(1)}, bf16[2,192,576]{2,1,0:T(8,128)(2,1)S(1)}, u32[]{:S(2)}, u32[]{:S(2)}) collective-permute-start(bf16[2,192,576]{2,1,0:T(8,128)(2,1)S(1)} %pad_maximum_fusion.25), channel_id=1, source_target_pairs={{0,8},{4,12},{8,0},{12,4},{16,24},{20,28},{24,16},{28,20},{1,9},{5... | collective-permute-start | bytes 1327112 | tf_op jit(solution)/shard_map/ppermute | solution.py:961
  477.7 24.1 %collective-permute-start.52 = (bf16[2,24,5376]{2,1,0:T(8,128)(2,1)S(1)}, bf16[2,24,5376]{2,1,0:T(8,128)(2,1)S(1)}, u32[]{:S(2)}, u32[]{:S(2)}) collective-permute-start(bf16[2,24,5376]{2,1,0:T(8,128)(2,1)S(1)} %pad_maximum_fusion.24), channel_id=1, source_target_pairs={{0,8},{4,12},{8,0},{12,4},{16,24},{20,28},{24,16},{28,20},{1,9},{5... | collective-permute-start | bytes 1548296 | tf_op jit(solution)/shard_map/ppermute | solution.py:961
  480.1 25.3 %collective-permute-start.56 = (bf16[1,24,1664]{2,1,0:T(8,128)(2,1)S(1)}, bf16[1,24,1664]{2,1,0:T(8,128)(2,1)S(1)}, u32[]{:S(2)}, u32[]{:S(2)}) collective-permute-start(bf16[1,24,1664]{2,1,0:T(8,128)(2,1)S(1)} %fusion.41), channel_id=1, source_target_pairs={{0,16},{4,20},{8,24},{12,28},{16,0},{20,4},{24,8},{28,12},{1,17},{... | collective-permute-start | bytes 239624 | tf_op jit(solution)/shard_map/ppermute | solution.py:961
  501.9 25.8 %collective-permute-start.55 = (bf16[4,24,5376]{2,1,0:T(8,128)(2,1)S(1)}, bf16[4,24,5376]{2,1,0:T(8,128)(2,1)S(1)}, u32[]{:S(2)}, u32[]{:S(2)}) collective-permute-start(bf16[4,24,5376]{2,1,0:T(8,128)(2,1)S(1)} %pad_maximum_fusion.9), channel_id=1, source_target_pairs={{0,4},{4,0},{8,12},{12,8},{16,20},{20,16},{24,28},{28,24},{1,5},{5... | collective-permute-start | bytes 3096584 | tf_op jit(solution)/shard_map/ppermute | solution.py:961
  502.9 18.7 %collective-permute-start.58 = (bf16[2,96,768]{2,1,0:T(8,128)(2,1)S(1)}, bf16[2,96,768]{2,1,0:T(8,128)(2,1)S(1)}, u32[]{:S(2)}, u32[]{:S(2)}) collective-permute-start(bf16[2,96,768]{2,1,0:T(8,128)(2,1)S(1)} %pad_maximum_fusion.31), channel_id=1, source_target_pairs={{0,8},{4,12},{8,0},{12,4},{16,24},{20,28},{24,16},{28,20},{1,9},{5... | collective-permute-start | bytes 884744 | tf_op jit(solution)/shard_map/ppermute | solution.py:961
  505.4 18.0 %collective-permute-start.57 = (bf16[2,24,1664]{2,1,0:T(8,128)(2,1)S(1)}, bf16[2,24,1664]{2,1,0:T(8,128)(2,1)S(1)}, u32[]{:S(2)}, u32[]{:S(2)}) collective-permute-start(bf16[2,24,1664]{2,1,0:T(8,128)(2,1)S(1)} %pad_maximum_fusion.34), channel_id=1, source_target_pairs={{0,8},{4,12},{8,0},{12,4},{16,24},{20,28},{24,16},{28,20},{1,9},{5... | collective-permute-start | bytes 479240 | tf_op jit(solution)/shard_map/ppermute | solution.py:961
  521.6 18.7 %collective-permute-start.60 = (bf16[4,96,768]{2,1,0:T(8,128)(2,1)S(1)}, bf16[4,96,768]{2,1,0:T(8,128)(2,1)S(1)}, u32[]{:S(2)}, u32[]{:S(2)}) collective-permute-start(bf16[4,96,768]{2,1,0:T(8,128)(2,1)S(1)} %pad_maximum_fusion.23), channel_id=1, source_target_pairs={{0,4},{4,0},{8,12},{12,8},{16,20},{20,16},{24,28},{28,24},{1,5},{5... | collective-permute-start | bytes 1769480 | tf_op jit(solution)/shard_map/ppermute | solution.py:961
  523.4 24.7 %collective-permute-start.59 = (bf16[4,24,1664]{2,1,0:T(8,128)(2,1)S(1)}, bf16[4,24,1664]{2,1,0:T(8,128)(2,1)S(1)}, u32[]{:S(2)}, u32[]{:S(2)}) collective-permute-start(bf16[4,24,1664]{2,1,0:T(8,128)(2,1)S(1)} %pad_maximum_fusion.29), channel_id=1, source_target_pairs={{0,4},{4,0},{8,12},{12,8},{16,20},{20,16},{24,28},{28,24},{1,5},{5... | collective-permute-start | bytes 958472 | tf_op jit(solution)/shard_map/ppermute | solution.py:961
  (150 other events, 823.9 us)
Sparse Core Ops, SparseCore 0:
  16.2 30.9 all-gather.7
  48.8 21.8 all-gather.9
  72.2 38.8 all-gather.11
  112.6 37.4 all-gather.13
  223.1 29.7 all-gather.15
  257.4 71.2 reduce-scatter.2
  330.8 19.6 all-gather.17
  357.4 40.3 reduce-scatter.4

commit v3 on v2

--- a/solution.py
+++ b/solution.py
@@ -13,7 +13,7 @@
 EPSILON = 1e-05
 BLOCK_LIMIT = 1024
 FAR = 1e9
-VMEM_BYTES = 40 * 1024 * 1024
+VMEM_BYTES = 32 * 1024 * 1024
 
 F32 = jnp.float32
 BF16 = jnp.bfloat16
@@ -1071,7 +1071,7 @@
     final = max(i for i, name in enumerate(ORDER[:-2]) if name == "G")
     for event, name in enumerate(ORDER):
         others = last
-        if event == final or event == len(ORDER) - 1:
+        if event == final or event >= len(ORDER) - 2:
             ready = [done[other] for other in "ABKDT" if other in done]
             others = others + tuple(jax.tree.leaves(ready))
         step = chains[name].advance if name in chains else begin[name]

time: 570 us -> 567 us (level)
  transfers between devices with their start and end apart: 72 -> 72, of which waited for: 26 -> 27; matrix products, arithmetic and copies ran while one was open for 21% -> 21% of each run, Pallas kernels for 18% -> 18%
where the time goes in v3:
time: 567 us; the launch traced here: 559 us
  waiting for transfers between devices  146 us (26%)
  starting transfers between devices  107 us (19%)
  Pallas kernels  102 us (18%)
  local copies, waits for them, and re-layouts  101 us (18%)
  other arithmetic  58.1 us (10%)
  matrix products  28.1 us (5%)
  between operations  16.6 us (3%)
    ppermute x57, waiting for transfers between devices, flip(): lax.ppermute(value, axis, [(i, i ^ bit) for i in range(lax.axis_size(axis...  133 us
    ppermute x57, starting transfers between devices, flip(): lax.ppermute(value, axis, [(i, i ^ bit) for i in range(lax.axis_size(axis...  68.5 us
    unnamed x292, local copies, waits for them, and re-layouts  62.1 us
    dot_general x8, matrix products, matmul_nt(): lax.dot_general(left, right, (((1,), (1,)), ((), ())), preferred_element_...  16.4 us
    pallas_call x1, Pallas kernels, attend_back(): pl.pallas_call(functools.partial(attend_back_kernel, heads, tokens), grid...  16.4 us
    pallas_call x2, Pallas kernels, finish(): pl.pallas_call(functools.partial(place_kernel, spans, self.order), in_spe...  15.2 us
    concatenate x6, other arithmetic, take(): jnp.concatenate([self.base, got], axis=0)  13.1 us
    convert_element_type x12, other arithmetic, advance(): piece = (self.keep.astype(F32) + got).astype(BF16)  12.3 us
  transfers between devices with their start and end apart: 72, of which 27 were waited for; matrix products, arithmetic and copies ran while one was open for 21% of the time, Pallas kernels for 18%

profile of v3, /device:TPU:0, one launch (start us, length us, event | category | flops | bytes accessed | tf_op | source)
XLA Modules:
  0.0 558.6 jit_solution(6529815046506685066)
XLA Ops:
  20.1 2.5 collective-permute-start.1
  23.9 5.8 %all-to-all-start = ((bf16[8,136,768]{2,1,0:T(8,128)(2,1)}), bf16[8,136,768]{2,1,0:T(8,128)(2,1)S(1)}, u32[]{:S(2)}, u32[]{:S(2)}) async-start(bf16[8,136,768]{2,1,0:T(8,128)(2,1)} %bitcast.2), calls=%async_computation | async-start | bytes 3342336 | tf_op jit(solution)/shard_map/all_to_all | solution.py:1352
  30.3 4.7 fusion.50
  51.7 2.9 collective-permute-start.14
  57.7 2.7 gru_forward.1
  65.6 2.4 collective-permute-start.6
  68.0 8.6 %all-to-all-done.tok_ref = bf16[8,136,768]{2,1,0:T(8,128)(2,1)S(1)} async-done(((bf16[8,136,768]{2,1,0:T(8,128)(2,1)}), bf16[8,136,768]{2,1,0:T(8,128)(2,1)S(1)}, u32[]{:S(2)}, u32[]{:S(2)}) %all-to-all-start) | async-done | bytes 1671200 | tf_op jit(solution)/shard_map/all_to_all | solution.py:1352
  76.6 9.3 %attend.1 = (bf16[1024,256]{1,0:T(8,128)(2,1)S(1)}, f32[1024,384]{1,0:T(8,128)S(1)}, bf16[3,1024,128]{2,1,0:T(8,128)(2,1)S(1)}, bf16[3,1024,128]{2,1,0:T(8,128)(...) custom-call(bf16[8,136,768]{2,1,0:T(8,128)(2,1)S(1)} %all-to-all-done.tok_ref, ...), custom_call_target="tpu_custom_call" | custom-call | flops 1 | bytes 1 | tf_op jit(solution)/shard_map/attend/pallas_call | solution.py:501
  91.5 4.1 all-to-all-start.1
  101.5 2.4 collective-permute-start.7
  109.6 2.8 place_own.2
  119.8 8.3 %collective-permute-done.15 = bf16[2,96,1536]{2,1,0:T(8,128)(2,1)} collective-permute-done((bf16[2,96,1536]{2,1,0:T(8,128)(2,1)}, bf16[2,96,1536]{2,1,0:T(8,128)(2,1)}, u32[]{:S(2)}, u32[]{:S(2)}) %collective-permute-start.15) | collective-permute-done | bytes 589856 | tf_op jit(solution)/shard_map/ppermute | solution.py:961
  128.1 2.4 pad_maximum_fusion.7
  137.7 2.5 copy-done.13
  140.2 5.4 feed_forward.1
  145.6 11.6 %collective-permute-done.16 = bf16[4,96,1536]{2,1,0:T(8,128)(2,1)} collective-permute-done((bf16[4,96,1536]{2,1,0:T(8,128)(2,1)}, bf16[4,96,1536]{2,1,0:T(8,128)(2,1)}, u32[]{:S(2)}, u32[]{:S(2)}) %collective-permute-start.16) | collective-permute-done | bytes 1179680 | tf_op jit(solution)/shard_map/ppermute | solution.py:961
  158.8 3.2 pad_maximum_fusion.1.piece_ref
  165.6 4.6 fusion.57
  170.7 2.5 copy-done.15
  173.2 7.6 %place.2 = (bf16[4,384,1536]{2,1,0:T(8,128)(2,1)S(1)}, bf16[4,192,1536]{2,1,0:T(8,128)(2,1)S(1)}) custom-call(bf16[8,72,1536]{2,1,0:T(8,128)(2,1)S(1)} %pad_maximum_fusion.4.piece_ref, bf16[8,72,1536]{2,1,0:T(8,128)(2,1)} %collective-permute-done.9.core_ref, bf16[4,384,1536]{2,1,0:T(8,128)(2,1)S(1)} %copy-done.15, ...), custom_call_target="tpu_custom_call", output_to_operand_aliasing={{0}: (2, {}), {1}: (3, {})} | custom-call | flops 1 | bytes 1 | tf_op jit(solution)/shard_map/place/pallas_call | solution.py:1252
  184.9 3.1 collective-permute-start.18
  196.2 7.6 %place.3 = (bf16[4,384,1536]{2,1,0:T(8,128)(2,1)S(1)}, bf16[4,384,1536]{2,1,0:T(8,128)(2,1)S(1)}) custom-call(bf16[8,96,1536]{2,1,0:T(8,128)(2,1)} %pad_maximum_fusion.1.piece_ref, bf16[8,96,1536]{2,1,0:T(8,128)(2,1)} %collective-permute-done.17.core_ref, bf16[4,384,1536]{2,1,0:T(8,128)(2,1)S(1)} %bitcast.165, ...), custom_call_target="tpu_custom_call", output_to_operand_aliasing={{0}: (2, {}), {1}: (3, {})} | custom-call | flops 1 | bytes 1 | tf_op jit(solution)/shard_map/place/pallas_call | solution.py:1252
  214.0 4.5 collective-permute-start.24
  224.9 3.9 fusion.60
  233.5 2.2 gru_back.1
  238.7 5.1 fusion.51
  243.9 2.2 multiply_reduce_fusion.1
  249.4 4.5 gradients.1
  254.0 3.3 copy-done
  257.3 5.8 %all-to-all-start.2 = ((bf16[8,128,256]{2,1,0:T(8,128)(2,1)}), bf16[8,128,256]{2,1,0:T(8,128)(2,1)S(1)}, u32[]{:S(2)}, u32[]{:S(2)}) async-start(bf16[8,128,256]{2,1,0:T(8,128)(2,1)} %copy-done.31), calls=%async_computation.2 | async-start | bytes 1048576 | tf_op jit(solution)/shard_map/all_to_all | solution.py:1459
  263.1 11.2 %all-gather.18.cloned.1.call-start = ((), (), s32[]{:S(2)}) async-start(), calls=%async_computation.12 | async-start | bytes 1966080 | tf_op jit(solution)/shard_map/all_gather | solution.py:1289
  279.1 5.8 %conv_gradient.2 = (bf16[3,192,768]{2,1,0:T(8,128)(2,1)S(1)}, bf16[3,192,768]{2,1,0:T(8,128)(2,1)}) custom-call(bf16[256,384]{1,0:T(8,128)(2,1)S(1)} %get-tuple-element.163.own_ref, bf16[256,384]{1,0:T(8,128)(2,1)S(1)} %copy-done.68, bf16[256,384]{1,0:T(8,128)(2,1)S(1)} %copy-done.70, bf16[256,384]{1,0:T(8,128)(2,1)S(1)} %copy-done.72, ...), custom_call_target="tpu_custom_call" | custom-call | flops 1 | bytes 1 | tf_op jit(solution)/shard_map/conv_gradient/pallas_call | solution.py:777
  287.5 5.8 %conv_gradient.3 = (bf16[3,192,768]{2,1,0:T(8,128)(2,1)S(1)}, bf16[3,192,768]{2,1,0:T(8,128)(2,1)}) custom-call(bf16[256,384]{1,0:T(8,128)(2,1)S(1)} %get-tuple-element.163.own_ref, bf16[256,384]{1,0:T(8,128)(2,1)S(1)} %copy-done.68, bf16[256,384]{1,0:T(8,128)(2,1)S(1)} %copy-done.70, bf16[256,384]{1,0:T(8,128)(2,1)S(1)} %copy-done.72, ...), custom_call_target="tpu_custom_call" | custom-call | flops 1 | bytes 1 | tf_op jit(solution)/shard_map/conv_gradient/pallas_call | solution.py:777
  302.0 16.4 %attend_back.1 = (bf16[1024,768]{1,0:T(8,128)(2,1)S(1)}, f32[768,576]{1,0:T(8,128)S(1)}, f32[2,1,768]{2,1,0:T(1,128)S(1)}) custom-call(bf16[8,136,768]{2,1,0:T(8,128)(2,1)S(1)} %all-to-all-done.tok_ref, bf16[768,576]{1,0:T(8,128)(2,1)S(1)} %copy-done.62, bf16[3,1024,128]{2,1,0:T(8,128)(2,1)S(1)} %copy-done.74, bf16[3,1024,128]{2,1,0:T(8,128)(2,1)S(1)} %copy-done.76, ...), custom_call_target="tpu_custom_call" | custom-call | flops 1 | bytes 1 | tf_op jit(solution)/shard_map/attend_back/pallas_call | solution.py:540
  318.4 2.2 add_convert_fusion.2
  327.2 2.3 collective-permute-start.28
  332.6 2.6 collective-permute-done.29
  337.1 10.2 %collective-permute-done.28 = bf16[3,96,768]{2,1,0:T(8,128)(2,1)} collective-permute-done((bf16[3,96,768]{2,1,0:T(8,128)(2,1)}, bf16[3,96,768]{2,1,0:T(8,128)(2,1)}, u32[]{:S(2)}, u32[]{:S(2)}) %collective-permute-start.28) | collective-permute-done | bytes 442400 | tf_op jit(solution)/shard_map/ppermute | solution.py:961
  349.9 2.2 constant_dynamic-slice_fusion.8
  353.7 3.3 last_gradients.1
  358.3 3.7 collective-permute-start.31
  362.6 15.3 %collective-permute-done.25 = bf16[2,2,1,128,768]{4,3,2,1,0:T(8,128)(2,1)} collective-permute-done((bf16[2,2,1,128,768]{4,3,2,1,0:T(8,128)(2,1)}, bf16[2,2,1,128,768]{4,3,2,1,0:T(8,128)(2,1)}, u32[]{:S(2)}, u32[]{:S(2)}) %collective-permute-start.25) | collective-permute-done | bytes 786464 | tf_op jit(solution)/shard_map/ppermute | solution.py:961
  381.3 3.3 collective-permute-start.36
  386.9 3.1 down_gradient.1
  394.0 6.1 %collective-permute-done.37 = bf16[96,5376]{1,0:T(8,128)(2,1)} collective-permute-done((bf16[96,5376]{1,0:T(8,128)(2,1)}, bf16[96,5376]{1,0:T(8,128)(2,1)}, u32[]{:S(2)}, u32[]{:S(2)}) %collective-permute-start.37) | collective-permute-done | bytes 1032224 | tf_op jit(solution)/shard_map/ppermute | solution.py:961
  416.8 11.4 %collective-permute-done.43 = bf16[48,5376]{1,0:T(8,128)(2,1)} collective-permute-done((bf16[48,5376]{1,0:T(8,128)(2,1)}, bf16[48,5376]{1,0:T(8,128)(2,1)}, u32[]{:S(2)}, u32[]{:S(2)}) %collective-permute-start.43) | collective-permute-done | bytes 516128 | tf_op jit(solution)/shard_map/ppermute | solution.py:961
  430.9 4.5 collective-permute-done.42
  442.8 5.3 collective-permute-start.46
  448.2 3.2 collective-permute-done.38
  451.5 5.4 collective-permute-done.47
  457.7 9.7 %collective-permute-done.46 = bf16[96,768]{1,0:T(8,128)(2,1)S(1)} collective-permute-done((bf16[96,768]{1,0:T(8,128)(2,1)S(1)}, bf16[96,768]{1,0:T(8,128)(2,1)S(1)}, u32[]{:S(2)}, u32[]{:S(2)}) %collective-permute-start.46) | collective-permute-done | bytes 147488 | tf_op jit(solution)/shard_map/ppermute | solution.py:961
  467.4 3.0 collective-permute-start.50
  470.5 3.2 collective-permute-done.44
  481.5 9.8 %collective-permute-done.48 = bf16[2,192,576]{2,1,0:T(8,128)(2,1)S(1)} collective-permute-done((bf16[2,192,576]{2,1,0:T(8,128)(2,1)S(1)}, bf16[2,192,576]{2,1,0:T(8,128)(2,1)S(1)}, u32[]{:S(2)}, u32[]{:S(2)}) %collective-permute-start.48) | collective-permute-done | bytes 442400 | tf_op jit(solution)/shard_map/ppermute | solution.py:961
  494.2 7.4 %collective-permute-done.52 = bf16[2,24,5376]{2,1,0:T(8,128)(2,1)S(1)} collective-permute-done((bf16[2,24,5376]{2,1,0:T(8,128)(2,1)S(1)}, bf16[2,24,5376]{2,1,0:T(8,128)(2,1)S(1)}, u32[]{:S(2)}, u32[]{:S(2)}) %collective-permute-start.52) | collective-permute-done | bytes 516128 | tf_op jit(solution)/shard_map/ppermute | solution.py:961
  502.6 2.5 collective-permute-start.58
  507.5 4.7 collective-permute-done.33
  512.2 3.9 settle_half.2.refs_0_
  517.5 3.9 settle_half.3
  523.6 3.9 collective-permute-done.55
  527.8 4.0 settle.3
  531.7 8.4 %collective-permute-done.60 = bf16[4,96,768]{2,1,0:T(8,128)(2,1)S(1)} collective-permute-done((bf16[4,96,768]{2,1,0:T(8,128)(2,1)S(1)}, bf16[4,96,768]{2,1,0:T(8,128)(2,1)S(1)}, u32[]{:S(2)}, u32[]{:S(2)}) %collective-permute-start.60) | collective-permute-done | bytes 589856 | tf_op jit(solution)/shard_map/ppermute | solution.py:961
  540.4 3.6 settle.4
  546.2 3.3 settle.5
  (595 shorter events, 209.0 us)
Async XLA Ops:
  7.2 47.5 %all-gather.8.cloned.1.call-start = ((), (), s32[]{:S(2)}) async-start(), calls=%async_computation.5 | async-start | bytes 3194880 | tf_op jit(solution)/shard_map/all_gather | solution.py:1289
  16.1 117.6 %all-gather.10.cloned.1.call-start = ((), (), s32[]{:S(2)}) async-start(), calls=%async_computation.6 | async-start | bytes 1474560 | tf_op jit(solution)/shard_map/all_gather | solution.py:1289
  16.8 120.9 %all-gather.12.cloned.1.call-start = ((), (), s32[]{:S(2)}) async-start(), calls=%async_computation.7 | async-start | bytes 5898240 | tf_op jit(solution)/shard_map/all_gather | solution.py:1289
  19.6 30.0 %collective-permute-start = (bf16[192,576]{1,0:T(8,128)(2,1)}, bf16[192,576]{1,0:T(8,128)(2,1)}, u32[]{:S(2)}, u32[]{:S(2)}) collective-permute-start(bf16[192,576]{1,0:T(8,128)(2,1)} %pad_maximum_fusion.32.own_ref), channel_id=1, source_target_pairs={{0,1},{1,0},{2,3},{3,2},{4,5},{5,4},{6,7},{7,6},{8,9},{9,8},{10,11... | collective-permute-start | bytes 663560 | tf_op jit(solution)/shard_map/ppermute | solution.py:961
  20.1 31.1 %collective-permute-start.1 = (bf16[192,576]{1,0:T(8,128)(2,1)}, bf16[192,576]{1,0:T(8,128)(2,1)}, u32[]{:S(2)}, u32[]{:S(2)}) collective-permute-start(bf16[192,576]{1,0:T(8,128)(2,1)} %pad_maximum_fusion.32.own_ref), channel_id=1, source_target_pairs={{0,2},{1,3},{2,0},{3,1},{4,6},{5,7},{6,4},{7,5},{8,10},{9,11},{10,... | collective-permute-start | bytes 663560 | tf_op jit(solution)/shard_map/ppermute | solution.py:961
  23.9 52.6 %all-to-all-start = ((bf16[8,136,768]{2,1,0:T(8,128)(2,1)}), bf16[8,136,768]{2,1,0:T(8,128)(2,1)S(1)}, u32[]{:S(2)}, u32[]{:S(2)}) async-start(bf16[8,136,768]{2,1,0:T(8,128)(2,1)} %bitcast.2), calls=%async_computation | async-start | bytes 3342336 | tf_op jit(solution)/shard_map/all_to_all | solution.py:1352
  29.7 135.9 %all-gather.14.cloned.1.call-start = ((), (), s32[]{:S(2)}) async-start(), calls=%async_computation.8 | async-start | bytes 5898240 | tf_op jit(solution)/shard_map/all_gather | solution.py:1289
  37.7 14.0 %collective-permute-start.13 = (bf16[96,1536]{1,0:T(8,128)(2,1)}, bf16[96,1536]{1,0:T(8,128)(2,1)}, u32[]{:S(2)}, u32[]{:S(2)}) collective-permute-start(bf16[96,1536]{1,0:T(8,128)(2,1)} %pad_maximum_fusion.30), channel_id=1, source_target_pairs={{0,2},{1,3},{2,0},{3,1},{4,6},{5,7},{6,4},{7,5},{8,10},{9,11},{10,... | collective-permute-start | bytes 884744 | tf_op jit(solution)/shard_map/ppermute | solution.py:961
  39.8 69.8 %collective-permute-start.3 = (bf16[768,1536]{1,0:T(8,128)(2,1)}, bf16[768,1536]{1,0:T(8,128)(2,1)}, u32[]{:S(2)}, u32[]{:S(2)}) collective-permute-start(bf16[768,1536]{1,0:T(8,128)(2,1)} %pad_maximum_fusion.own_ref), channel_id=1, source_target_pairs={{0,1},{1,0},{2,3},{3,2},{4,5},{5,4},{6,7},{7,6},{8,9},{9,8},{10,11... | collective-permute-start | bytes 7077896 | tf_op jit(solution)/shard_map/ppermute | solution.py:961
  41.4 62.5 %collective-permute-start.4 = (bf16[576,1536]{1,0:T(8,128)(2,1)S(1)}, bf16[576,1536]{1,0:T(8,128)(2,1)}, u32[]{:S(2)}, u32[]{:S(2)}) collective-permute-start(bf16[576,1536]{1,0:T(8,128)(2,1)S(1)} %pad_maximum_fusion.3.own_ref), channel_id=1, source_target_pairs={{0,1},{1,0},{2,3},{3,2},{4,5},{5,4},{6,7},{7,6},{8,9},{9,8},{10,11... | collective-permute-start | bytes 5308424 | tf_op jit(solution)/shard_map/ppermute | solution.py:961
  49.7 18.3 %collective-permute-start.2 = (bf16[192,576]{1,0:T(8,128)(2,1)}, bf16[192,576]{1,0:T(8,128)(2,1)}, u32[]{:S(2)}, u32[]{:S(2)}) collective-permute-start(bf16[192,576]{1,0:T(8,128)(2,1)} %pad_maximum_fusion.32.own_ref), channel_id=1, source_target_pairs={{0,3},{1,2},{2,1},{3,0},{4,7},{5,6},{6,5},{7,4},{8,11},{9,10},{10,... | collective-permute-start | bytes 663560 | tf_op jit(solution)/shard_map/ppermute | solution.py:961
  51.2 14.4 %collective-permute-start.5 = (bf16[72,1536]{1,0:T(8,128)(2,1)}, bf16[72,1536]{1,0:T(8,128)(2,1)}, u32[]{:S(2)}, u32[]{:S(2)}) collective-permute-start(bf16[72,1536]{1,0:T(8,128)(2,1)} %pad_maximum_fusion.33), channel_id=1, source_target_pairs={{0,2},{1,3},{2,0},{3,1},{4,6},{5,7},{6,4},{7,5},{8,10},{9,11},{10,... | collective-permute-start | bytes 663560 | tf_op jit(solution)/shard_map/ppermute | solution.py:961
  51.7 39.7 %collective-permute-start.14 = (bf16[1,96,1536]{2,1,0:T(8,128)(2,1)}, bf16[1,96,1536]{2,1,0:T(8,128)(2,1)}, u32[]{:S(2)}, u32[]{:S(2)}) collective-permute-start(bf16[1,96,1536]{2,1,0:T(8,128)(2,1)} %bitcast.22), channel_id=1, source_target_pairs={{0,16},{4,20},{8,24},{12,28},{16,0},{20,4},{24,8},{28,12},{1,17},{... | collective-permute-start | bytes 884744 | tf_op jit(solution)/shard_map/ppermute | solution.py:961
  65.6 34.1 %collective-permute-start.6 = (bf16[1,72,1536]{2,1,0:T(8,128)(2,1)}, bf16[1,72,1536]{2,1,0:T(8,128)(2,1)}, u32[]{:S(2)}, u32[]{:S(2)}) collective-permute-start(bf16[1,72,1536]{2,1,0:T(8,128)(2,1)} %bitcast.16), channel_id=1, source_target_pairs={{0,4},{4,0},{8,12},{12,8},{16,20},{20,16},{24,28},{28,24},{1,5},{5... | collective-permute-start | bytes 663560 | tf_op jit(solution)/shard_map/ppermute | solution.py:961
  91.5 27.0 %all-to-all-start.1 = ((bf16[8,128,256]{2,1,0:T(8,128)(2,1)}), bf16[8,128,256]{2,1,0:T(8,128)(2,1)}, u32[]{:S(2)}, u32[]{:S(2)}) async-start(bf16[8,128,256]{2,1,0:T(8,128)(2,1)} %bitcast.189), calls=%async_computation.1 | async-start | bytes 1048576 | tf_op jit(solution)/shard_map/all_to_all | solution.py:1358
  95.6 178.7 %all-gather.16.cloned.1.call-start = ((), (), s32[]{:S(2)}) async-start(), calls=%async_computation.9 | async-start | bytes 4177920 | tf_op jit(solution)/shard_map/all_gather | solution.py:1289
  97.8 30.3 %collective-permute-start.15 = (bf16[2,96,1536]{2,1,0:T(8,128)(2,1)}, bf16[2,96,1536]{2,1,0:T(8,128)(2,1)}, u32[]{:S(2)}, u32[]{:S(2)}) collective-permute-start(bf16[2,96,1536]{2,1,0:T(8,128)(2,1)} %pad_maximum_fusion.22), channel_id=1, source_target_pairs={{0,8},{4,12},{8,0},{12,4},{16,24},{20,28},{24,16},{28,20},{1,9},{5... | collective-permute-start | bytes 1769480 | tf_op jit(solution)/shard_map/ppermute | solution.py:961
  101.5 29.9 %collective-permute-start.7 = (bf16[2,72,1536]{2,1,0:T(8,128)(2,1)}, bf16[2,72,1536]{2,1,0:T(8,128)(2,1)}, u32[]{:S(2)}, u32[]{:S(2)}) collective-permute-start(bf16[2,72,1536]{2,1,0:T(8,128)(2,1)} %pad_maximum_fusion.26), channel_id=1, source_target_pairs={{0,16},{4,20},{8,24},{12,28},{16,0},{20,4},{24,8},{28,12},{1,17},{... | collective-permute-start | bytes 1327112 | tf_op jit(solution)/shard_map/ppermute | solution.py:961
  130.4 26.7 %collective-permute-start.16 = (bf16[4,96,1536]{2,1,0:T(8,128)(2,1)}, bf16[4,96,1536]{2,1,0:T(8,128)(2,1)}, u32[]{:S(2)}, u32[]{:S(2)}) collective-permute-start(bf16[4,96,1536]{2,1,0:T(8,128)(2,1)} %pad_maximum_fusion.7), channel_id=1, source_target_pairs={{0,4},{4,0},{8,12},{12,8},{16,20},{20,16},{24,28},{28,24},{1,5},{5... | collective-permute-start | bytes 3538952 | tf_op jit(solution)/shard_map/ppermute | solution.py:961
  133.6 23.5 %collective-permute-start.8 = (bf16[4,72,1536]{2,1,0:T(8,128)(2,1)}, bf16[4,72,1536]{2,1,0:T(8,128)(2,1)}, u32[]{:S(2)}, u32[]{:S(2)}) collective-permute-start(bf16[4,72,1536]{2,1,0:T(8,128)(2,1)} %pad_maximum_fusion.11), channel_id=1, source_target_pairs={{0,8},{4,12},{8,0},{12,4},{16,24},{20,28},{24,16},{28,20},{1,9},{5... | collective-permute-start | bytes 2654216 | tf_op jit(solution)/shard_map/ppermute | solution.py:961
  158.7 12.0 %collective-permute-start.9 = (bf16[8,72,1536]{2,1,0:T(8,128)(2,1)S(1)}, bf16[8,72,1536]{2,1,0:T(8,128)(2,1)}, u32[]{:S(2)}, u32[]{:S(2)}) collective-permute-start(bf16[8,72,1536]{2,1,0:T(8,128)(2,1)S(1)} %pad_maximum_fusion.4.piece_ref), channel_id=1, source_target_pairs={{0,1},{1,0},{2,3},{3,2},{4,5},{5,4},{6,7},{7,6},{8,9},{9,8},{10,11... | collective-permute-start | bytes 5308424 | tf_op jit(solution)/shard_map/ppermute | solution.py:961
  162.0 33.3 %collective-permute-start.17 = (bf16[8,96,1536]{2,1,0:T(8,128)(2,1)}, bf16[8,96,1536]{2,1,0:T(8,128)(2,1)}, u32[]{:S(2)}, u32[]{:S(2)}) collective-permute-start(bf16[8,96,1536]{2,1,0:T(8,128)(2,1)} %pad_maximum_fusion.1.piece_ref), channel_id=1, source_target_pairs={{0,1},{1,0},{2,3},{3,2},{4,5},{5,4},{6,7},{7,6},{8,9},{9,8},{10,11... | collective-permute-start | bytes 7077896 | tf_op jit(solution)/shard_map/ppermute | solution.py:961
  163.7 21.1 %collective-permute-start.10 = (bf16[256,768]{1,0:T(8,128)(2,1)}, bf16[256,768]{1,0:T(8,128)(2,1)}, u32[]{:S(2)}, u32[]{:S(2)}) collective-permute-start(bf16[256,768]{1,0:T(8,128)(2,1)} %get-tuple-element.289), channel_id=1, source_target_pairs={{0,1},{1,0},{2,3},{3,2},{4,5},{5,4},{6,7},{7,6},{8,9},{9,8},{10,11... | collective-permute-start | bytes 1179656 | tf_op jit(solution)/shard_map/ppermute | solution.py:961
  163.7 21.1 %collective-permute-start.11 = (bf16[256,768]{1,0:T(8,128)(2,1)}, bf16[256,768]{1,0:T(8,128)(2,1)}, u32[]{:S(2)}, u32[]{:S(2)}) collective-permute-start(bf16[256,768]{1,0:T(8,128)(2,1)} %get-tuple-element.288), channel_id=1, source_target_pairs={{0,2},{1,3},{2,0},{3,1},{4,6},{5,7},{6,4},{7,5},{8,10},{9,11},{10,... | collective-permute-start | bytes 1179656 | tf_op jit(solution)/shard_map/ppermute | solution.py:961
  164.2 20.6 %collective-permute-start.12 = (bf16[256,768]{1,0:T(8,128)(2,1)}, bf16[256,768]{1,0:T(8,128)(2,1)}, u32[]{:S(2)}, u32[]{:S(2)}) collective-permute-start(bf16[256,768]{1,0:T(8,128)(2,1)} %get-tuple-element.287), channel_id=1, source_target_pairs={{0,3},{1,2},{2,1},{3,0},{4,7},{5,6},{6,5},{7,4},{8,11},{9,10},{10,... | collective-permute-start | bytes 1179656 | tf_op jit(solution)/shard_map/ppermute | solution.py:961
  189.9 28.7 %collective-permute-start.20 = (bf16[256,384]{1,0:T(8,128)(2,1)S(1)}, bf16[256,384]{1,0:T(8,128)(2,1)S(1)}, u32[]{:S(2)}, u32[]{:S(2)}) collective-permute-start(bf16[256,384]{1,0:T(8,128)(2,1)S(1)} %get-tuple-element.300), channel_id=1, source_target_pairs={{0,1},{1,0},{2,3},{3,2},{4,5},{5,4},{6,7},{7,6},{8,9},{9,8},{10,11... | collective-permute-start | bytes 589832 | tf_op jit(solution)/shard_map/ppermute | solution.py:961
  190.0 29.3 %collective-permute-start.21 = (bf16[256,384]{1,0:T(8,128)(2,1)S(1)}, bf16[256,384]{1,0:T(8,128)(2,1)S(1)}, u32[]{:S(2)}, u32[]{:S(2)}) collective-permute-start(bf16[256,384]{1,0:T(8,128)(2,1)S(1)} %get-tuple-element.299), channel_id=1, source_target_pairs={{0,2},{1,3},{2,0},{3,1},{4,6},{5,7},{6,4},{7,5},{8,10},{9,11},{10,... | collective-permute-start | bytes 589832 | tf_op jit(solution)/shard_map/ppermute | solution.py:961
  190.6 29.4 %collective-permute-start.22 = (bf16[256,384]{1,0:T(8,128)(2,1)S(1)}, bf16[256,384]{1,0:T(8,128)(2,1)S(1)}, u32[]{:S(2)}, u32[]{:S(2)}) collective-permute-start(bf16[256,384]{1,0:T(8,128)(2,1)S(1)} %get-tuple-element.298), channel_id=1, source_target_pairs={{0,3},{1,2},{2,1},{3,0},{4,7},{5,6},{6,5},{7,4},{8,11},{9,10},{10,... | collective-permute-start | bytes 589832 | tf_op jit(solution)/shard_map/ppermute | solution.py:961
  223.0 126.9 %reduce-scatter.3.cloned.1.call-start = ((), (), s32[]{:S(2)}) async-start(), calls=%async_computation.10 | async-start | bytes 10321920 | tf_op jit(solution)/shard_map/reduce_scatter | solution.py:1267
  257.3 37.6 %all-to-all-start.2 = ((bf16[8,128,256]{2,1,0:T(8,128)(2,1)}), bf16[8,128,256]{2,1,0:T(8,128)(2,1)S(1)}, u32[]{:S(2)}, u32[]{:S(2)}) async-start(bf16[8,128,256]{2,1,0:T(8,128)(2,1)} %copy-done.31), calls=%async_computation.2 | async-start | bytes 1048576 | tf_op jit(solution)/shard_map/all_to_all | solution.py:1459
  263.1 122.4 %all-gather.18.cloned.1.call-start = ((), (), s32[]{:S(2)}) async-start(), calls=%async_computation.12 | async-start | bytes 1966080 | tf_op jit(solution)/shard_map/all_gather | solution.py:1289
  285.8 32.6 %collective-permute-start.27 = (bf16[3,192,768]{2,1,0:T(8,128)(2,1)}, bf16[3,192,768]{2,1,0:T(8,128)(2,1)}, u32[]{:S(2)}, u32[]{:S(2)}) collective-permute-start(bf16[3,192,768]{2,1,0:T(8,128)(2,1)} %get-tuple-element.164), channel_id=1, source_target_pairs={{0,4},{4,0},{8,12},{12,8},{16,20},{20,16},{24,28},{28,24},{1,5},{5... | collective-permute-start | bytes 2654216 | tf_op jit(solution)/shard_map/ppermute | solution.py:961
  294.2 30.6 %collective-permute-start.26 = (bf16[3,192,768]{2,1,0:T(8,128)(2,1)}, bf16[3,192,768]{2,1,0:T(8,128)(2,1)}, u32[]{:S(2)}, u32[]{:S(2)}) collective-permute-start(bf16[3,192,768]{2,1,0:T(8,128)(2,1)} %get-tuple-element.165), channel_id=1, source_target_pairs={{0,4},{4,0},{8,12},{12,8},{16,20},{20,16},{24,28},{28,24},{1,5},{5... | collective-permute-start | bytes 2654216 | tf_op jit(solution)/shard_map/ppermute | solution.py:961
  294.8 118.3 %reduce-scatter.5.cloned.1.call-start = ((), (), s32[]{:S(2)}) async-start(), calls=%async_computation.11 | async-start | bytes 4423680 | tf_op jit(solution)/shard_map/reduce_scatter | solution.py:1267
  321.5 13.7 %collective-permute-start.29 = (bf16[3,96,768]{2,1,0:T(8,128)(2,1)}, bf16[3,96,768]{2,1,0:T(8,128)(2,1)S(1)}, u32[]{:S(2)}, u32[]{:S(2)}) collective-permute-start(bf16[3,96,768]{2,1,0:T(8,128)(2,1)} %constant_dynamic-slice_fusion.12), channel_id=1, source_target_pairs={{0,8},{4,12},{8,0},{12,4},{16,24},{20,28},{24,16},{28,20},{1,9},{5... | collective-permute-start | bytes 1327112 | tf_op jit(solution)/shard_map/ppermute | solution.py:961
  327.2 20.1 %collective-permute-start.28 = (bf16[3,96,768]{2,1,0:T(8,128)(2,1)}, bf16[3,96,768]{2,1,0:T(8,128)(2,1)}, u32[]{:S(2)}, u32[]{:S(2)}) collective-permute-start(bf16[3,96,768]{2,1,0:T(8,128)(2,1)} %constant_dynamic-slice_fusion.11), channel_id=1, source_target_pairs={{0,16},{4,20},{8,24},{12,28},{16,0},{20,4},{24,8},{28,12},{1,17},{... | collective-permute-start | bytes 1327112 | tf_op jit(solution)/shard_map/ppermute | solution.py:961
  357.1 20.9 %collective-permute-start.25 = (bf16[2,2,1,128,768]{4,3,2,1,0:T(8,128)(2,1)}, bf16[2,2,1,128,768]{4,3,2,1,0:T(8,128)(2,1)}, u32[]{:S(2)}, u32[]{:S(2)}) collective-permute-start(bf16[2,2,1,128,768]{4,3,2,1,0:T(8,128)(2,1)} %constant_dynamic-slice_fusion.13), channel_id=1, source_target_pairs={{0,4},{4,0},{8,12},{12,8},{16,20},{20,16},{24,28},{28,24},{1,5},{5... | collective-permute-start | bytes 2359304 | tf_op jit(solution)/shard_map/ppermute | solution.py:961
  358.3 21.9 %collective-permute-start.32 = (bf16[3,48,768]{2,1,0:T(8,128)(2,1)S(1)}, bf16[3,48,768]{2,1,0:T(8,128)(2,1)S(1)}, u32[]{:S(2)}, u32[]{:S(2)}) collective-permute-start(bf16[3,48,768]{2,1,0:T(8,128)(2,1)S(1)} %constant_dynamic-slice_fusion.10), channel_id=1, source_target_pairs={{0,16},{4,20},{8,24},{12,28},{16,0},{20,4},{24,8},{28,12},{1,17},{... | collective-permute-start | bytes 663560 | tf_op jit(solution)/shard_map/ppermute | solution.py:961
  358.3 26.3 %collective-permute-start.31 = (bf16[3,48,768]{2,1,0:T(8,128)(2,1)}, bf16[3,48,768]{2,1,0:T(8,128)(2,1)S(1)}, u32[]{:S(2)}, u32[]{:S(2)}) collective-permute-start(bf16[3,48,768]{2,1,0:T(8,128)(2,1)} %constant_dynamic-slice_fusion.9), channel_id=1, source_target_pairs={{0,8},{4,12},{8,0},{12,4},{16,24},{20,28},{24,16},{28,20},{1,9},{5... | collective-permute-start | bytes 663560 | tf_op jit(solution)/shard_map/ppermute | solution.py:961
  362.0 38.0 %collective-permute-start.37 = (bf16[96,5376]{1,0:T(8,128)(2,1)}, bf16[96,5376]{1,0:T(8,128)(2,1)}, u32[]{:S(2)}, u32[]{:S(2)}) collective-permute-start(bf16[96,5376]{1,0:T(8,128)(2,1)} %constant_dynamic-slice_fusion.8), channel_id=1, source_target_pairs={{0,4},{4,0},{8,12},{12,8},{16,20},{20,16},{24,28},{28,24},{1,5},{5... | collective-permute-start | bytes 3096584 | tf_op jit(solution)/shard_map/ppermute | solution.py:961
  380.1 12.0 %collective-permute-start.30 = (bf16[2,1,128,768]{3,2,0,1:T(8,128)(2,1)}, bf16[2,1,128,768]{3,2,0,1:T(8,128)(2,1)}, u32[]{:S(2)}, u32[]{:S(2)}) collective-permute-start(bf16[2,1,128,768]{3,2,0,1:T(8,128)(2,1)} %dynamic-slice_bitcast_fusion), channel_id=1, source_target_pairs={{0,8},{4,12},{8,0},{12,4},{16,24},{20,28},{24,16},{28,20},{1,9},{5... | collective-permute-start | bytes 1179656 | tf_op jit(solution)/shard_map/ppermute | solution.py:961
  381.3 21.2 %collective-permute-start.36 = (bf16[1,3,48,768]{3,2,1,0:T(8,128)(2,1)S(1)}, bf16[1,3,48,768]{3,2,1,0:T(8,128)(2,1)}, u32[]{:S(2)}, u32[]{:S(2)}) collective-permute-start(bf16[1,3,48,768]{3,2,1,0:T(8,128)(2,1)S(1)} %fusion.38), channel_id=1, source_target_pairs={{0,16},{4,20},{8,24},{12,28},{16,0},{20,4},{24,8},{28,12},{1,17},{... | collective-permute-start | bytes 663560 | tf_op jit(solution)/shard_map/ppermute | solution.py:961
  385.4 20.8 %collective-permute-start.35 = (bf16[1,3,48,768]{3,2,1,0:T(8,128)(2,1)}, bf16[1,3,48,768]{3,2,1,0:T(8,128)(2,1)}, u32[]{:S(2)}, u32[]{:S(2)}) collective-permute-start(bf16[1,3,48,768]{3,2,1,0:T(8,128)(2,1)} %fusion.39), channel_id=1, source_target_pairs={{0,8},{4,12},{8,0},{12,4},{16,24},{20,28},{24,16},{28,20},{1,9},{5... | collective-permute-start | bytes 663560 | tf_op jit(solution)/shard_map/ppermute | solution.py:961
  390.0 19.4 %collective-permute-start.34 = (bf16[384,768]{1,0:T(8,128)(2,1)S(1)}, bf16[384,768]{1,0:T(8,128)(2,1)S(1)}, u32[]{:S(2)}, u32[]{:S(2)}) collective-permute-start(bf16[384,768]{1,0:T(8,128)(2,1)S(1)} %get-tuple-element.183), channel_id=1, source_target_pairs={{0,4},{4,0},{8,12},{12,8},{16,20},{20,16},{24,28},{28,24},{1,5},{5... | collective-permute-start | bytes 1769480 | tf_op jit(solution)/shard_map/ppermute | solution.py:961
  402.4 25.8 %collective-permute-start.43 = (bf16[48,5376]{1,0:T(8,128)(2,1)}, bf16[48,5376]{1,0:T(8,128)(2,1)}, u32[]{:S(2)}, u32[]{:S(2)}) collective-permute-start(bf16[48,5376]{1,0:T(8,128)(2,1)} %constant_dynamic-slice_fusion.6), channel_id=1, source_target_pairs={{0,8},{4,12},{8,0},{12,4},{16,24},{20,28},{24,16},{28,20},{1,9},{5... | collective-permute-start | bytes 1548296 | tf_op jit(solution)/shard_map/ppermute | solution.py:961
  404.2 31.1 %collective-permute-start.42 = (bf16[2,3,48,768]{3,2,1,0:T(8,128)(2,1)}, bf16[2,3,48,768]{3,2,1,0:T(8,128)(2,1)}, u32[]{:S(2)}, u32[]{:S(2)}) collective-permute-start(bf16[2,3,48,768]{3,2,1,0:T(8,128)(2,1)} %pad_maximum_fusion.27), channel_id=1, source_target_pairs={{0,8},{4,12},{8,0},{12,4},{16,24},{20,28},{24,16},{28,20},{1,9},{5... | collective-permute-start | bytes 1327112 | tf_op jit(solution)/shard_map/ppermute | solution.py:961
  408.0 29.4 %collective-permute-start.41 = (bf16[2,3,48,768]{3,2,1,0:T(8,128)(2,1)}, bf16[2,3,48,768]{3,2,1,0:T(8,128)(2,1)S(1)}, u32[]{:S(2)}, u32[]{:S(2)}) collective-permute-start(bf16[2,3,48,768]{3,2,1,0:T(8,128)(2,1)} %pad_maximum_fusion.28), channel_id=1, source_target_pairs={{0,16},{4,20},{8,24},{12,28},{16,0},{20,4},{24,8},{28,12},{1,17},{... | collective-permute-start | bytes 1327112 | tf_op jit(solution)/shard_map/ppermute | solution.py:961
  411.1 29.2 %collective-permute-start.40 = (bf16[192,768]{1,0:T(8,128)(2,1)}, bf16[192,768]{1,0:T(8,128)(2,1)}, u32[]{:S(2)}, u32[]{:S(2)}) collective-permute-start(bf16[192,768]{1,0:T(8,128)(2,1)} %constant_dynamic-slice_fusion.5), channel_id=1, source_target_pairs={{0,8},{4,12},{8,0},{12,4},{16,24},{20,28},{24,16},{28,20},{1,9},{5... | collective-permute-start | bytes 884744 | tf_op jit(solution)/shard_map/ppermute | solution.py:961
  415.3 27.6 %collective-permute-start.39 = (bf16[96,1664]{1,0:T(8,128)(2,1)S(1)}, bf16[96,1664]{1,0:T(8,128)(2,1)S(1)}, u32[]{:S(2)}, u32[]{:S(2)}) collective-permute-start(bf16[96,1664]{1,0:T(8,128)(2,1)S(1)} %constant_dynamic-slice_fusion.4), channel_id=1, source_target_pairs={{0,4},{4,0},{8,12},{12,8},{16,20},{20,16},{24,28},{28,24},{1,5},{5... | collective-permute-start | bytes 958472 | tf_op jit(solution)/shard_map/ppermute | solution.py:961
  428.1 23.2 %collective-permute-start.38 = (bf16[192,576]{1,0:T(8,128)(2,1)S(1)}, bf16[192,576]{1,0:T(8,128)(2,1)S(1)}, u32[]{:S(2)}, u32[]{:S(2)}) collective-permute-start(bf16[192,576]{1,0:T(8,128)(2,1)S(1)} %slice.205), channel_id=1, source_target_pairs={{0,16},{4,20},{8,24},{12,28},{16,0},{20,4},{24,8},{28,12},{1,17},{... | collective-permute-start | bytes 663560 | tf_op jit(solution)/shard_map/ppermute | solution.py:961
  435.3 21.5 %collective-permute-start.47 = (bf16[24,5376]{1,0:T(8,128)(2,1)S(1)}, bf16[24,5376]{1,0:T(8,128)(2,1)S(1)}, u32[]{:S(2)}, u32[]{:S(2)}) collective-permute-start(bf16[24,5376]{1,0:T(8,128)(2,1)S(1)} %constant_dynamic-slice_fusion.3), channel_id=1, source_target_pairs={{0,16},{4,20},{8,24},{12,28},{16,0},{20,4},{24,8},{28,12},{1,17},{... | collective-permute-start | bytes 774152 | tf_op jit(solution)/shard_map/ppermute | solution.py:961
  437.4 54.1 %collective-permute-start.54 = (bf16[4,3,48,768]{3,2,1,0:T(8,128)(2,1)S(1)}, bf16[4,3,48,768]{3,2,1,0:T(8,128)(2,1)S(1)}, u32[]{:S(2)}, u32[]{:S(2)}) collective-permute-start(bf16[4,3,48,768]{3,2,1,0:T(8,128)(2,1)S(1)} %pad_maximum_fusion.12), channel_id=1, source_target_pairs={{0,4},{4,0},{8,12},{12,8},{16,20},{20,16},{24,28},{28,24},{1,5},{5... | collective-permute-start | bytes 2654216 | tf_op jit(solution)/shard_map/ppermute | solution.py:961
  440.3 52.5 %collective-permute-start.53 = (bf16[4,3,48,768]{3,2,1,0:T(8,128)(2,1)S(1)}, bf16[4,3,48,768]{3,2,1,0:T(8,128)(2,1)S(1)}, u32[]{:S(2)}, u32[]{:S(2)}) collective-permute-start(bf16[4,3,48,768]{3,2,1,0:T(8,128)(2,1)S(1)} %pad_maximum_fusion.13), channel_id=1, source_target_pairs={{0,4},{4,0},{8,12},{12,8},{16,20},{20,16},{24,28},{28,24},{1,5},{5... | collective-permute-start | bytes 2654216 | tf_op jit(solution)/shard_map/ppermute | solution.py:961
  442.8 24.5 %collective-permute-start.46 = (bf16[96,768]{1,0:T(8,128)(2,1)S(1)}, bf16[96,768]{1,0:T(8,128)(2,1)S(1)}, u32[]{:S(2)}, u32[]{:S(2)}) collective-permute-start(bf16[96,768]{1,0:T(8,128)(2,1)S(1)} %constant_dynamic-slice_fusion.2), channel_id=1, source_target_pairs={{0,16},{4,20},{8,24},{12,28},{16,0},{20,4},{24,8},{28,12},{1,17},{... | collective-permute-start | bytes 442376 | tf_op jit(solution)/shard_map/ppermute | solution.py:961
  451.4 16.0 %collective-permute-start.45 = (bf16[48,1664]{1,0:T(8,128)(2,1)S(1)}, bf16[48,1664]{1,0:T(8,128)(2,1)S(1)}, u32[]{:S(2)}, u32[]{:S(2)}) collective-permute-start(bf16[48,1664]{1,0:T(8,128)(2,1)S(1)} %constant_dynamic-slice_fusion.1), channel_id=1, source_target_pairs={{0,8},{4,12},{8,0},{12,4},{16,24},{20,28},{24,16},{28,20},{1,9},{5... | collective-permute-start | bytes 479240 | tf_op jit(solution)/shard_map/ppermute | solution.py:961
  456.8 16.9 %collective-permute-start.44 = (bf16[1,192,576]{2,1,0:T(8,128)(2,1)S(1)}, bf16[1,192,576]{2,1,0:T(8,128)(2,1)S(1)}, u32[]{:S(2)}, u32[]{:S(2)}) collective-permute-start(bf16[1,192,576]{2,1,0:T(8,128)(2,1)S(1)} %fusion.37), channel_id=1, source_target_pairs={{0,4},{4,0},{8,12},{12,8},{16,20},{20,16},{24,28},{28,24},{1,5},{5... | collective-permute-start | bytes 663560 | tf_op jit(solution)/shard_map/ppermute | solution.py:961
  476.0 15.4 %collective-permute-start.48 = (bf16[2,192,576]{2,1,0:T(8,128)(2,1)S(1)}, bf16[2,192,576]{2,1,0:T(8,128)(2,1)S(1)}, u32[]{:S(2)}, u32[]{:S(2)}) collective-permute-start(bf16[2,192,576]{2,1,0:T(8,128)(2,1)S(1)} %pad_maximum_fusion.25), channel_id=1, source_target_pairs={{0,8},{4,12},{8,0},{12,4},{16,24},{20,28},{24,16},{28,20},{1,9},{5... | collective-permute-start | bytes 1327112 | tf_op jit(solution)/shard_map/ppermute | solution.py:961
  477.5 24.1 %collective-permute-start.52 = (bf16[2,24,5376]{2,1,0:T(8,128)(2,1)S(1)}, bf16[2,24,5376]{2,1,0:T(8,128)(2,1)S(1)}, u32[]{:S(2)}, u32[]{:S(2)}) collective-permute-start(bf16[2,24,5376]{2,1,0:T(8,128)(2,1)S(1)} %pad_maximum_fusion.24), channel_id=1, source_target_pairs={{0,8},{4,12},{8,0},{12,4},{16,24},{20,28},{24,16},{28,20},{1,9},{5... | collective-permute-start | bytes 1548296 | tf_op jit(solution)/shard_map/ppermute | solution.py:961
  479.9 25.2 %collective-permute-start.56 = (bf16[1,24,1664]{2,1,0:T(8,128)(2,1)S(1)}, bf16[1,24,1664]{2,1,0:T(8,128)(2,1)S(1)}, u32[]{:S(2)}, u32[]{:S(2)}) collective-permute-start(bf16[1,24,1664]{2,1,0:T(8,128)(2,1)S(1)} %fusion.41), channel_id=1, source_target_pairs={{0,16},{4,20},{8,24},{12,28},{16,0},{20,4},{24,8},{28,12},{1,17},{... | collective-permute-start | bytes 239624 | tf_op jit(solution)/shard_map/ppermute | solution.py:961
  501.7 25.8 %collective-permute-start.55 = (bf16[4,24,5376]{2,1,0:T(8,128)(2,1)S(1)}, bf16[4,24,5376]{2,1,0:T(8,128)(2,1)S(1)}, u32[]{:S(2)}, u32[]{:S(2)}) collective-permute-start(bf16[4,24,5376]{2,1,0:T(8,128)(2,1)S(1)} %pad_maximum_fusion.9), channel_id=1, source_target_pairs={{0,4},{4,0},{8,12},{12,8},{16,20},{20,16},{24,28},{28,24},{1,5},{5... | collective-permute-start | bytes 3096584 | tf_op jit(solution)/shard_map/ppermute | solution.py:961
  502.6 18.7 %collective-permute-start.58 = (bf16[2,96,768]{2,1,0:T(8,128)(2,1)S(1)}, bf16[2,96,768]{2,1,0:T(8,128)(2,1)S(1)}, u32[]{:S(2)}, u32[]{:S(2)}) collective-permute-start(bf16[2,96,768]{2,1,0:T(8,128)(2,1)S(1)} %pad_maximum_fusion.31), channel_id=1, source_target_pairs={{0,8},{4,12},{8,0},{12,4},{16,24},{20,28},{24,16},{28,20},{1,9},{5... | collective-permute-start | bytes 884744 | tf_op jit(solution)/shard_map/ppermute | solution.py:961
  505.1 18.1 %collective-permute-start.57 = (bf16[2,24,1664]{2,1,0:T(8,128)(2,1)S(1)}, bf16[2,24,1664]{2,1,0:T(8,128)(2,1)S(1)}, u32[]{:S(2)}, u32[]{:S(2)}) collective-permute-start(bf16[2,24,1664]{2,1,0:T(8,128)(2,1)S(1)} %pad_maximum_fusion.34), channel_id=1, source_target_pairs={{0,8},{4,12},{8,0},{12,4},{16,24},{20,28},{24,16},{28,20},{1,9},{5... | collective-permute-start | bytes 479240 | tf_op jit(solution)/shard_map/ppermute | solution.py:961
  521.4 18.7 %collective-permute-start.60 = (bf16[4,96,768]{2,1,0:T(8,128)(2,1)S(1)}, bf16[4,96,768]{2,1,0:T(8,128)(2,1)S(1)}, u32[]{:S(2)}, u32[]{:S(2)}) collective-permute-start(bf16[4,96,768]{2,1,0:T(8,128)(2,1)S(1)} %pad_maximum_fusion.23), channel_id=1, source_target_pairs={{0,4},{4,0},{8,12},{12,8},{16,20},{20,16},{24,28},{28,24},{1,5},{5... | collective-permute-start | bytes 1769480 | tf_op jit(solution)/shard_map/ppermute | solution.py:961
  523.2 22.1 %collective-permute-start.59 = (bf16[4,24,1664]{2,1,0:T(8,128)(2,1)S(1)}, bf16[4,24,1664]{2,1,0:T(8,128)(2,1)S(1)}, u32[]{:S(2)}, u32[]{:S(2)}) collective-permute-start(bf16[4,24,1664]{2,1,0:T(8,128)(2,1)S(1)} %pad_maximum_fusion.29), channel_id=1, source_target_pairs={{0,4},{4,0},{8,12},{12,8},{16,20},{20,16},{24,28},{28,24},{1,5},{5... | collective-permute-start | bytes 958472 | tf_op jit(solution)/shard_map/ppermute | solution.py:961
  (150 other events, 824.5 us)
Sparse Core Ops, SparseCore 0:
  16.2 30.9 all-gather.7
  48.8 21.8 all-gather.9
  72.2 38.8 all-gather.11
  112.6 37.4 all-gather.13
  223.1 29.7 all-gather.15
  257.4 71.1 reduce-scatter.2
  330.8 19.6 all-gather.17
  357.2 40.5 reduce-scatter.4

commit v4 on v3

--- a/solution.py
+++ b/solution.py
@@ -13,7 +13,7 @@
 EPSILON = 1e-05
 BLOCK_LIMIT = 1024
 FAR = 1e9
-VMEM_BYTES = 32 * 1024 * 1024
+VMEM_BYTES = 24 * 1024 * 1024
 
 F32 = jnp.float32
 BF16 = jnp.bfloat16

time: 567 us -> 567 us (level)
  no operation moved by 1% of the time
where the time goes in v4:
time: 567 us; the launch traced here: 559 us
  waiting for transfers between devices  145 us (26%)
  starting transfers between devices  107 us (19%)
  Pallas kernels  102 us (18%)
  local copies, waits for them, and re-layouts  101 us (18%)
  other arithmetic  58.1 us (10%)
  matrix products  28.3 us (5%)
  between operations  16.6 us (3%)
    ppermute x57, waiting for transfers between devices, flip(): lax.ppermute(value, axis, [(i, i ^ bit) for i in range(lax.axis_size(axis...  133 us
    ppermute x57, starting transfers between devices, flip(): lax.ppermute(value, axis, [(i, i ^ bit) for i in range(lax.axis_size(axis...  68.9 us
    unnamed x292, local copies, waits for them, and re-layouts  62 us
    dot_general x8, matrix products, matmul_nt(): lax.dot_general(left, right, (((1,), (1,)), ((), ())), preferred_element_...  16.5 us
    pallas_call x1, Pallas kernels, attend_back(): pl.pallas_call(functools.partial(attend_back_kernel, heads, tokens), grid...  16.3 us
    pallas_call x2, Pallas kernels, finish(): pl.pallas_call(functools.partial(place_kernel, spans, self.order), in_spe...  15.2 us
    concatenate x6, other arithmetic, take(): jnp.concatenate([self.base, got], axis=0)  13.1 us
    convert_element_type x12, other arithmetic, advance(): piece = (self.keep.astype(F32) + got).astype(BF16)  12.3 us
  transfers between devices with their start and end apart: 72, of which 27 were waited for; matrix products, arithmetic and copies ran while one was open for 21% of the time, Pallas kernels for 18%

profile of v4, /device:TPU:0, one launch (start us, length us, event | category | flops | bytes accessed | tf_op | source)
XLA Modules:
  0.0 558.9 jit_solution(6586202175273563725)
XLA Ops:
  20.1 2.5 collective-permute-start.1
  23.9 5.8 %all-to-all-start = ((bf16[8,136,768]{2,1,0:T(8,128)(2,1)}), bf16[8,136,768]{2,1,0:T(8,128)(2,1)S(1)}, u32[]{:S(2)}, u32[]{:S(2)}) async-start(bf16[8,136,768]{2,1,0:T(8,128)(2,1)} %bitcast.2), calls=%async_computation | async-start | bytes 3342336 | tf_op jit(solution)/shard_map/all_to_all | solution.py:1352
  30.3 4.7 fusion.50
  51.7 2.9 collective-permute-start.14
  57.7 2.7 gru_forward.1
  65.6 2.4 collective-permute-start.6
  68.0 8.6 %all-to-all-done.tok_ref = bf16[8,136,768]{2,1,0:T(8,128)(2,1)S(1)} async-done(((bf16[8,136,768]{2,1,0:T(8,128)(2,1)}), bf16[8,136,768]{2,1,0:T(8,128)(2,1)S(1)}, u32[]{:S(2)}, u32[]{:S(2)}) %all-to-all-start) | async-done | bytes 1671200 | tf_op jit(solution)/shard_map/all_to_all | solution.py:1352
  76.6 9.3 %attend.1 = (bf16[1024,256]{1,0:T(8,128)(2,1)S(1)}, f32[1024,384]{1,0:T(8,128)S(1)}, bf16[3,1024,128]{2,1,0:T(8,128)(2,1)S(1)}, bf16[3,1024,128]{2,1,0:T(8,128)(...) custom-call(bf16[8,136,768]{2,1,0:T(8,128)(2,1)S(1)} %all-to-all-done.tok_ref, ...), custom_call_target="tpu_custom_call" | custom-call | flops 1 | bytes 1 | tf_op jit(solution)/shard_map/attend/pallas_call | solution.py:501
  91.5 4.1 all-to-all-start.1
  101.5 2.4 collective-permute-start.7
  109.6 2.8 place_own.2
  119.8 8.3 %collective-permute-done.15 = bf16[2,96,1536]{2,1,0:T(8,128)(2,1)} collective-permute-done((bf16[2,96,1536]{2,1,0:T(8,128)(2,1)}, bf16[2,96,1536]{2,1,0:T(8,128)(2,1)}, u32[]{:S(2)}, u32[]{:S(2)}) %collective-permute-start.15) | collective-permute-done | bytes 589856 | tf_op jit(solution)/shard_map/ppermute | solution.py:961
  128.1 2.4 pad_maximum_fusion.7
  137.7 2.5 copy-done.13
  140.2 5.4 feed_forward.1
  145.6 11.6 %collective-permute-done.16 = bf16[4,96,1536]{2,1,0:T(8,128)(2,1)} collective-permute-done((bf16[4,96,1536]{2,1,0:T(8,128)(2,1)}, bf16[4,96,1536]{2,1,0:T(8,128)(2,1)}, u32[]{:S(2)}, u32[]{:S(2)}) %collective-permute-start.16) | collective-permute-done | bytes 1179680 | tf_op jit(solution)/shard_map/ppermute | solution.py:961
  158.8 3.2 pad_maximum_fusion.1.piece_ref
  165.6 4.6 fusion.57
  170.7 2.5 copy-done.15
  173.2 7.6 %place.2 = (bf16[4,384,1536]{2,1,0:T(8,128)(2,1)S(1)}, bf16[4,192,1536]{2,1,0:T(8,128)(2,1)S(1)}) custom-call(bf16[8,72,1536]{2,1,0:T(8,128)(2,1)S(1)} %pad_maximum_fusion.4.piece_ref, bf16[8,72,1536]{2,1,0:T(8,128)(2,1)} %collective-permute-done.9.core_ref, bf16[4,384,1536]{2,1,0:T(8,128)(2,1)S(1)} %copy-done.15, ...), custom_call_target="tpu_custom_call", output_to_operand_aliasing={{0}: (2, {}), {1}: (3, {})} | custom-call | flops 1 | bytes 1 | tf_op jit(solution)/shard_map/place/pallas_call | solution.py:1252
  184.9 3.1 collective-permute-start.18
  196.2 7.6 %place.3 = (bf16[4,384,1536]{2,1,0:T(8,128)(2,1)S(1)}, bf16[4,384,1536]{2,1,0:T(8,128)(2,1)S(1)}) custom-call(bf16[8,96,1536]{2,1,0:T(8,128)(2,1)} %pad_maximum_fusion.1.piece_ref, bf16[8,96,1536]{2,1,0:T(8,128)(2,1)} %collective-permute-done.17.core_ref, bf16[4,384,1536]{2,1,0:T(8,128)(2,1)S(1)} %bitcast.165, ...), custom_call_target="tpu_custom_call", output_to_operand_aliasing={{0}: (2, {}), {1}: (3, {})} | custom-call | flops 1 | bytes 1 | tf_op jit(solution)/shard_map/place/pallas_call | solution.py:1252
  214.0 4.5 collective-permute-start.24
  224.9 3.9 fusion.60
  233.5 2.2 gru_back.1
  238.7 5.2 fusion.51
  243.9 2.2 multiply_reduce_fusion.1
  249.5 4.5 gradients.1
  254.0 3.3 copy-done
  257.3 5.8 %all-to-all-start.2 = ((bf16[8,128,256]{2,1,0:T(8,128)(2,1)}), bf16[8,128,256]{2,1,0:T(8,128)(2,1)S(1)}, u32[]{:S(2)}, u32[]{:S(2)}) async-start(bf16[8,128,256]{2,1,0:T(8,128)(2,1)} %copy-done.31), calls=%async_computation.2 | async-start | bytes 1048576 | tf_op jit(solution)/shard_map/all_to_all | solution.py:1459
  263.2 11.2 %all-gather.18.cloned.1.call-start = ((), (), s32[]{:S(2)}) async-start(), calls=%async_computation.12 | async-start | bytes 1966080 | tf_op jit(solution)/shard_map/all_gather | solution.py:1289
  279.2 5.8 %conv_gradient.2 = (bf16[3,192,768]{2,1,0:T(8,128)(2,1)S(1)}, bf16[3,192,768]{2,1,0:T(8,128)(2,1)}) custom-call(bf16[256,384]{1,0:T(8,128)(2,1)S(1)} %get-tuple-element.163.own_ref, bf16[256,384]{1,0:T(8,128)(2,1)S(1)} %copy-done.68, bf16[256,384]{1,0:T(8,128)(2,1)S(1)} %copy-done.70, bf16[256,384]{1,0:T(8,128)(2,1)S(1)} %copy-done.72, ...), custom_call_target="tpu_custom_call" | custom-call | flops 1 | bytes 1 | tf_op jit(solution)/shard_map/conv_gradient/pallas_call | solution.py:777
  287.6 5.8 %conv_gradient.3 = (bf16[3,192,768]{2,1,0:T(8,128)(2,1)S(1)}, bf16[3,192,768]{2,1,0:T(8,128)(2,1)}) custom-call(bf16[256,384]{1,0:T(8,128)(2,1)S(1)} %get-tuple-element.163.own_ref, bf16[256,384]{1,0:T(8,128)(2,1)S(1)} %copy-done.68, bf16[256,384]{1,0:T(8,128)(2,1)S(1)} %copy-done.70, bf16[256,384]{1,0:T(8,128)(2,1)S(1)} %copy-done.72, ...), custom_call_target="tpu_custom_call" | custom-call | flops 1 | bytes 1 | tf_op jit(solution)/shard_map/conv_gradient/pallas_call | solution.py:777
  302.1 16.3 %attend_back.1 = (bf16[1024,768]{1,0:T(8,128)(2,1)S(1)}, f32[768,576]{1,0:T(8,128)S(1)}, f32[2,1,768]{2,1,0:T(1,128)S(1)}) custom-call(bf16[8,136,768]{2,1,0:T(8,128)(2,1)S(1)} %all-to-all-done.tok_ref, bf16[768,576]{1,0:T(8,128)(2,1)S(1)} %copy-done.62, bf16[3,1024,128]{2,1,0:T(8,128)(2,1)S(1)} %copy-done.74, bf16[3,1024,128]{2,1,0:T(8,128)(2,1)S(1)} %copy-done.76, ...), custom_call_target="tpu_custom_call" | custom-call | flops 1 | bytes 1 | tf_op jit(solution)/shard_map/attend_back/pallas_call | solution.py:540
  318.5 2.2 add_convert_fusion.2
  327.3 2.3 collective-permute-start.28
  332.7 2.6 collective-permute-done.29
  337.2 10.3 %collective-permute-done.28 = bf16[3,96,768]{2,1,0:T(8,128)(2,1)} collective-permute-done((bf16[3,96,768]{2,1,0:T(8,128)(2,1)}, bf16[3,96,768]{2,1,0:T(8,128)(2,1)}, u32[]{:S(2)}, u32[]{:S(2)}) %collective-permute-start.28) | collective-permute-done | bytes 442400 | tf_op jit(solution)/shard_map/ppermute | solution.py:961
  350.1 2.2 constant_dynamic-slice_fusion.8
  353.9 3.3 last_gradients.1
  358.5 3.8 collective-permute-start.31
  362.8 15.3 %collective-permute-done.25 = bf16[2,2,1,128,768]{4,3,2,1,0:T(8,128)(2,1)} collective-permute-done((bf16[2,2,1,128,768]{4,3,2,1,0:T(8,128)(2,1)}, bf16[2,2,1,128,768]{4,3,2,1,0:T(8,128)(2,1)}, u32[]{:S(2)}, u32[]{:S(2)}) %collective-permute-start.25) | collective-permute-done | bytes 786464 | tf_op jit(solution)/shard_map/ppermute | solution.py:961
  381.4 3.3 collective-permute-start.36
  387.1 3.1 down_gradient.1
  394.1 6.1 %collective-permute-done.37 = bf16[96,5376]{1,0:T(8,128)(2,1)} collective-permute-done((bf16[96,5376]{1,0:T(8,128)(2,1)}, bf16[96,5376]{1,0:T(8,128)(2,1)}, u32[]{:S(2)}, u32[]{:S(2)}) %collective-permute-start.37) | collective-permute-done | bytes 1032224 | tf_op jit(solution)/shard_map/ppermute | solution.py:961
  417.0 11.3 %collective-permute-done.43 = bf16[48,5376]{1,0:T(8,128)(2,1)} collective-permute-done((bf16[48,5376]{1,0:T(8,128)(2,1)}, bf16[48,5376]{1,0:T(8,128)(2,1)}, u32[]{:S(2)}, u32[]{:S(2)}) %collective-permute-start.43) | collective-permute-done | bytes 516128 | tf_op jit(solution)/shard_map/ppermute | solution.py:961
  431.1 4.5 collective-permute-done.42
  443.0 5.3 collective-permute-start.46
  448.4 3.2 collective-permute-done.38
  451.7 5.3 collective-permute-done.47
  457.9 9.6 %collective-permute-done.46 = bf16[96,768]{1,0:T(8,128)(2,1)S(1)} collective-permute-done((bf16[96,768]{1,0:T(8,128)(2,1)S(1)}, bf16[96,768]{1,0:T(8,128)(2,1)S(1)}, u32[]{:S(2)}, u32[]{:S(2)}) %collective-permute-start.46) | collective-permute-done | bytes 147488 | tf_op jit(solution)/shard_map/ppermute | solution.py:961
  467.6 3.0 collective-permute-start.50
  470.6 3.3 collective-permute-done.44
  481.7 9.8 %collective-permute-done.48 = bf16[2,192,576]{2,1,0:T(8,128)(2,1)S(1)} collective-permute-done((bf16[2,192,576]{2,1,0:T(8,128)(2,1)S(1)}, bf16[2,192,576]{2,1,0:T(8,128)(2,1)S(1)}, u32[]{:S(2)}, u32[]{:S(2)}) %collective-permute-start.48) | collective-permute-done | bytes 442400 | tf_op jit(solution)/shard_map/ppermute | solution.py:961
  494.3 7.4 %collective-permute-done.52 = bf16[2,24,5376]{2,1,0:T(8,128)(2,1)S(1)} collective-permute-done((bf16[2,24,5376]{2,1,0:T(8,128)(2,1)S(1)}, bf16[2,24,5376]{2,1,0:T(8,128)(2,1)S(1)}, u32[]{:S(2)}, u32[]{:S(2)}) %collective-permute-start.52) | collective-permute-done | bytes 516128 | tf_op jit(solution)/shard_map/ppermute | solution.py:961
  502.9 2.5 collective-permute-start.58
  507.7 4.7 collective-permute-done.33
  512.4 3.9 settle_half.2.refs_0_
  517.7 3.9 settle_half.3
  523.9 3.8 collective-permute-done.55
  527.9 4.0 settle.3
  531.9 8.4 %collective-permute-done.60 = bf16[4,96,768]{2,1,0:T(8,128)(2,1)S(1)} collective-permute-done((bf16[4,96,768]{2,1,0:T(8,128)(2,1)S(1)}, bf16[4,96,768]{2,1,0:T(8,128)(2,1)S(1)}, u32[]{:S(2)}, u32[]{:S(2)}) %collective-permute-start.60) | collective-permute-done | bytes 589856 | tf_op jit(solution)/shard_map/ppermute | solution.py:961
  540.5 3.6 settle.4
  546.4 3.3 settle.5
  (595 shorter events, 209.3 us)
Async XLA Ops:
  7.2 47.5 %all-gather.8.cloned.1.call-start = ((), (), s32[]{:S(2)}) async-start(), calls=%async_computation.5 | async-start | bytes 3194880 | tf_op jit(solution)/shard_map/all_gather | solution.py:1289
  16.1 117.6 %all-gather.10.cloned.1.call-start = ((), (), s32[]{:S(2)}) async-start(), calls=%async_computation.6 | async-start | bytes 1474560 | tf_op jit(solution)/shard_map/all_gather | solution.py:1289
  16.8 120.9 %all-gather.12.cloned.1.call-start = ((), (), s32[]{:S(2)}) async-start(), calls=%async_computation.7 | async-start | bytes 5898240 | tf_op jit(solution)/shard_map/all_gather | solution.py:1289
  19.6 30.0 %collective-permute-start = (bf16[192,576]{1,0:T(8,128)(2,1)}, bf16[192,576]{1,0:T(8,128)(2,1)}, u32[]{:S(2)}, u32[]{:S(2)}) collective-permute-start(bf16[192,576]{1,0:T(8,128)(2,1)} %pad_maximum_fusion.32.own_ref), channel_id=1, source_target_pairs={{0,1},{1,0},{2,3},{3,2},{4,5},{5,4},{6,7},{7,6},{8,9},{9,8},{10,11... | collective-permute-start | bytes 663560 | tf_op jit(solution)/shard_map/ppermute | solution.py:961
  20.1 31.1 %collective-permute-start.1 = (bf16[192,576]{1,0:T(8,128)(2,1)}, bf16[192,576]{1,0:T(8,128)(2,1)}, u32[]{:S(2)}, u32[]{:S(2)}) collective-permute-start(bf16[192,576]{1,0:T(8,128)(2,1)} %pad_maximum_fusion.32.own_ref), channel_id=1, source_target_pairs={{0,2},{1,3},{2,0},{3,1},{4,6},{5,7},{6,4},{7,5},{8,10},{9,11},{10,... | collective-permute-start | bytes 663560 | tf_op jit(solution)/shard_map/ppermute | solution.py:961
  23.9 52.6 %all-to-all-start = ((bf16[8,136,768]{2,1,0:T(8,128)(2,1)}), bf16[8,136,768]{2,1,0:T(8,128)(2,1)S(1)}, u32[]{:S(2)}, u32[]{:S(2)}) async-start(bf16[8,136,768]{2,1,0:T(8,128)(2,1)} %bitcast.2), calls=%async_computation | async-start | bytes 3342336 | tf_op jit(solution)/shard_map/all_to_all | solution.py:1352
  29.7 135.9 %all-gather.14.cloned.1.call-start = ((), (), s32[]{:S(2)}) async-start(), calls=%async_computation.8 | async-start | bytes 5898240 | tf_op jit(solution)/shard_map/all_gather | solution.py:1289
  37.7 14.0 %collective-permute-start.13 = (bf16[96,1536]{1,0:T(8,128)(2,1)}, bf16[96,1536]{1,0:T(8,128)(2,1)}, u32[]{:S(2)}, u32[]{:S(2)}) collective-permute-start(bf16[96,1536]{1,0:T(8,128)(2,1)} %pad_maximum_fusion.30), channel_id=1, source_target_pairs={{0,2},{1,3},{2,0},{3,1},{4,6},{5,7},{6,4},{7,5},{8,10},{9,11},{10,... | collective-permute-start | bytes 884744 | tf_op jit(solution)/shard_map/ppermute | solution.py:961
  39.8 69.8 %collective-permute-start.3 = (bf16[768,1536]{1,0:T(8,128)(2,1)}, bf16[768,1536]{1,0:T(8,128)(2,1)}, u32[]{:S(2)}, u32[]{:S(2)}) collective-permute-start(bf16[768,1536]{1,0:T(8,128)(2,1)} %pad_maximum_fusion.own_ref), channel_id=1, source_target_pairs={{0,1},{1,0},{2,3},{3,2},{4,5},{5,4},{6,7},{7,6},{8,9},{9,8},{10,11... | collective-permute-start | bytes 7077896 | tf_op jit(solution)/shard_map/ppermute | solution.py:961
  41.4 62.5 %collective-permute-start.4 = (bf16[576,1536]{1,0:T(8,128)(2,1)S(1)}, bf16[576,1536]{1,0:T(8,128)(2,1)}, u32[]{:S(2)}, u32[]{:S(2)}) collective-permute-start(bf16[576,1536]{1,0:T(8,128)(2,1)S(1)} %pad_maximum_fusion.3.own_ref), channel_id=1, source_target_pairs={{0,1},{1,0},{2,3},{3,2},{4,5},{5,4},{6,7},{7,6},{8,9},{9,8},{10,11... | collective-permute-start | bytes 5308424 | tf_op jit(solution)/shard_map/ppermute | solution.py:961
  49.7 18.3 %collective-permute-start.2 = (bf16[192,576]{1,0:T(8,128)(2,1)}, bf16[192,576]{1,0:T(8,128)(2,1)}, u32[]{:S(2)}, u32[]{:S(2)}) collective-permute-start(bf16[192,576]{1,0:T(8,128)(2,1)} %pad_maximum_fusion.32.own_ref), channel_id=1, source_target_pairs={{0,3},{1,2},{2,1},{3,0},{4,7},{5,6},{6,5},{7,4},{8,11},{9,10},{10,... | collective-permute-start | bytes 663560 | tf_op jit(solution)/shard_map/ppermute | solution.py:961
  51.2 14.4 %collective-permute-start.5 = (bf16[72,1536]{1,0:T(8,128)(2,1)}, bf16[72,1536]{1,0:T(8,128)(2,1)}, u32[]{:S(2)}, u32[]{:S(2)}) collective-permute-start(bf16[72,1536]{1,0:T(8,128)(2,1)} %pad_maximum_fusion.33), channel_id=1, source_target_pairs={{0,2},{1,3},{2,0},{3,1},{4,6},{5,7},{6,4},{7,5},{8,10},{9,11},{10,... | collective-permute-start | bytes 663560 | tf_op jit(solution)/shard_map/ppermute | solution.py:961
  51.7 39.7 %collective-permute-start.14 = (bf16[1,96,1536]{2,1,0:T(8,128)(2,1)}, bf16[1,96,1536]{2,1,0:T(8,128)(2,1)}, u32[]{:S(2)}, u32[]{:S(2)}) collective-permute-start(bf16[1,96,1536]{2,1,0:T(8,128)(2,1)} %bitcast.22), channel_id=1, source_target_pairs={{0,16},{4,20},{8,24},{12,28},{16,0},{20,4},{24,8},{28,12},{1,17},{... | collective-permute-start | bytes 884744 | tf_op jit(solution)/shard_map/ppermute | solution.py:961
  65.6 34.1 %collective-permute-start.6 = (bf16[1,72,1536]{2,1,0:T(8,128)(2,1)}, bf16[1,72,1536]{2,1,0:T(8,128)(2,1)}, u32[]{:S(2)}, u32[]{:S(2)}) collective-permute-start(bf16[1,72,1536]{2,1,0:T(8,128)(2,1)} %bitcast.16), channel_id=1, source_target_pairs={{0,4},{4,0},{8,12},{12,8},{16,20},{20,16},{24,28},{28,24},{1,5},{5... | collective-permute-start | bytes 663560 | tf_op jit(solution)/shard_map/ppermute | solution.py:961
  91.5 27.0 %all-to-all-start.1 = ((bf16[8,128,256]{2,1,0:T(8,128)(2,1)}), bf16[8,128,256]{2,1,0:T(8,128)(2,1)}, u32[]{:S(2)}, u32[]{:S(2)}) async-start(bf16[8,128,256]{2,1,0:T(8,128)(2,1)} %bitcast.189), calls=%async_computation.1 | async-start | bytes 1048576 | tf_op jit(solution)/shard_map/all_to_all | solution.py:1358
  95.6 178.8 %all-gather.16.cloned.1.call-start = ((), (), s32[]{:S(2)}) async-start(), calls=%async_computation.9 | async-start | bytes 4177920 | tf_op jit(solution)/shard_map/all_gather | solution.py:1289
  97.8 30.3 %collective-permute-start.15 = (bf16[2,96,1536]{2,1,0:T(8,128)(2,1)}, bf16[2,96,1536]{2,1,0:T(8,128)(2,1)}, u32[]{:S(2)}, u32[]{:S(2)}) collective-permute-start(bf16[2,96,1536]{2,1,0:T(8,128)(2,1)} %pad_maximum_fusion.22), channel_id=1, source_target_pairs={{0,8},{4,12},{8,0},{12,4},{16,24},{20,28},{24,16},{28,20},{1,9},{5... | collective-permute-start | bytes 1769480 | tf_op jit(solution)/shard_map/ppermute | solution.py:961
  101.5 29.9 %collective-permute-start.7 = (bf16[2,72,1536]{2,1,0:T(8,128)(2,1)}, bf16[2,72,1536]{2,1,0:T(8,128)(2,1)}, u32[]{:S(2)}, u32[]{:S(2)}) collective-permute-start(bf16[2,72,1536]{2,1,0:T(8,128)(2,1)} %pad_maximum_fusion.26), channel_id=1, source_target_pairs={{0,16},{4,20},{8,24},{12,28},{16,0},{20,4},{24,8},{28,12},{1,17},{... | collective-permute-start | bytes 1327112 | tf_op jit(solution)/shard_map/ppermute | solution.py:961
  130.4 26.7 %collective-permute-start.16 = (bf16[4,96,1536]{2,1,0:T(8,128)(2,1)}, bf16[4,96,1536]{2,1,0:T(8,128)(2,1)}, u32[]{:S(2)}, u32[]{:S(2)}) collective-permute-start(bf16[4,96,1536]{2,1,0:T(8,128)(2,1)} %pad_maximum_fusion.7), channel_id=1, source_target_pairs={{0,4},{4,0},{8,12},{12,8},{16,20},{20,16},{24,28},{28,24},{1,5},{5... | collective-permute-start | bytes 3538952 | tf_op jit(solution)/shard_map/ppermute | solution.py:961
  133.6 23.5 %collective-permute-start.8 = (bf16[4,72,1536]{2,1,0:T(8,128)(2,1)}, bf16[4,72,1536]{2,1,0:T(8,128)(2,1)}, u32[]{:S(2)}, u32[]{:S(2)}) collective-permute-start(bf16[4,72,1536]{2,1,0:T(8,128)(2,1)} %pad_maximum_fusion.11), channel_id=1, source_target_pairs={{0,8},{4,12},{8,0},{12,4},{16,24},{20,28},{24,16},{28,20},{1,9},{5... | collective-permute-start | bytes 2654216 | tf_op jit(solution)/shard_map/ppermute | solution.py:961
  158.7 12.0 %collective-permute-start.9 = (bf16[8,72,1536]{2,1,0:T(8,128)(2,1)S(1)}, bf16[8,72,1536]{2,1,0:T(8,128)(2,1)}, u32[]{:S(2)}, u32[]{:S(2)}) collective-permute-start(bf16[8,72,1536]{2,1,0:T(8,128)(2,1)S(1)} %pad_maximum_fusion.4.piece_ref), channel_id=1, source_target_pairs={{0,1},{1,0},{2,3},{3,2},{4,5},{5,4},{6,7},{7,6},{8,9},{9,8},{10,11... | collective-permute-start | bytes 5308424 | tf_op jit(solution)/shard_map/ppermute | solution.py:961
  162.0 33.3 %collective-permute-start.17 = (bf16[8,96,1536]{2,1,0:T(8,128)(2,1)}, bf16[8,96,1536]{2,1,0:T(8,128)(2,1)}, u32[]{:S(2)}, u32[]{:S(2)}) collective-permute-start(bf16[8,96,1536]{2,1,0:T(8,128)(2,1)} %pad_maximum_fusion.1.piece_ref), channel_id=1, source_target_pairs={{0,1},{1,0},{2,3},{3,2},{4,5},{5,4},{6,7},{7,6},{8,9},{9,8},{10,11... | collective-permute-start | bytes 7077896 | tf_op jit(solution)/shard_map/ppermute | solution.py:961
  163.7 21.1 %collective-permute-start.10 = (bf16[256,768]{1,0:T(8,128)(2,1)}, bf16[256,768]{1,0:T(8,128)(2,1)}, u32[]{:S(2)}, u32[]{:S(2)}) collective-permute-start(bf16[256,768]{1,0:T(8,128)(2,1)} %get-tuple-element.289), channel_id=1, source_target_pairs={{0,1},{1,0},{2,3},{3,2},{4,5},{5,4},{6,7},{7,6},{8,9},{9,8},{10,11... | collective-permute-start | bytes 1179656 | tf_op jit(solution)/shard_map/ppermute | solution.py:961
  163.7 21.1 %collective-permute-start.11 = (bf16[256,768]{1,0:T(8,128)(2,1)}, bf16[256,768]{1,0:T(8,128)(2,1)}, u32[]{:S(2)}, u32[]{:S(2)}) collective-permute-start(bf16[256,768]{1,0:T(8,128)(2,1)} %get-tuple-element.288), channel_id=1, source_target_pairs={{0,2},{1,3},{2,0},{3,1},{4,6},{5,7},{6,4},{7,5},{8,10},{9,11},{10,... | collective-permute-start | bytes 1179656 | tf_op jit(solution)/shard_map/ppermute | solution.py:961
  164.2 20.6 %collective-permute-start.12 = (bf16[256,768]{1,0:T(8,128)(2,1)}, bf16[256,768]{1,0:T(8,128)(2,1)}, u32[]{:S(2)}, u32[]{:S(2)}) collective-permute-start(bf16[256,768]{1,0:T(8,128)(2,1)} %get-tuple-element.287), channel_id=1, source_target_pairs={{0,3},{1,2},{2,1},{3,0},{4,7},{5,6},{6,5},{7,4},{8,11},{9,10},{10,... | collective-permute-start | bytes 1179656 | tf_op jit(solution)/shard_map/ppermute | solution.py:961
  189.9 28.7 %collective-permute-start.20 = (bf16[256,384]{1,0:T(8,128)(2,1)S(1)}, bf16[256,384]{1,0:T(8,128)(2,1)S(1)}, u32[]{:S(2)}, u32[]{:S(2)}) collective-permute-start(bf16[256,384]{1,0:T(8,128)(2,1)S(1)} %get-tuple-element.300), channel_id=1, source_target_pairs={{0,1},{1,0},{2,3},{3,2},{4,5},{5,4},{6,7},{7,6},{8,9},{9,8},{10,11... | collective-permute-start | bytes 589832 | tf_op jit(solution)/shard_map/ppermute | solution.py:961
  190.0 29.3 %collective-permute-start.21 = (bf16[256,384]{1,0:T(8,128)(2,1)S(1)}, bf16[256,384]{1,0:T(8,128)(2,1)S(1)}, u32[]{:S(2)}, u32[]{:S(2)}) collective-permute-start(bf16[256,384]{1,0:T(8,128)(2,1)S(1)} %get-tuple-element.299), channel_id=1, source_target_pairs={{0,2},{1,3},{2,0},{3,1},{4,6},{5,7},{6,4},{7,5},{8,10},{9,11},{10,... | collective-permute-start | bytes 589832 | tf_op jit(solution)/shard_map/ppermute | solution.py:961
  190.6 29.4 %collective-permute-start.22 = (bf16[256,384]{1,0:T(8,128)(2,1)S(1)}, bf16[256,384]{1,0:T(8,128)(2,1)S(1)}, u32[]{:S(2)}, u32[]{:S(2)}) collective-permute-start(bf16[256,384]{1,0:T(8,128)(2,1)S(1)} %get-tuple-element.298), channel_id=1, source_target_pairs={{0,3},{1,2},{2,1},{3,0},{4,7},{5,6},{6,5},{7,4},{8,11},{9,10},{10,... | collective-permute-start | bytes 589832 | tf_op jit(solution)/shard_map/ppermute | solution.py:961
  223.0 127.1 %reduce-scatter.3.cloned.1.call-start = ((), (), s32[]{:S(2)}) async-start(), calls=%async_computation.10 | async-start | bytes 10321920 | tf_op jit(solution)/shard_map/reduce_scatter | solution.py:1267
  257.3 37.6 %all-to-all-start.2 = ((bf16[8,128,256]{2,1,0:T(8,128)(2,1)}), bf16[8,128,256]{2,1,0:T(8,128)(2,1)S(1)}, u32[]{:S(2)}, u32[]{:S(2)}) async-start(bf16[8,128,256]{2,1,0:T(8,128)(2,1)} %copy-done.31), calls=%async_computation.2 | async-start | bytes 1048576 | tf_op jit(solution)/shard_map/all_to_all | solution.py:1459
  263.2 122.5 %all-gather.18.cloned.1.call-start = ((), (), s32[]{:S(2)}) async-start(), calls=%async_computation.12 | async-start | bytes 1966080 | tf_op jit(solution)/shard_map/all_gather | solution.py:1289
  285.9 32.6 %collective-permute-start.27 = (bf16[3,192,768]{2,1,0:T(8,128)(2,1)}, bf16[3,192,768]{2,1,0:T(8,128)(2,1)}, u32[]{:S(2)}, u32[]{:S(2)}) collective-permute-start(bf16[3,192,768]{2,1,0:T(8,128)(2,1)} %get-tuple-element.164), channel_id=1, source_target_pairs={{0,4},{4,0},{8,12},{12,8},{16,20},{20,16},{24,28},{28,24},{1,5},{5... | collective-permute-start | bytes 2654216 | tf_op jit(solution)/shard_map/ppermute | solution.py:961
  294.3 30.7 %collective-permute-start.26 = (bf16[3,192,768]{2,1,0:T(8,128)(2,1)}, bf16[3,192,768]{2,1,0:T(8,128)(2,1)}, u32[]{:S(2)}, u32[]{:S(2)}) collective-permute-start(bf16[3,192,768]{2,1,0:T(8,128)(2,1)} %get-tuple-element.165), channel_id=1, source_target_pairs={{0,4},{4,0},{8,12},{12,8},{16,20},{20,16},{24,28},{28,24},{1,5},{5... | collective-permute-start | bytes 2654216 | tf_op jit(solution)/shard_map/ppermute | solution.py:961
  294.9 118.4 %reduce-scatter.5.cloned.1.call-start = ((), (), s32[]{:S(2)}) async-start(), calls=%async_computation.11 | async-start | bytes 4423680 | tf_op jit(solution)/shard_map/reduce_scatter | solution.py:1267
  321.6 13.7 %collective-permute-start.29 = (bf16[3,96,768]{2,1,0:T(8,128)(2,1)}, bf16[3,96,768]{2,1,0:T(8,128)(2,1)S(1)}, u32[]{:S(2)}, u32[]{:S(2)}) collective-permute-start(bf16[3,96,768]{2,1,0:T(8,128)(2,1)} %constant_dynamic-slice_fusion.12), channel_id=1, source_target_pairs={{0,8},{4,12},{8,0},{12,4},{16,24},{20,28},{24,16},{28,20},{1,9},{5... | collective-permute-start | bytes 1327112 | tf_op jit(solution)/shard_map/ppermute | solution.py:961
  327.3 20.1 %collective-permute-start.28 = (bf16[3,96,768]{2,1,0:T(8,128)(2,1)}, bf16[3,96,768]{2,1,0:T(8,128)(2,1)}, u32[]{:S(2)}, u32[]{:S(2)}) collective-permute-start(bf16[3,96,768]{2,1,0:T(8,128)(2,1)} %constant_dynamic-slice_fusion.11), channel_id=1, source_target_pairs={{0,16},{4,20},{8,24},{12,28},{16,0},{20,4},{24,8},{28,12},{1,17},{... | collective-permute-start | bytes 1327112 | tf_op jit(solution)/shard_map/ppermute | solution.py:961
  357.2 20.9 %collective-permute-start.25 = (bf16[2,2,1,128,768]{4,3,2,1,0:T(8,128)(2,1)}, bf16[2,2,1,128,768]{4,3,2,1,0:T(8,128)(2,1)}, u32[]{:S(2)}, u32[]{:S(2)}) collective-permute-start(bf16[2,2,1,128,768]{4,3,2,1,0:T(8,128)(2,1)} %constant_dynamic-slice_fusion.13), channel_id=1, source_target_pairs={{0,4},{4,0},{8,12},{12,8},{16,20},{20,16},{24,28},{28,24},{1,5},{5... | collective-permute-start | bytes 2359304 | tf_op jit(solution)/shard_map/ppermute | solution.py:961
  358.5 21.9 %collective-permute-start.32 = (bf16[3,48,768]{2,1,0:T(8,128)(2,1)S(1)}, bf16[3,48,768]{2,1,0:T(8,128)(2,1)S(1)}, u32[]{:S(2)}, u32[]{:S(2)}) collective-permute-start(bf16[3,48,768]{2,1,0:T(8,128)(2,1)S(1)} %constant_dynamic-slice_fusion.10), channel_id=1, source_target_pairs={{0,16},{4,20},{8,24},{12,28},{16,0},{20,4},{24,8},{28,12},{1,17},{... | collective-permute-start | bytes 663560 | tf_op jit(solution)/shard_map/ppermute | solution.py:961
  358.5 26.3 %collective-permute-start.31 = (bf16[3,48,768]{2,1,0:T(8,128)(2,1)}, bf16[3,48,768]{2,1,0:T(8,128)(2,1)S(1)}, u32[]{:S(2)}, u32[]{:S(2)}) collective-permute-start(bf16[3,48,768]{2,1,0:T(8,128)(2,1)} %constant_dynamic-slice_fusion.9), channel_id=1, source_target_pairs={{0,8},{4,12},{8,0},{12,4},{16,24},{20,28},{24,16},{28,20},{1,9},{5... | collective-permute-start | bytes 663560 | tf_op jit(solution)/shard_map/ppermute | solution.py:961
  362.2 38.0 %collective-permute-start.37 = (bf16[96,5376]{1,0:T(8,128)(2,1)}, bf16[96,5376]{1,0:T(8,128)(2,1)}, u32[]{:S(2)}, u32[]{:S(2)}) collective-permute-start(bf16[96,5376]{1,0:T(8,128)(2,1)} %constant_dynamic-slice_fusion.8), channel_id=1, source_target_pairs={{0,4},{4,0},{8,12},{12,8},{16,20},{20,16},{24,28},{28,24},{1,5},{5... | collective-permute-start | bytes 3096584 | tf_op jit(solution)/shard_map/ppermute | solution.py:961
  380.3 12.0 %collective-permute-start.30 = (bf16[2,1,128,768]{3,2,0,1:T(8,128)(2,1)}, bf16[2,1,128,768]{3,2,0,1:T(8,128)(2,1)}, u32[]{:S(2)}, u32[]{:S(2)}) collective-permute-start(bf16[2,1,128,768]{3,2,0,1:T(8,128)(2,1)} %dynamic-slice_bitcast_fusion), channel_id=1, source_target_pairs={{0,8},{4,12},{8,0},{12,4},{16,24},{20,28},{24,16},{28,20},{1,9},{5... | collective-permute-start | bytes 1179656 | tf_op jit(solution)/shard_map/ppermute | solution.py:961
  381.4 21.2 %collective-permute-start.36 = (bf16[1,3,48,768]{3,2,1,0:T(8,128)(2,1)S(1)}, bf16[1,3,48,768]{3,2,1,0:T(8,128)(2,1)}, u32[]{:S(2)}, u32[]{:S(2)}) collective-permute-start(bf16[1,3,48,768]{3,2,1,0:T(8,128)(2,1)S(1)} %fusion.38), channel_id=1, source_target_pairs={{0,16},{4,20},{8,24},{12,28},{16,0},{20,4},{24,8},{28,12},{1,17},{... | collective-permute-start | bytes 663560 | tf_op jit(solution)/shard_map/ppermute | solution.py:961
  385.5 20.8 %collective-permute-start.35 = (bf16[1,3,48,768]{3,2,1,0:T(8,128)(2,1)}, bf16[1,3,48,768]{3,2,1,0:T(8,128)(2,1)}, u32[]{:S(2)}, u32[]{:S(2)}) collective-permute-start(bf16[1,3,48,768]{3,2,1,0:T(8,128)(2,1)} %fusion.39), channel_id=1, source_target_pairs={{0,8},{4,12},{8,0},{12,4},{16,24},{20,28},{24,16},{28,20},{1,9},{5... | collective-permute-start | bytes 663560 | tf_op jit(solution)/shard_map/ppermute | solution.py:961
  390.2 19.4 %collective-permute-start.34 = (bf16[384,768]{1,0:T(8,128)(2,1)S(1)}, bf16[384,768]{1,0:T(8,128)(2,1)S(1)}, u32[]{:S(2)}, u32[]{:S(2)}) collective-permute-start(bf16[384,768]{1,0:T(8,128)(2,1)S(1)} %get-tuple-element.183), channel_id=1, source_target_pairs={{0,4},{4,0},{8,12},{12,8},{16,20},{20,16},{24,28},{28,24},{1,5},{5... | collective-permute-start | bytes 1769480 | tf_op jit(solution)/shard_map/ppermute | solution.py:961
  402.5 25.8 %collective-permute-start.43 = (bf16[48,5376]{1,0:T(8,128)(2,1)}, bf16[48,5376]{1,0:T(8,128)(2,1)}, u32[]{:S(2)}, u32[]{:S(2)}) collective-permute-start(bf16[48,5376]{1,0:T(8,128)(2,1)} %constant_dynamic-slice_fusion.6), channel_id=1, source_target_pairs={{0,8},{4,12},{8,0},{12,4},{16,24},{20,28},{24,16},{28,20},{1,9},{5... | collective-permute-start | bytes 1548296 | tf_op jit(solution)/shard_map/ppermute | solution.py:961
  404.3 31.2 %collective-permute-start.42 = (bf16[2,3,48,768]{3,2,1,0:T(8,128)(2,1)}, bf16[2,3,48,768]{3,2,1,0:T(8,128)(2,1)}, u32[]{:S(2)}, u32[]{:S(2)}) collective-permute-start(bf16[2,3,48,768]{3,2,1,0:T(8,128)(2,1)} %pad_maximum_fusion.27), channel_id=1, source_target_pairs={{0,8},{4,12},{8,0},{12,4},{16,24},{20,28},{24,16},{28,20},{1,9},{5... | collective-permute-start | bytes 1327112 | tf_op jit(solution)/shard_map/ppermute | solution.py:961
  408.2 29.5 %collective-permute-start.41 = (bf16[2,3,48,768]{3,2,1,0:T(8,128)(2,1)}, bf16[2,3,48,768]{3,2,1,0:T(8,128)(2,1)S(1)}, u32[]{:S(2)}, u32[]{:S(2)}) collective-permute-start(bf16[2,3,48,768]{3,2,1,0:T(8,128)(2,1)} %pad_maximum_fusion.28), channel_id=1, source_target_pairs={{0,16},{4,20},{8,24},{12,28},{16,0},{20,4},{24,8},{28,12},{1,17},{... | collective-permute-start | bytes 1327112 | tf_op jit(solution)/shard_map/ppermute | solution.py:961
  411.3 29.2 %collective-permute-start.40 = (bf16[192,768]{1,0:T(8,128)(2,1)}, bf16[192,768]{1,0:T(8,128)(2,1)}, u32[]{:S(2)}, u32[]{:S(2)}) collective-permute-start(bf16[192,768]{1,0:T(8,128)(2,1)} %constant_dynamic-slice_fusion.5), channel_id=1, source_target_pairs={{0,8},{4,12},{8,0},{12,4},{16,24},{20,28},{24,16},{28,20},{1,9},{5... | collective-permute-start | bytes 884744 | tf_op jit(solution)/shard_map/ppermute | solution.py:961
  415.4 27.6 %collective-permute-start.39 = (bf16[96,1664]{1,0:T(8,128)(2,1)S(1)}, bf16[96,1664]{1,0:T(8,128)(2,1)S(1)}, u32[]{:S(2)}, u32[]{:S(2)}) collective-permute-start(bf16[96,1664]{1,0:T(8,128)(2,1)S(1)} %constant_dynamic-slice_fusion.4), channel_id=1, source_target_pairs={{0,4},{4,0},{8,12},{12,8},{16,20},{20,16},{24,28},{28,24},{1,5},{5... | collective-permute-start | bytes 958472 | tf_op jit(solution)/shard_map/ppermute | solution.py:961
  428.3 23.3 %collective-permute-start.38 = (bf16[192,576]{1,0:T(8,128)(2,1)S(1)}, bf16[192,576]{1,0:T(8,128)(2,1)S(1)}, u32[]{:S(2)}, u32[]{:S(2)}) collective-permute-start(bf16[192,576]{1,0:T(8,128)(2,1)S(1)} %slice.205), channel_id=1, source_target_pairs={{0,16},{4,20},{8,24},{12,28},{16,0},{20,4},{24,8},{28,12},{1,17},{... | collective-permute-start | bytes 663560 | tf_op jit(solution)/shard_map/ppermute | solution.py:961
  435.5 21.5 %collective-permute-start.47 = (bf16[24,5376]{1,0:T(8,128)(2,1)S(1)}, bf16[24,5376]{1,0:T(8,128)(2,1)S(1)}, u32[]{:S(2)}, u32[]{:S(2)}) collective-permute-start(bf16[24,5376]{1,0:T(8,128)(2,1)S(1)} %constant_dynamic-slice_fusion.3), channel_id=1, source_target_pairs={{0,16},{4,20},{8,24},{12,28},{16,0},{20,4},{24,8},{28,12},{1,17},{... | collective-permute-start | bytes 774152 | tf_op jit(solution)/shard_map/ppermute | solution.py:961
  437.6 54.0 %collective-permute-start.54 = (bf16[4,3,48,768]{3,2,1,0:T(8,128)(2,1)S(1)}, bf16[4,3,48,768]{3,2,1,0:T(8,128)(2,1)S(1)}, u32[]{:S(2)}, u32[]{:S(2)}) collective-permute-start(bf16[4,3,48,768]{3,2,1,0:T(8,128)(2,1)S(1)} %pad_maximum_fusion.12), channel_id=1, source_target_pairs={{0,4},{4,0},{8,12},{12,8},{16,20},{20,16},{24,28},{28,24},{1,5},{5... | collective-permute-start | bytes 2654216 | tf_op jit(solution)/shard_map/ppermute | solution.py:961
  440.4 52.5 %collective-permute-start.53 = (bf16[4,3,48,768]{3,2,1,0:T(8,128)(2,1)S(1)}, bf16[4,3,48,768]{3,2,1,0:T(8,128)(2,1)S(1)}, u32[]{:S(2)}, u32[]{:S(2)}) collective-permute-start(bf16[4,3,48,768]{3,2,1,0:T(8,128)(2,1)S(1)} %pad_maximum_fusion.13), channel_id=1, source_target_pairs={{0,4},{4,0},{8,12},{12,8},{16,20},{20,16},{24,28},{28,24},{1,5},{5... | collective-permute-start | bytes 2654216 | tf_op jit(solution)/shard_map/ppermute | solution.py:961
  443.0 24.5 %collective-permute-start.46 = (bf16[96,768]{1,0:T(8,128)(2,1)S(1)}, bf16[96,768]{1,0:T(8,128)(2,1)S(1)}, u32[]{:S(2)}, u32[]{:S(2)}) collective-permute-start(bf16[96,768]{1,0:T(8,128)(2,1)S(1)} %constant_dynamic-slice_fusion.2), channel_id=1, source_target_pairs={{0,16},{4,20},{8,24},{12,28},{16,0},{20,4},{24,8},{28,12},{1,17},{... | collective-permute-start | bytes 442376 | tf_op jit(solution)/shard_map/ppermute | solution.py:961
  451.6 16.0 %collective-permute-start.45 = (bf16[48,1664]{1,0:T(8,128)(2,1)S(1)}, bf16[48,1664]{1,0:T(8,128)(2,1)S(1)}, u32[]{:S(2)}, u32[]{:S(2)}) collective-permute-start(bf16[48,1664]{1,0:T(8,128)(2,1)S(1)} %constant_dynamic-slice_fusion.1), channel_id=1, source_target_pairs={{0,8},{4,12},{8,0},{12,4},{16,24},{20,28},{24,16},{28,20},{1,9},{5... | collective-permute-start | bytes 479240 | tf_op jit(solution)/shard_map/ppermute | solution.py:961
  457.0 16.9 %collective-permute-start.44 = (bf16[1,192,576]{2,1,0:T(8,128)(2,1)S(1)}, bf16[1,192,576]{2,1,0:T(8,128)(2,1)S(1)}, u32[]{:S(2)}, u32[]{:S(2)}) collective-permute-start(bf16[1,192,576]{2,1,0:T(8,128)(2,1)S(1)} %fusion.37), channel_id=1, source_target_pairs={{0,4},{4,0},{8,12},{12,8},{16,20},{20,16},{24,28},{28,24},{1,5},{5... | collective-permute-start | bytes 663560 | tf_op jit(solution)/shard_map/ppermute | solution.py:961
  476.1 15.3 %collective-permute-start.48 = (bf16[2,192,576]{2,1,0:T(8,128)(2,1)S(1)}, bf16[2,192,576]{2,1,0:T(8,128)(2,1)S(1)}, u32[]{:S(2)}, u32[]{:S(2)}) collective-permute-start(bf16[2,192,576]{2,1,0:T(8,128)(2,1)S(1)} %pad_maximum_fusion.25), channel_id=1, source_target_pairs={{0,8},{4,12},{8,0},{12,4},{16,24},{20,28},{24,16},{28,20},{1,9},{5... | collective-permute-start | bytes 1327112 | tf_op jit(solution)/shard_map/ppermute | solution.py:961
  477.7 24.1 %collective-permute-start.52 = (bf16[2,24,5376]{2,1,0:T(8,128)(2,1)S(1)}, bf16[2,24,5376]{2,1,0:T(8,128)(2,1)S(1)}, u32[]{:S(2)}, u32[]{:S(2)}) collective-permute-start(bf16[2,24,5376]{2,1,0:T(8,128)(2,1)S(1)} %pad_maximum_fusion.24), channel_id=1, source_target_pairs={{0,8},{4,12},{8,0},{12,4},{16,24},{20,28},{24,16},{28,20},{1,9},{5... | collective-permute-start | bytes 1548296 | tf_op jit(solution)/shard_map/ppermute | solution.py:961
  480.0 25.3 %collective-permute-start.56 = (bf16[1,24,1664]{2,1,0:T(8,128)(2,1)S(1)}, bf16[1,24,1664]{2,1,0:T(8,128)(2,1)S(1)}, u32[]{:S(2)}, u32[]{:S(2)}) collective-permute-start(bf16[1,24,1664]{2,1,0:T(8,128)(2,1)S(1)} %fusion.41), channel_id=1, source_target_pairs={{0,16},{4,20},{8,24},{12,28},{16,0},{20,4},{24,8},{28,12},{1,17},{... | collective-permute-start | bytes 239624 | tf_op jit(solution)/shard_map/ppermute | solution.py:961
  501.9 25.8 %collective-permute-start.55 = (bf16[4,24,5376]{2,1,0:T(8,128)(2,1)S(1)}, bf16[4,24,5376]{2,1,0:T(8,128)(2,1)S(1)}, u32[]{:S(2)}, u32[]{:S(2)}) collective-permute-start(bf16[4,24,5376]{2,1,0:T(8,128)(2,1)S(1)} %pad_maximum_fusion.9), channel_id=1, source_target_pairs={{0,4},{4,0},{8,12},{12,8},{16,20},{20,16},{24,28},{28,24},{1,5},{5... | collective-permute-start | bytes 3096584 | tf_op jit(solution)/shard_map/ppermute | solution.py:961
  502.9 18.7 %collective-permute-start.58 = (bf16[2,96,768]{2,1,0:T(8,128)(2,1)S(1)}, bf16[2,96,768]{2,1,0:T(8,128)(2,1)S(1)}, u32[]{:S(2)}, u32[]{:S(2)}) collective-permute-start(bf16[2,96,768]{2,1,0:T(8,128)(2,1)S(1)} %pad_maximum_fusion.31), channel_id=1, source_target_pairs={{0,8},{4,12},{8,0},{12,4},{16,24},{20,28},{24,16},{28,20},{1,9},{5... | collective-permute-start | bytes 884744 | tf_op jit(solution)/shard_map/ppermute | solution.py:961
  505.4 18.0 %collective-permute-start.57 = (bf16[2,24,1664]{2,1,0:T(8,128)(2,1)S(1)}, bf16[2,24,1664]{2,1,0:T(8,128)(2,1)S(1)}, u32[]{:S(2)}, u32[]{:S(2)}) collective-permute-start(bf16[2,24,1664]{2,1,0:T(8,128)(2,1)S(1)} %pad_maximum_fusion.34), channel_id=1, source_target_pairs={{0,8},{4,12},{8,0},{12,4},{16,24},{20,28},{24,16},{28,20},{1,9},{5... | collective-permute-start | bytes 479240 | tf_op jit(solution)/shard_map/ppermute | solution.py:961
  521.6 18.7 %collective-permute-start.60 = (bf16[4,96,768]{2,1,0:T(8,128)(2,1)S(1)}, bf16[4,96,768]{2,1,0:T(8,128)(2,1)S(1)}, u32[]{:S(2)}, u32[]{:S(2)}) collective-permute-start(bf16[4,96,768]{2,1,0:T(8,128)(2,1)S(1)} %pad_maximum_fusion.23), channel_id=1, source_target_pairs={{0,4},{4,0},{8,12},{12,8},{16,20},{20,16},{24,28},{28,24},{1,5},{5... | collective-permute-start | bytes 1769480 | tf_op jit(solution)/shard_map/ppermute | solution.py:961
  523.5 22.1 %collective-permute-start.59 = (bf16[4,24,1664]{2,1,0:T(8,128)(2,1)S(1)}, bf16[4,24,1664]{2,1,0:T(8,128)(2,1)S(1)}, u32[]{:S(2)}, u32[]{:S(2)}) collective-permute-start(bf16[4,24,1664]{2,1,0:T(8,128)(2,1)S(1)} %pad_maximum_fusion.29), channel_id=1, source_target_pairs={{0,4},{4,0},{8,12},{12,8},{16,20},{20,16},{24,28},{28,24},{1,5},{5... | collective-permute-start | bytes 958472 | tf_op jit(solution)/shard_map/ppermute | solution.py:961
  (150 other events, 825.2 us)
Sparse Core Ops, SparseCore 0:
  16.2 30.9 all-gather.7
  48.8 21.8 all-gather.9
  72.2 38.8 all-gather.11
  112.6 37.4 all-gather.13
  223.1 29.7 all-gather.15
  257.4 71.2 reduce-scatter.2
  330.9 19.6 all-gather.17
  357.4 40.4 reduce-scatter.4
